TPU v7x, 32 devices: a whole 2x2x4 slice. The times are simulated.
32 devices in a mesh: gx: 4 (over z), gy: 8 (over y, x, core).
Axes of the slice: x: 2, y: 2, z: 4, core: 2. Of those that a mesh axis runs over, the one named last changes fastest.
Arguments:
- features: bfloat16 [8192, 512], P(('gx', 'gy')), may hold values from -6 to 6
- cotangent: bfloat16 [8192, 512], P(('gx', 'gy')), may hold values from -6 to 6
- self_weight: bfloat16 [3, 512, 512], replicated, may hold values from -0.25 to 0.25
- neigh_weight: bfloat16 [3, 512, 512], replicated, may hold values from -0.25 to 0.25
- block_val: bfloat16 [64, 4, 128, 128], P(('gx', 'gy')), may hold values from -0.25 to 0.25
- block_col: int32 [64, 4], P(('gx', 'gy')), may hold values from 0 to 5
- send_idx: int32 [32, 32, 16], P(('gx', 'gy')), may hold values from 0 to 255
- send_count: int32 [32, 32], P(('gx', 'gy')), may hold values from 0 to 16, as said below
Outputs:
- self_grad: bfloat16 [3, 512, 512], replicated
- neigh_grad: bfloat16 [3, 512, 512], replicated
- input_grad: bfloat16 [8192, 512], P(('gx', 'gy'))
Inputs may be any that keep to these rules, and one draw needn't show every extreme that they name: `send_count`: at most 16 rows from one device to one peer; in every draw some receivers get exactly 16 from every device.
All inputs are finite; a program needn't handle non-finite values.
Results may differ from a plain program's by a relative error of at most 0.02.
Values may be sent and summed in bfloat16 or wider, within the bound.
No kernel may reach another device: no remote copies, remote signals or barrier semaphores. Data moves between devices by JAX's collectives and lax.ppermute only.
A program may use at most 128 MiB of HBM per device.

v0:
```python
import math

import jax
import jax.numpy as jnp
from jax import lax
from jax.sharding import PartitionSpec as P


def gather_sum(extended, values, columns, tile):
    width = extended.shape[1]
    tiled = extended.reshape(-1, tile, width)[columns]
    total = jnp.einsum("rbij,rbjd->rid", values, tiled, preferred_element_type=jnp.float32)
    return total.reshape(-1, width)


def spread_back(upstream, values, columns, ext_tiles, tile):
    width = upstream.shape[1]
    contrib = jnp.einsum(
        "rbij,rid->rbjd",
        values,
        upstream.reshape(-1, tile, width),
        preferred_element_type=jnp.float32,
    )
    onehot = (
        columns.reshape(-1)[None, :] == jnp.arange(ext_tiles, dtype=jnp.int32)[:, None]
    ).astype(jnp.float32)
    total = jnp.einsum(
        "cn,njd->cjd", onehot, contrib.reshape(-1, tile, width), precision=lax.Precision.HIGHEST
    )
    return total.reshape(-1, width)


def per_device(
    features, cotangent, self_weight, neigh_weight, block_val, block_col, send_idx, send_count
):
    outer = lax.axis_size("gx")
    inner = lax.axis_size("gy")
    devices = outer * inner
    node_rows, width = features.shape
    tile = block_val.shape[2]
    layers = self_weight.shape[0]
    slots = send_idx.shape[2]
    halo_rows = devices * slots
    ext_tiles = (node_rows + halo_rows) // tile
    scale = 1.0 / math.sqrt(node_rows * devices)
    row_ids = send_idx.reshape(-1)
    live = (jnp.arange(slots, dtype=jnp.int32)[None, :] < send_count.reshape(-1)[:, None]).reshape(
        -1, 1
    )
    hiddens = [features]
    aggregates = []
    preacts = []
    hidden = features
    for layer_at in range(layers):
        picked = jnp.where(live, jnp.take(hidden, row_ids, axis=0), jnp.zeros((), hidden.dtype))
        picked = picked.reshape(outer, inner, slots, width)
        send_arrived = lax.all_to_all(
            lax.all_to_all(picked, "gx", split_axis=0, concat_axis=0, tiled=True),
            "gy",
            split_axis=1,
            concat_axis=1,
            tiled=True,
        )
        extended = jnp.concatenate([hidden, send_arrived.reshape(halo_rows, width)], axis=0)
        aggregate = gather_sum(extended, block_val, block_col, tile).astype(jnp.bfloat16)
        preact = jnp.dot(
            hidden, self_weight[layer_at], preferred_element_type=jnp.float32
        ) + jnp.dot(aggregate, neigh_weight[layer_at], preferred_element_type=jnp.float32)
        aggregates.append(aggregate)
        preacts.append(preact)
        if layer_at < layers - 1:
            hidden = jax.nn.silu(preact).astype(jnp.bfloat16)
            hiddens.append(hidden)
    transposed = (((0,), (0,)), ((), ()))
    against = (((1,), (1,)), ((), ()))
    self_list = [None] * layers
    neigh_list = [None] * layers
    grad = cotangent
    for layer_at in reversed(range(layers)):
        preact = preacts[layer_at]
        sigma = jax.nn.sigmoid(preact)
        delta = (grad.astype(jnp.float32) * sigma * (1.0 + preact * (1.0 - sigma))).astype(
            jnp.bfloat16
        )
        self_term = lax.dot_general(
            hiddens[layer_at], delta, transposed, preferred_element_type=jnp.float32
        )
        neigh_term = lax.dot_general(
            aggregates[layer_at], delta, transposed, preferred_element_type=jnp.float32
        )
        self_sum, neigh_sum = lax.psum((self_term, neigh_term), ("gx", "gy"))
        self_list[layer_at] = (self_sum * scale).astype(jnp.bfloat16)
        neigh_list[layer_at] = (neigh_sum * scale).astype(jnp.bfloat16)
        own_part = lax.dot_general(
            delta, self_weight[layer_at], against, preferred_element_type=jnp.float32
        )
        upstream = lax.dot_general(
            delta, neigh_weight[layer_at], against, preferred_element_type=jnp.float32
        ).astype(jnp.bfloat16)
        ext_grad = spread_back(upstream, block_val, block_col, ext_tiles, tile)
        outgoing = ext_grad[node_rows:].astype(jnp.bfloat16).reshape(outer, inner, slots, width)
        arrived = lax.all_to_all(
            lax.all_to_all(outgoing, "gx", split_axis=0, concat_axis=0, tiled=True),
            "gy",
            split_axis=1,
            concat_axis=1,
            tiled=True,
        )
        masked = jnp.where(
            live, arrived.reshape(halo_rows, width).astype(jnp.float32), jnp.zeros((), jnp.float32)
        )
        returned = jnp.zeros((node_rows, width), jnp.float32).at[row_ids].add(masked)
        grad = (own_part + ext_grad[:node_rows] + returned).astype(jnp.bfloat16)
    self_grad = jnp.stack(self_list)
    neigh_grad = jnp.stack(neigh_list)
    return (self_grad, neigh_grad, grad)


def solution(mesh):
    return jax.shard_map(
        per_device,
        mesh=mesh,
        in_specs=(
            P(("gx", "gy"), None),
            P(("gx", "gy"), None),
            P(),
            P(),
            P(("gx", "gy"), None, None, None),
            P(("gx", "gy"), None),
            P(("gx", "gy"), None, None),
            P(("gx", "gy"), None),
        ),
        out_specs=(P(), P(), P(("gx", "gy"), None)),
        check_vma=False,
    )
```

profile of v0, /device:TPU:0, one launch (start us, length us, event | category | flops | bytes accessed | tf_op | source)
XLA Modules:
  0.0 399.9 jit_solution(2928996028955188981)
XLA Ops:
  12.1 20.8 %all_to_all.60 = bf16[4,8,16,512]{3,2,1,0:T(8,128)(2,1)S(1)} all-to-all(bf16[4,8,16,512]{3,2,1,0:T(8,128)(2,1)S(1)} %bitcast.184), channel_id=1, replica_groups=mesh['gx'=4,'gy'=8] {'gx'}, dimensions={0} | all-to-all | bytes 1048576 | tf_op jit(solution)/shard_map/all_to_all | solution.py:58
  33.7 3.7 all-to-all-start.1
  38.7 8.5 %all-to-all-done.1 = bf16[4,8,16,512]{3,2,0,1:T(8,128)(2,1)S(1)} async-done(((bf16[4,8,16,512]{3,2,0,1:T(8,128)(2,1)}), bf16[4,8,16,512]{3,2,0,1:T(8,128)(2,1)S(1)}, u32[]{:S(2)}, u32[]{:S(2)}) %all-to-all-start.1) | async-done | bytes 524320 | tf_op jit(solution)/shard_map/all_to_all | solution.py:57
  54.9 14.9 %all_to_all.61 = bf16[4,8,16,512]{3,2,1,0:T(8,128)(2,1)S(1)} all-to-all(bf16[4,8,16,512]{3,2,1,0:T(8,128)(2,1)S(1)} %bitcast.185), channel_id=1, replica_groups=mesh['gx'=4,'gy'=8] {'gx'}, dimensions={0} | all-to-all | bytes 1048576 | tf_op jit(solution)/shard_map/all_to_all | solution.py:58
  70.7 4.3 %all-to-all-start.3 = ((bf16[4,8,16,512]{3,2,0,1:T(8,128)(2,1)}), bf16[4,8,16,512]{3,2,0,1:T(8,128)(2,1)S(1)}, u32[]{:S(2)}, u32[]{:S(2)}) async-start(bf16[4,8,16,512]{3,2,0,1:T(8,128)(2,1)} %copy.111), calls=%async_computation.3 | async-start | bytes 1048576 | tf_op jit(solution)/shard_map/all_to_all | solution.py:57
  76.1 8.6 %all-to-all-done.3 = bf16[4,8,16,512]{3,2,0,1:T(8,128)(2,1)S(1)} async-done(((bf16[4,8,16,512]{3,2,0,1:T(8,128)(2,1)}), bf16[4,8,16,512]{3,2,0,1:T(8,128)(2,1)S(1)}, u32[]{:S(2)}, u32[]{:S(2)}) %all-to-all-start.3) | async-done | bytes 524320 | tf_op jit(solution)/shard_map/all_to_all | solution.py:57
  92.4 14.9 %all_to_all.62 = bf16[4,8,16,512]{3,2,1,0:T(8,128)(2,1)S(1)} all-to-all(bf16[4,8,16,512]{3,2,1,0:T(8,128)(2,1)S(1)} %bitcast.183), channel_id=1, replica_groups=mesh['gx'=4,'gy'=8] {'gx'}, dimensions={0} | all-to-all | bytes 1048576 | tf_op jit(solution)/shard_map/all_to_all | solution.py:58
  108.2 4.3 %all-to-all-start.5 = ((bf16[4,8,16,512]{3,2,0,1:T(8,128)(2,1)}), bf16[4,8,16,512]{3,2,0,1:T(8,128)(2,1)S(1)}, u32[]{:S(2)}, u32[]{:S(2)}) async-start(bf16[4,8,16,512]{3,2,0,1:T(8,128)(2,1)} %copy.113), calls=%async_computation.5 | async-start | bytes 1048576 | tf_op jit(solution)/shard_map/all_to_all | solution.py:57
  113.7 8.5 %all-to-all-done.5 = bf16[4,8,16,512]{3,2,0,1:T(8,128)(2,1)S(1)} async-done(((bf16[4,8,16,512]{3,2,0,1:T(8,128)(2,1)}), bf16[4,8,16,512]{3,2,0,1:T(8,128)(2,1)S(1)}, u32[]{:S(2)}, u32[]{:S(2)}) %all-to-all-start.5) | async-done | bytes 524320 | tf_op jit(solution)/shard_map/all_to_all | solution.py:57
  133.5 4.1 %all-to-all-start.6 = ((bf16[4,8,16,512]{3,2,1,0:T(8,128)(2,1)}), bf16[4,8,16,512]{3,2,1,0:T(8,128)(2,1)}, u32[]{:S(2)}, u32[]{:S(2)}) async-start(bf16[4,8,16,512]{3,2,1,0:T(8,128)(2,1)} %copy.119), calls=%async_computation.6 | async-start | bytes 1048576 | tf_op jit(solution)/shard_map/all_to_all | solution.py:103
  137.7 12.5 %all-to-all-done.6 = bf16[4,8,16,512]{3,2,1,0:T(8,128)(2,1)} async-done(((bf16[4,8,16,512]{3,2,1,0:T(8,128)(2,1)}), bf16[4,8,16,512]{3,2,1,0:T(8,128)(2,1)}, u32[]{:S(2)}, u32[]{:S(2)}) %all-to-all-start.6) | async-done | bytes 524320 | tf_op jit(solution)/shard_map/all_to_all | solution.py:103
  152.1 4.3 %all-to-all-start.7 = ((bf16[4,8,16,512]{3,2,0,1:T(8,128)(2,1)}), bf16[4,8,16,512]{3,2,0,1:T(8,128)(2,1)}, u32[]{:S(2)}, u32[]{:S(2)}) async-start(bf16[4,8,16,512]{3,2,0,1:T(8,128)(2,1)} %copy.120), calls=%async_computation.7 | async-start | bytes 1048576 | tf_op jit(solution)/shard_map/all_to_all | solution.py:102
  158.1 8.1 %all-to-all-done.7 = bf16[4,8,16,512]{3,2,0,1:T(8,128)(2,1)} async-done(((bf16[4,8,16,512]{3,2,0,1:T(8,128)(2,1)}), bf16[4,8,16,512]{3,2,0,1:T(8,128)(2,1)}, u32[]{:S(2)}, u32[]{:S(2)}) %all-to-all-start.7) | async-done | bytes 524320 | tf_op jit(solution)/shard_map/all_to_all | solution.py:102
  167.5 4.0 scatter_fusion
  179.6 4.1 %all-to-all-start.8 = ((bf16[4,8,16,512]{3,2,1,0:T(8,128)(2,1)}), bf16[4,8,16,512]{3,2,1,0:T(8,128)(2,1)}, u32[]{:S(2)}, u32[]{:S(2)}) async-start(bf16[4,8,16,512]{3,2,1,0:T(8,128)(2,1)} %copy.125), calls=%async_computation.8 | async-start | bytes 1048576 | tf_op jit(solution)/shard_map/all_to_all | solution.py:103
  189.1 7.2 %all-to-all-done.8 = bf16[4,8,16,512]{3,2,1,0:T(8,128)(2,1)} async-done(((bf16[4,8,16,512]{3,2,1,0:T(8,128)(2,1)}), bf16[4,8,16,512]{3,2,1,0:T(8,128)(2,1)}, u32[]{:S(2)}, u32[]{:S(2)}) %all-to-all-start.8) | async-done | bytes 524320 | tf_op jit(solution)/shard_map/all_to_all | solution.py:103
  198.2 4.3 %all-to-all-start.9 = ((bf16[4,8,16,512]{3,2,0,1:T(8,128)(2,1)}), bf16[4,8,16,512]{3,2,0,1:T(8,128)(2,1)S(1)}, u32[]{:S(2)}, u32[]{:S(2)}) async-start(bf16[4,8,16,512]{3,2,0,1:T(8,128)(2,1)} %copy.126), calls=%async_computation.9 | async-start | bytes 1048576 | tf_op jit(solution)/shard_map/all_to_all | solution.py:102
  205.2 7.0 %all-to-all-done.9 = bf16[4,8,16,512]{3,2,0,1:T(8,128)(2,1)S(1)} async-done(((bf16[4,8,16,512]{3,2,0,1:T(8,128)(2,1)}), bf16[4,8,16,512]{3,2,0,1:T(8,128)(2,1)S(1)}, u32[]{:S(2)}, u32[]{:S(2)}) %all-to-all-start.9) | async-done | bytes 524320 | tf_op jit(solution)/shard_map/all_to_all | solution.py:102
  212.5 4.0 %scatter_fusion.1 = f32[256,512]{1,0:T(8,128)S(1)} fusion(f32[256,512]{1,0:T(8,128)S(1)} %convolution_add_fusion.1, s32[512]{0:T(512)S(1)} %bitcast.199, f32[512,512]{1,0:T(8,128)S(1)} %bitcast_select_fusion.1), kind=kCustom, calls=%fused_computation.7 | custom fusion | flops 262144 | bytes 3147776 | tf_op jit(solution)/shard_map/scatter-add | solution.py:112
  226.5 22.2 %all_to_all.63 = bf16[4,8,16,512]{3,2,1,0:T(8,128)(2,1)S(1)} all-to-all(bf16[4,8,16,512]{3,2,1,0:T(8,128)(2,1)S(1)} %copy.136), channel_id=1, replica_groups=mesh['gx'=4,'gy'=8] {'gx'}, dimensions={0} | all-to-all | bytes 1048576 | tf_op jit(solution)/shard_map/all_to_all | solution.py:103
  249.5 3.5 all-to-all-start.11
  254.8 7.9 %all-to-all-done.11 = bf16[4,8,16,512]{3,2,0,1:T(8,128)(2,1)S(1)} async-done(((bf16[4,8,16,512]{3,2,0,1:T(8,128)(2,1)}), bf16[4,8,16,512]{3,2,0,1:T(8,128)(2,1)S(1)}, u32[]{:S(2)}, u32[]{:S(2)}) %all-to-all-start.11) | async-done | bytes 524320 | tf_op jit(solution)/shard_map/all_to_all | solution.py:102
  263.0 3.8 scatter_fusion.2
  267.5 117.8 %all-reduce.3.cloned.1.call-done = (f32[512,512]{0,1:T(8,128)}, f32[512,512]{0,1:T(8,128)}, f32[512,512]{0,1:T(8,128)}, f32[512,512]{0,1:T(8,128)}, f32[512,512]{0,1:T(8,128)}, /*index=5*/f32[512,512]{0,1:T(8,128)}) async-done(((f32[512,512]{0,1:T(8,128)}, f32[512,512]{0,1:T(8,128)}, f32[512,512]{0,1:T(8,128)}, f32[512,512]{0,1:T(8,128)}, f32[512,512]{0,1:T(8,128)}, /*index=5*/f32[512,512]{0,1:T(8,128)}), ...) | async-done | bytes 6291472 | tf_op jit(solution)/shard_map/psum | solution.py:91
  (132 shorter events, 81.8 us)
Async XLA Ops:
  7.2 41.7 %copy-start = (bf16[2,4,128,128]{3,2,1,0:T(8,128)(2,1)S(1)}, bf16[2,4,128,128]{3,2,1,0:T(8,128)(2,1)}, u32[]{:S(2)}) copy-start(bf16[2,4,128,128]{3,2,1,0:T(8,128)(2,1)} %param.14) | copy-start | bytes 786436
  12.1 25.4 %copy-start.17 = (s32[2,4]{1,0:T(2,128)S(1)}, s32[2,4]{1,0:T(2,128)}, u32[]{:S(2)}) copy-start(s32[2,4]{1,0:T(2,128)} %param.15) | copy-start | bytes 100
  12.1 25.5 %copy-start.1 = (bf16[256,512]{1,0:T(8,128)(2,1)S(1)}, bf16[256,512]{1,0:T(8,128)(2,1)}, u32[]{:S(2)}) copy-start(bf16[256,512]{1,0:T(8,128)(2,1)} %param.10) | copy-start | bytes 786436
  12.1 25.4 %copy-start.2 = (bf16[3,512,512]{2,1,0:T(8,128)(2,1)S(1)}, bf16[3,512,512]{2,1,0:T(8,128)(2,1)}, u32[]{:S(2)}) copy-start(bf16[3,512,512]{2,1,0:T(8,128)(2,1)} %param.12) | copy-start | bytes 4718596
  33.7 13.4 %all-to-all-start.1 = ((bf16[4,8,16,512]{3,2,0,1:T(8,128)(2,1)}), bf16[4,8,16,512]{3,2,0,1:T(8,128)(2,1)S(1)}, u32[]{:S(2)}, u32[]{:S(2)}) async-start(bf16[4,8,16,512]{3,2,0,1:T(8,128)(2,1)} %copy.109), calls=%async_computation.1 | async-start | bytes 1048576 | tf_op jit(solution)/shard_map/all_to_all | solution.py:57
  50.5 2.3 copy-start.7
  70.7 14.0 %all-to-all-start.3 = ((bf16[4,8,16,512]{3,2,0,1:T(8,128)(2,1)}), bf16[4,8,16,512]{3,2,0,1:T(8,128)(2,1)S(1)}, u32[]{:S(2)}, u32[]{:S(2)}) async-start(bf16[4,8,16,512]{3,2,0,1:T(8,128)(2,1)} %copy.111), calls=%async_computation.3 | async-start | bytes 1048576 | tf_op jit(solution)/shard_map/all_to_all | solution.py:57
  88.0 2.3 copy-start.9
  108.2 14.0 %all-to-all-start.5 = ((bf16[4,8,16,512]{3,2,0,1:T(8,128)(2,1)}), bf16[4,8,16,512]{3,2,0,1:T(8,128)(2,1)S(1)}, u32[]{:S(2)}, u32[]{:S(2)}) async-start(bf16[4,8,16,512]{3,2,0,1:T(8,128)(2,1)} %copy.113), calls=%async_computation.5 | async-start | bytes 1048576 | tf_op jit(solution)/shard_map/all_to_all | solution.py:57
  123.3 2.3 copy-start.11
  125.6 31.2 %copy-start.3 = (bf16[256,512]{1,0:T(8,128)(2,1)}, bf16[256,512]{1,0:T(8,128)(2,1)S(1)}, u32[]{:S(2)}) copy-start(bf16[256,512]{1,0:T(8,128)(2,1)S(1)} %multiply_convert_fusion.8) | copy-start | bytes 786436
  133.5 16.7 %all-to-all-start.6 = ((bf16[4,8,16,512]{3,2,1,0:T(8,128)(2,1)}), bf16[4,8,16,512]{3,2,1,0:T(8,128)(2,1)}, u32[]{:S(2)}, u32[]{:S(2)}) async-start(bf16[4,8,16,512]{3,2,1,0:T(8,128)(2,1)} %copy.119), calls=%async_computation.6 | async-start | bytes 1048576 | tf_op jit(solution)/shard_map/all_to_all | solution.py:103
  152.1 14.1 %all-to-all-start.7 = ((bf16[4,8,16,512]{3,2,0,1:T(8,128)(2,1)}), bf16[4,8,16,512]{3,2,0,1:T(8,128)(2,1)}, u32[]{:S(2)}, u32[]{:S(2)}) async-start(bf16[4,8,16,512]{3,2,0,1:T(8,128)(2,1)} %copy.120), calls=%async_computation.7 | async-start | bytes 1048576 | tf_op jit(solution)/shard_map/all_to_all | solution.py:102
  167.5 4.0 %copy-start.13 = (f32[256,512]{1,0:T(8,128)S(1)}, f32[256,512]{1,0:T(8,128)}, u32[]{:S(2)}) copy-start(f32[256,512]{1,0:T(8,128)} %get-tuple-element.28) | copy-start | bytes 1572868
  179.6 16.7 %all-to-all-start.8 = ((bf16[4,8,16,512]{3,2,1,0:T(8,128)(2,1)}), bf16[4,8,16,512]{3,2,1,0:T(8,128)(2,1)}, u32[]{:S(2)}, u32[]{:S(2)}) async-start(bf16[4,8,16,512]{3,2,1,0:T(8,128)(2,1)} %copy.125), calls=%async_computation.8 | async-start | bytes 1048576 | tf_op jit(solution)/shard_map/all_to_all | solution.py:103
  183.7 2.4 copy-start.4
  186.1 1.7 copy-start.10
  198.2 14.0 %all-to-all-start.9 = ((bf16[4,8,16,512]{3,2,0,1:T(8,128)(2,1)}), bf16[4,8,16,512]{3,2,0,1:T(8,128)(2,1)S(1)}, u32[]{:S(2)}, u32[]{:S(2)}) async-start(bf16[4,8,16,512]{3,2,0,1:T(8,128)(2,1)} %copy.126), calls=%async_computation.9 | async-start | bytes 1048576 | tf_op jit(solution)/shard_map/all_to_all | solution.py:102
  202.5 182.8 %all-reduce.3.cloned.1.call-start = ((), (), s32[]{:S(2)}) async-start(), calls=%async_computation.12 | async-start | bytes 12582912 | tf_op jit(solution)/shard_map/psum | solution.py:91
  212.5 4.1 %copy-start.12 = (f32[256,512]{1,0:T(8,128)S(1)}, f32[256,512]{1,0:T(8,128)}, u32[]{:S(2)}) copy-start(f32[256,512]{1,0:T(8,128)} %get-tuple-element.26) | copy-start | bytes 1572868
  212.5 4.3 %copy-start.8 = (bf16[2,512,128]{1,2,0:T(8,128)(2,1)S(1)}, bf16[2,512,128]{1,2,0:T(8,128)(2,1)}, u32[]{:S(2)}) copy-start(bf16[2,512,128]{1,2,0:T(8,128)(2,1)} %copy-done.7) | copy-start | bytes 786436
  249.5 13.1 %all-to-all-start.11 = ((bf16[4,8,16,512]{3,2,0,1:T(8,128)(2,1)}), bf16[4,8,16,512]{3,2,0,1:T(8,128)(2,1)S(1)}, u32[]{:S(2)}, u32[]{:S(2)}) async-start(bf16[4,8,16,512]{3,2,0,1:T(8,128)(2,1)} %copy.137), calls=%async_computation.11 | async-start | bytes 1048576 | tf_op jit(solution)/shard_map/all_to_all | solution.py:102
  385.3 2.0 copy-start.5
  385.3 2.2 copy-start.6
  (4 other events, 5.4 us)
Sparse Core Ops, SparseCore 0:
  219.6 165.6 all-reduce.2
where the time goes:
time: 402 us; the launch traced here: 400 us
  waiting for transfers between devices  186 us (46%)
  blocking collectives  72.8 us (18%)
  matrix products  39.5 us (10%)
  local copies, waits for them, and re-layouts  34.6 us (9%)
  starting transfers between devices  32.8 us (8%)
  other arithmetic  19.4 us (5%)
  between operations  14.7 us (4%)
    psum x1, waiting for transfers between devices, per_device(): self_sum, neigh_sum = lax.psum((self_term, neigh_term), ('gx', 'gy'))  118 us
    all_to_all x3, blocking collectives, per_device(): lax.all_to_all(picked, 'gx', split_axis=0, concat_axis=0, tiled=True)  50.6 us
    all_to_all x3, waiting for transfers between devices, per_device(): lax.all_to_all(lax.all_to_all(picked, 'gx', split_axis=0, concat_axis=0,...  25.7 us
    all_to_all x3, waiting for transfers between devices, per_device(): lax.all_to_all(lax.all_to_all(outgoing, 'gx', split_axis=0, concat_axis=0...  23 us
    all_to_all x1, blocking collectives, per_device(): lax.all_to_all(outgoing, 'gx', split_axis=0, concat_axis=0, tiled=True)  22.2 us
    all_to_all x2, waiting for transfers between devices, per_device(): lax.all_to_all(outgoing, 'gx', split_axis=0, concat_axis=0, tiled=True)  19.7 us
    all_to_all x3, starting transfers between devices, per_device(): lax.all_to_all(lax.all_to_all(picked, 'gx', split_axis=0, concat_axis=0,...  12.4 us
    all_to_all x3, starting transfers between devices, per_device(): lax.all_to_all(lax.all_to_all(outgoing, 'gx', split_axis=0, concat_axis=0...  12.1 us
  transfers between devices with their start and end apart: 9, of which 9 were waited for; matrix products, arithmetic and copies ran while one was open for 7% of the time, Pallas kernels for 0%

commit v1 on v0

v1 whole, which is shorter than its diff:
```python
import functools
import math

import jax
import jax.numpy as jnp
from jax import lax
from jax.experimental import pallas as pl
from jax.experimental.pallas import tpu as pltpu
from jax.sharding import PartitionSpec as P

AXES = ("gx", "gy")
VMEM = pl.BlockSpec(memory_space=pltpu.VMEM)
SMEM = pl.BlockSpec(memory_space=pltpu.SMEM)


def mm(a, b):
    return jnp.dot(a, b, preferred_element_type=jnp.float32)


def mm_tn(a, b):
    return lax.dot_general(a, b, (((0,), (0,)), ((), ())), preferred_element_type=jnp.float32)


def mm_nt(a, b):
    return lax.dot_general(a, b, (((1,), (1,)), ((), ())), preferred_element_type=jnp.float32)


def iota(shape, dim):
    return lax.broadcasted_iota(jnp.int32, shape, dim)


def ones_where(mask):
    return jnp.where(mask, 1.0, 0.0).astype(jnp.bfloat16)


def pick_rows(col, table):
    hot = ones_where(iota((col.shape[0], table.shape[0]), 1) == col)
    return mm(hot, table).astype(jnp.bfloat16)


def return_rows(row, arrived, nodes):
    hot = ones_where(iota((nodes, row.shape[1]), 0) == row)
    return mm(hot, arrived)


def first_kernel(idx_ref, cnt_ref, x_ref, row_ref, col_ref, send_ref):
    peers, slots = idx_ref.shape
    total = peers * slots
    eye = iota((peers, peers), 0) == iota((peers, peers), 1)
    counts = jnp.broadcast_to(cnt_ref[...].astype(jnp.float32), (peers, peers))
    count_col = jnp.sum(jnp.where(eye, counts, 0.0), axis=1, keepdims=True)
    live = iota((peers, slots), 1).astype(jnp.float32) < count_col
    code = jnp.where(live, idx_ref[...].astype(jnp.float32) + 1.0, 0.0).astype(jnp.bfloat16)
    spread = ones_where((iota((slots, total), 1) & (slots - 1)) == iota((slots, total), 0))
    start = iota((peers, total), 0) * slots
    place = iota((peers, total), 1)
    inside = (place >= start) & (place < start + slots)
    row = jnp.sum(jnp.where(inside, mm(code, spread), 0.0), axis=0, keepdims=True) - 1.0
    row_ref[...] = row.astype(jnp.int32)
    start_t = iota((total, peers), 1) * slots
    place_t = iota((total, peers), 0)
    inside_t = ones_where((place_t >= start_t) & (place_t < start_t + slots))
    here = (iota((total, slots), 0) & (slots - 1)) == iota((total, slots), 1)
    col = jnp.sum(jnp.where(here, mm(inside_t, code), 0.0), axis=1, keepdims=True) - 1.0
    col = col.astype(jnp.int32)
    col_ref[...] = col
    send_ref[...] = pick_rows(col, x_ref[...])


def aggregate_into(agg_ref, ext_ref, cols_ref, hid_ref, arr_ref, val_ref):
    tiles, blocks, tile, _ = val_ref.shape
    own = hid_ref.shape[0] // tile
    for t in range(own):
        ext_ref[t] = hid_ref[t * tile : (t + 1) * tile, :]
    for t in range(arr_ref.shape[0] // tile):
        ext_ref[own + t] = arr_ref[t * tile : (t + 1) * tile, :]
    for r in range(tiles):
        total = mm(val_ref[r, 0], ext_ref[cols_ref[r, 0]])
        for b in range(1, blocks):
            total += mm(val_ref[r, b], ext_ref[cols_ref[r, b]])
        agg_ref[r * tile : (r + 1) * tile, :] = total.astype(jnp.bfloat16)


def pre_and_sigma(agg_ref, hid_ref, ws_ref, wn_ref):
    pre = mm(hid_ref[...], ws_ref[0]) + mm(agg_ref[...], wn_ref[0])
    return pre, jax.nn.sigmoid(pre)


def middle_kernel(
    cols_ref, hid_ref, arr_ref, val_ref, ws_ref, wn_ref, col_ref,
    agg_ref, slope_ref, next_ref, send_ref, ext_ref,
):
    aggregate_into(agg_ref, ext_ref, cols_ref, hid_ref, arr_ref, val_ref)
    pre, sigma = pre_and_sigma(agg_ref, hid_ref, ws_ref, wn_ref)
    hidden = (pre * sigma).astype(jnp.bfloat16)
    next_ref[...] = hidden
    send_ref[...] = pick_rows(col_ref[...], hidden)
    slope_ref[...] = sigma * (1.0 + pre * (1.0 - sigma))


def spread_back(delta, cols_ref, val_ref, ws_ref, wn_ref, halo_ref, base_ref, acc_ref):
    tiles, blocks, tile, _ = val_ref.shape
    own = base_ref.shape[0] // tile
    acc_ref[...] = jnp.zeros_like(acc_ref)
    upstream = mm_nt(delta, wn_ref[0]).astype(jnp.bfloat16)
    for r in range(tiles):
        part = upstream[r * tile : (r + 1) * tile, :]
        for b in range(blocks):
            c = cols_ref[r, b]
            acc_ref[c] += mm_tn(val_ref[r, b], part)
    for t in range(halo_ref.shape[0] // tile):
        halo_ref[t * tile : (t + 1) * tile, :] = acc_ref[own + t].astype(jnp.bfloat16)
    own_part = mm_nt(delta, ws_ref[0])
    for t in range(own):
        rows = slice(t * tile, (t + 1) * tile)
        base_ref[rows, :] = own_part[rows, :] + acc_ref[t]


def last_kernel(
    cols_ref, hid_ref, arr_ref, val_ref, ws_ref, wn_ref, cot_ref,
    agg_ref, delta_ref, halo_ref, base_ref, ext_ref, acc_ref,
):
    aggregate_into(agg_ref, ext_ref, cols_ref, hid_ref, arr_ref, val_ref)
    pre, sigma = pre_and_sigma(agg_ref, hid_ref, ws_ref, wn_ref)
    slope = sigma * (1.0 + pre * (1.0 - sigma))
    delta = (cot_ref[...].astype(jnp.float32) * slope).astype(jnp.bfloat16)
    delta_ref[...] = delta
    spread_back(delta, cols_ref, val_ref, ws_ref, wn_ref, halo_ref, base_ref, acc_ref)


def backward_kernel(
    cols_ref, arr_ref, before_ref, slope_ref, row_ref, val_ref, ws_ref, wn_ref,
    delta_ref, halo_ref, base_ref, acc_ref,
):
    back = return_rows(row_ref[...], arr_ref[...], before_ref.shape[0])
    grad = (before_ref[...] + back).astype(jnp.bfloat16)
    delta = (grad.astype(jnp.float32) * slope_ref[...]).astype(jnp.bfloat16)
    delta_ref[...] = delta
    spread_back(delta, cols_ref, val_ref, ws_ref, wn_ref, halo_ref, base_ref, acc_ref)


def final_kernel(arr_ref, before_ref, row_ref, out_ref):
    back = return_rows(row_ref[...], arr_ref[...], before_ref.shape[0])
    out_ref[...] = (before_ref[...] + back).astype(jnp.bfloat16)


def weight_kernel(core_ref, hid_ref, agg_ref, delta_ref, keep_ref, give_ref):
    delta = delta_ref[...]

    @pl.when(core_ref[0] == 0)
    def _():
        keep_ref[...] = mm_tn(hid_ref[...], delta)
        give_ref[...] = mm_tn(agg_ref[...], delta).astype(jnp.bfloat16)

    @pl.when(core_ref[0] != 0)
    def _():
        keep_ref[...] = mm_tn(agg_ref[...], delta)
        give_ref[...] = mm_tn(hid_ref[...], delta).astype(jnp.bfloat16)


def per_device(
    features, cotangent, self_weight, neigh_weight, block_val, block_col, send_idx, send_count
):
    outer = lax.axis_size("gx")
    inner = lax.axis_size("gy")
    devices = outer * inner
    nodes, width = features.shape
    tile = block_val.shape[2]
    layers = self_weight.shape[0]
    slots = send_idx.shape[2]
    halo = devices * slots
    ext_tiles = (nodes + halo) // tile
    scale = 1.0 / math.sqrt(nodes * devices)
    bf16, f32 = jnp.bfloat16, jnp.float32

    def shape(rows, dtype):
        return jax.ShapeDtypeStruct((rows, width), dtype)

    def layer_spec(layer):
        return pl.BlockSpec((1, width, width), lambda i, layer=layer: (layer, 0, 0))

    def whole(array):
        return pl.BlockSpec(array.shape, lambda i, n=array.ndim: (0,) * n)

    def call(body, name, args, outs, scratch=(), layer=None, flops=0):
        specs = []
        for array in args:
            if array is block_col or array.ndim == 1:
                specs.append(SMEM)
            elif array is self_weight or array is neigh_weight:
                specs.append(layer_spec(layer))
            else:
                specs.append(whole(array))
        moved = sum(math.prod(o.shape) * o.dtype.itemsize for o in outs)
        return pl.pallas_call(
            body,
            grid=(1,),
            name=name,
            in_specs=specs,
            out_specs=[whole(o) for o in outs],
            out_shape=list(outs),
            scratch_shapes=list(scratch),
            cost_estimate=pl.CostEstimate(
                flops=flops, bytes_accessed=2 * moved, transcendentals=0
            ),
            compiler_params=pltpu.CompilerParams(vmem_limit_bytes=24 << 20),
        )(*args)

    def exchange(rows):
        blocks = rows.reshape(devices, slots, width)
        return lax.all_to_all(blocks, AXES, 0, 0, tiled=True).reshape(halo, width)

    position = lax.axis_index("gy")
    core = position & 1
    core_arg = core.reshape(1)
    ext_scratch = pltpu.VMEM((ext_tiles, tile, width), bf16)
    acc_scratch = pltpu.VMEM((ext_tiles, tile, width), f32)
    big = 8 * nodes * width * width

    bits = list(range(1, inner.bit_length() - 1))
    turn = bits[len(bits) // 2 :] + bits[: len(bits) // 2]
    gx_bits = list(range(outer.bit_length() - 1))

    def flip(array, even, odd):
        perm = [(j, j ^ (1 << (odd if j & 1 else even))) for j in range(inner)]
        return lax.ppermute(array, "gy", perm)

    def side(even, odd):
        return jnp.where(core == 0, (position >> even) & 1, (position >> odd) & 1)

    def reduce_all(keep, give):
        total = keep + flip(give, 0, 0).astype(f32)
        for even, odd in zip(bits, turn):
            half = total.shape[0] // 2
            b = side(even, odd)
            mine = lax.dynamic_slice(total, (b * half, 0), (half, width))
            theirs = lax.dynamic_slice(total, ((1 - b) * half, 0), (half, width))
            total = mine + flip(theirs.astype(bf16), even, odd).astype(f32)
        for bit in gx_bits:
            mine = total.astype(bf16)
            perm = [(j, j ^ (1 << bit)) for j in range(outer)]
            total = mine.astype(f32) + lax.ppermute(mine, "gx", perm).astype(f32)
        piece = (total * scale).astype(bf16)
        for even, odd in zip(bits[::-1], turn[::-1]):
            b = side(even, odd)
            got = flip(piece, even, odd)
            piece = jnp.where(
                b == 0, jnp.concatenate([piece, got]), jnp.concatenate([got, piece])
            )
        other = flip(piece, 0, 0)
        return jnp.where(core == 0, piece, other), jnp.where(core == 0, other, piece)

    row, col, send = call(
        first_kernel,
        "first",
        (send_idx.reshape(devices, slots), send_count, features),
        (
            jax.ShapeDtypeStruct((1, halo), jnp.int32),
            jax.ShapeDtypeStruct((halo, 1), jnp.int32),
            shape(halo, bf16),
        ),
    )
    hiddens, aggregates, slopes, deltas = [features], [], [], [None] * layers
    hidden = features
    for layer in range(layers - 1):
        arrived = exchange(send)
        aggregate, slope, hidden, send = call(
            middle_kernel,
            f"forward{layer}",
            (block_col, hidden, arrived, block_val, self_weight, neigh_weight, col),
            (shape(nodes, bf16), shape(nodes, f32), shape(nodes, bf16), shape(halo, bf16)),
            (ext_scratch,),
            layer,
            big,
        )
        hiddens.append(hidden)
        aggregates.append(aggregate)
        slopes.append(slope)
    arrived = exchange(send)
    aggregate, delta, outgoing, base = call(
        last_kernel,
        "turn",
        (block_col, hidden, arrived, block_val, self_weight, neigh_weight, cotangent),
        (shape(nodes, bf16), shape(nodes, bf16), shape(halo, bf16), shape(nodes, f32)),
        (ext_scratch, acc_scratch),
        layers - 1,
        2 * big,
    )
    aggregates.append(aggregate)
    self_list, neigh_list = [None] * layers, [None] * layers
    for layer in reversed(range(layers)):
        keep, give = call(
            weight_kernel,
            f"weight{layer}",
            (core_arg, hiddens[layer], aggregates[layer], delta),
            (shape(width, f32), shape(width, bf16)),
            flops=4 * nodes * width * width,
        )
        self_list[layer], neigh_list[layer] = reduce_all(keep, give)
        arrived = exchange(outgoing)
        if layer:
            delta, outgoing, base = call(
                backward_kernel,
                f"backward{layer - 1}",
                (block_col, arrived, base, slopes[layer - 1], row, block_val)
                + (self_weight, neigh_weight),
                (shape(nodes, bf16), shape(halo, bf16), shape(nodes, f32)),
                (acc_scratch,),
                layer - 1,
                big,
            )
    (grad,) = call(final_kernel, "final", (arrived, base, row), (shape(nodes, bf16),))
    return jnp.stack(self_list), jnp.stack(neigh_list), grad


def solution(mesh):
    return jax.shard_map(
        per_device,
        mesh=mesh,
        in_specs=(
            P(AXES, None),
            P(AXES, None),
            P(),
            P(),
            P(AXES, None, None, None),
            P(AXES, None),
            P(AXES, None, None),
            P(AXES, None),
        ),
        out_specs=(P(), P(), P(AXES, None)),
        check_vma=False,
    )
```

time: 402 us -> 196 us (0.49)
  waiting for transfers between devices: 186 us -> 54.3 us
  matrix products: 39.5 us -> 0 us
  blocking collectives: 72.8 us -> 41.1 us
  Pallas kernels: 0 us -> 16 us
  between operations: 14.7 us -> 1.13 us
  other arithmetic: 19.4 us -> 13.8 us
  starting transfers between devices: 32.8 us -> 38.3 us
  local copies, waits for them, and re-layouts: 34.6 us -> 29.7 us
    psum x1 -> x0, waiting for transfers between devices: 118 us -> none  [per_device(): self_sum, neigh_sum = lax.psum((self_term, neigh_term), ('gx', 'gy'))]
    all_to_all x8 -> x4, waiting for transfers between devices: 68.3 us -> 26.4 us  [exchange(): return lax.all_to_all(blocks, AXES, 0, 0, tiled=True).reshape(halo, width)]
    dot_general x27 -> x0, matrix products: 39.5 us -> none  [the longest x3 8 us: spread_back(): jnp.einsum('cn,njd->cjd', onehot, contrib.reshape(-1, tile, width), preci...]
    all_to_all x4 -> x2, blocking collectives: 72.8 us -> 41.1 us  [exchange(): return lax.all_to_all(blocks, AXES, 0, 0, tiled=True).reshape(halo, width)]
    ppermute x0 -> x24, waiting for transfers between devices: none -> 28 us  [the longest x18 16.6 us: flip(): return lax.ppermute(array, 'gy', perm)]
    ppermute x0 -> x24, starting transfers between devices: none -> 25.1 us  [the longest x18 17.3 us: flip(): return lax.ppermute(array, 'gy', perm)]
    unnamed x41 -> x83, local copies, waits for them, and re-layouts: 4.99 us -> 28.1 us
    all_to_all x8 -> x4, starting transfers between devices: 32.8 us -> 13.3 us  [exchange(): return lax.all_to_all(blocks, AXES, 0, 0, tiled=True).reshape(halo, width)]
  transfers between devices with their start and end apart: 9 -> 28, of which waited for: 9 -> 11; matrix products, arithmetic and copies ran while one was open for 7% -> 6% of each run, Pallas kernels for 0% -> 4%
where the time goes in v1:
time: 196 us; the launch traced here: 194 us
  waiting for transfers between devices  54.3 us (28%)
  blocking collectives  41.1 us (21%)
  starting transfers between devices  38.3 us (20%)
  local copies, waits for them, and re-layouts  29.7 us (15%)
  Pallas kernels  16 us (8%)
  other arithmetic  13.8 us (7%)
    all_to_all x2, blocking collectives, exchange(): return lax.all_to_all(blocks, AXES, 0, 0, tiled=True).reshape(halo, width)  41.1 us
    unnamed x83, local copies, waits for them, and re-layouts  28.1 us
    all_to_all x4, waiting for transfers between devices, exchange(): return lax.all_to_all(blocks, AXES, 0, 0, tiled=True).reshape(halo, width)  26.4 us
    ppermute x18, starting transfers between devices, flip(): return lax.ppermute(array, 'gy', perm)  17.3 us
    ppermute x18, waiting for transfers between devices, flip(): return lax.ppermute(array, 'gy', perm)  16.6 us
    pallas_call x10, Pallas kernels, call(): pl.pallas_call(body, grid=(1,), name=name, in_specs=specs, out_specs=[who...  16 us
    all_to_all x4, starting transfers between devices, exchange(): return lax.all_to_all(blocks, AXES, 0, 0, tiled=True).reshape(halo, width)  13.3 us
    ppermute x6, waiting for transfers between devices, reduce_all(): total = mine.astype(f32) + lax.ppermute(mine, 'gx', perm).astype(f32)  11.4 us
  transfers between devices with their start and end apart: 28, of which 11 were waited for; matrix products, arithmetic and copies ran while one was open for 6% of the time, Pallas kernels for 4%

profile of v1, /device:TPU:0, one launch (start us, length us, event | category | flops | bytes accessed | tf_op | source)
XLA Modules:
  0.0 194.4 jit_solution(3943411605765591266)
XLA Ops:
  3.6 22.7 %all_to_all.30 = bf16[32,16,512]{2,1,0:T(8,128)(2,1)S(1)} all-to-all(bf16[32,16,512]{2,1,0:T(8,128)(2,1)S(1)} %bitcast.33), channel_id=1, replica_groups=mesh['gx'=4,'gy'=8] {'gx','gy'}, dimensions={0} | all-to-all | bytes 1048576 | tf_op jit(solution)/shard_map/all_to_all | solution.py:211
  30.8 1.7 forward0.1
  32.6 18.4 %all_to_all.31 = bf16[32,16,512]{2,1,0:T(8,128)(2,1)S(1)} all-to-all(bf16[32,16,512]{2,1,0:T(8,128)(2,1)S(1)} %bitcast.32), channel_id=1, replica_groups=mesh['gx'=4,'gy'=8] {'gx','gy'}, dimensions={0} | all-to-all | bytes 1048576 | tf_op jit(solution)/shard_map/all_to_all | solution.py:211
  55.7 3.3 %all-to-all-start.2 = ((bf16[32,16,512]{2,1,0:T(8,128)(2,1)}), bf16[32,16,512]{2,1,0:T(8,128)(2,1)}, u32[]{:S(2)}, u32[]{:S(2)}) async-start(bf16[32,16,512]{2,1,0:T(8,128)(2,1)} %bitcast.31), calls=%async_computation.2 | async-start | bytes 1048576 | tf_op jit(solution)/shard_map/all_to_all | solution.py:211
  59.1 15.6 %all-to-all-done.2 = bf16[32,16,512]{2,1,0:T(8,128)(2,1)} async-done(((bf16[32,16,512]{2,1,0:T(8,128)(2,1)}), bf16[32,16,512]{2,1,0:T(8,128)(2,1)}, u32[]{:S(2)}, u32[]{:S(2)}) %all-to-all-start.2) | async-done | bytes 524320 | tf_op jit(solution)/shard_map/all_to_all | solution.py:211
  76.6 2.8 %turn.1 = (bf16[256,512]{1,0:T(8,128)(2,1)S(1)}, bf16[256,512]{1,0:T(8,128)(2,1)S(1)}, bf16[512,512]{1,0:T(8,128)(2,1)S(1)}, f32[256,512]{1,0:T(8,128)S(1)}) custom-call(s32[2,4]{1,0:T(2,128)S(1)} %copy-done.29, bf16[256,512]{1,0:T(8,128)(2,1)S(1)} %copy-done.27, bf16[512,512]{1,0:T(8,128)(2,1)} %bitcast.7.arr_ref, bf16[2,4,128,128]{3,2,1,0:T(8,128)(2,1)S(1)} %copy-done.5, ...), custom_call_target="tpu_custom_call" | custom-call | flops 1073741824 | bytes 3145728 | tf_op jit(solution)/shard_map/turn/pallas_call | solution.py:195
  83.2 3.3 %all-to-all-start.3 = ((bf16[32,16,512]{2,1,0:T(8,128)(2,1)}), bf16[32,16,512]{2,1,0:T(8,128)(2,1)}, u32[]{:S(2)}, u32[]{:S(2)}) async-start(bf16[32,16,512]{2,1,0:T(8,128)(2,1)} %bitcast.29), calls=%async_computation.3 | async-start | bytes 1048576 | tf_op jit(solution)/shard_map/all_to_all | solution.py:211
  91.4 10.8 %all-to-all-done.3 = bf16[32,16,512]{2,1,0:T(8,128)(2,1)} async-done(((bf16[32,16,512]{2,1,0:T(8,128)(2,1)}), bf16[32,16,512]{2,1,0:T(8,128)(2,1)}, u32[]{:S(2)}, u32[]{:S(2)}) %all-to-all-start.3) | async-done | bytes 524320 | tf_op jit(solution)/shard_map/all_to_all | solution.py:211
  104.2 2.2 %backward1.1 = (bf16[256,512]{1,0:T(8,128)(2,1)S(1)}, bf16[512,512]{1,0:T(8,128)(2,1)S(1)}, f32[256,512]{1,0:T(8,128)S(1)}) custom-call(s32[2,4]{1,0:T(2,128)S(1)} %copy-done.29, bf16[512,512]{1,0:T(8,128)(2,1)} %bitcast.9.arr_ref, f32[256,512]{1,0:T(8,128)S(1)} %copy-done.17, f32[256,512]{1,0:T(8,128)S(1)} %copy-done.15, ...), custom_call_target="tpu_custom_call" | custom-call | flops 536870912 | bytes 2621440 | tf_op jit(solution)/shard_map/backward1/pallas_call | solution.py:195
  108.8 3.3 %all-to-all-start.4 = ((bf16[32,16,512]{2,1,0:T(8,128)(2,1)}), bf16[32,16,512]{2,1,0:T(8,128)(2,1)}, u32[]{:S(2)}, u32[]{:S(2)}) async-start(bf16[32,16,512]{2,1,0:T(8,128)(2,1)} %bitcast.30), calls=%async_computation.4 | async-start | bytes 1048576 | tf_op jit(solution)/shard_map/all_to_all | solution.py:211
  119.3 1.7 collective-permute-start.18
  121.0 4.2 %collective-permute-done.18 = bf16[128,512]{1,0:T(8,128)(2,1)} collective-permute-done((bf16[128,512]{1,0:T(8,128)(2,1)S(1)}, bf16[128,512]{1,0:T(8,128)(2,1)}, u32[]{:S(2)}, u32[]{:S(2)}) %collective-permute-start.18) | collective-permute-done | bytes 131104 | tf_op jit(solution)/shard_map/ppermute | solution.py:226
  134.4 2.9 %backward0.1 = (bf16[256,512]{1,0:T(8,128)(2,1)S(1)}, bf16[512,512]{1,0:T(8,128)(2,1)}, f32[256,512]{1,0:T(8,128)S(1)}) custom-call(s32[2,4]{1,0:T(2,128)S(1)} %copy-done.29, bf16[512,512]{1,0:T(8,128)(2,1)} %bitcast.11.arr_ref, f32[256,512]{1,0:T(8,128)S(1)} %copy-done.19, f32[256,512]{1,0:T(8,128)S(1)} %copy-done.13, ...), custom_call_target="tpu_custom_call" | custom-call | flops 536870912 | bytes 2621440 | tf_op jit(solution)/shard_map/backward0/pallas_call | solution.py:195
  139.7 2.7 %collective-permute-start.20 = (bf16[128,512]{1,0:T(8,128)(2,1)S(1)}, bf16[128,512]{1,0:T(8,128)(2,1)S(1)}, u32[]{:S(2)}, u32[]{:S(2)}) collective-permute-start(bf16[128,512]{1,0:T(8,128)(2,1)S(1)} %add_convert_fusion), channel_id=1, source_target_pairs={{0,16},{8,24},{16,0},{24,8},{1,17},{9,25},{17,1},{25,9},{2,18},{10... | collective-permute-start | bytes 393224 | tf_op jit(solution)/shard_map/ppermute | solution.py:242
  145.8 3.5 %collective-permute-done.20 = bf16[128,512]{1,0:T(8,128)(2,1)S(1)} collective-permute-done((bf16[128,512]{1,0:T(8,128)(2,1)S(1)}, bf16[128,512]{1,0:T(8,128)(2,1)S(1)}, u32[]{:S(2)}, u32[]{:S(2)}) %collective-permute-start.20) | collective-permute-done | bytes 131104 | tf_op jit(solution)/shard_map/ppermute | solution.py:242
  152.4 3.6 %collective-permute-done.11 = bf16[128,512]{1,0:T(8,128)(2,1)S(1)} collective-permute-done((bf16[128,512]{1,0:T(8,128)(2,1)S(1)}, bf16[128,512]{1,0:T(8,128)(2,1)S(1)}, u32[]{:S(2)}, u32[]{:S(2)}) %collective-permute-start.11) | collective-permute-done | bytes 131104 | tf_op jit(solution)/shard_map/ppermute | solution.py:242
  157.3 1.9 %collective-permute-start.3 = (bf16[128,512]{1,0:T(8,128)(2,1)S(1)}, bf16[128,512]{1,0:T(8,128)(2,1)S(1)}, u32[]{:S(2)}, u32[]{:S(2)}) collective-permute-start(bf16[128,512]{1,0:T(8,128)(2,1)S(1)} %add_convert_fusion.5), channel_id=1, source_target_pairs={{0,8},{8,0},{16,24},{24,16},{1,9},{9,1},{17,25},{25,17},{2,10},{10... | collective-permute-start | bytes 393224 | tf_op jit(solution)/shard_map/ppermute | solution.py:242
  159.2 4.3 %collective-permute-done.12 = bf16[128,512]{1,0:T(8,128)(2,1)S(1)} collective-permute-done((bf16[128,512]{1,0:T(8,128)(2,1)S(1)}, bf16[128,512]{1,0:T(8,128)(2,1)S(1)}, u32[]{:S(2)}, u32[]{:S(2)}) %collective-permute-start.12) | collective-permute-done | bytes 131104 | tf_op jit(solution)/shard_map/ppermute | solution.py:242
  165.3 2.0 %collective-permute-start.22 = (bf16[256,512]{1,0:T(8,128)(2,1)S(1)}, bf16[256,512]{1,0:T(8,128)(2,1)S(1)}, u32[]{:S(2)}, u32[]{:S(2)}) collective-permute-start(bf16[256,512]{1,0:T(8,128)(2,1)S(1)} %maximum_select_fusion.5), channel_id=1, source_target_pairs={{0,2},{1,5},{2,0},{3,7},{4,6},{5,1},{6,4},{7,3},{8,10},{9,13},{10,... | collective-permute-start | bytes 786440 | tf_op jit(solution)/shard_map/ppermute | solution.py:226
  167.3 3.3 %all-to-all-start.5 = ((bf16[32,16,512]{2,1,0:T(8,128)(2,1)}), bf16[32,16,512]{2,1,0:T(8,128)(2,1)S(1)}, u32[]{:S(2)}, u32[]{:S(2)}) async-start(bf16[32,16,512]{2,1,0:T(8,128)(2,1)} %bitcast.18), calls=%async_computation.5 | async-start | bytes 1048576 | tf_op jit(solution)/shard_map/all_to_all | solution.py:211
  170.7 1.8 collective-permute-start.14
  174.5 6.5 %collective-permute-done.5 = bf16[128,512]{1,0:T(8,128)(2,1)S(1)} collective-permute-done((bf16[128,512]{1,0:T(8,128)(2,1)S(1)}, bf16[128,512]{1,0:T(8,128)(2,1)S(1)}, u32[]{:S(2)}, u32[]{:S(2)}) %collective-permute-start.5) | collective-permute-done | bytes 131104 | tf_op jit(solution)/shard_map/ppermute | solution.py:226
  182.7 5.2 %collective-permute-done.6 = bf16[256,512]{1,0:T(8,128)(2,1)S(1)} collective-permute-done((bf16[256,512]{1,0:T(8,128)(2,1)S(1)}, bf16[256,512]{1,0:T(8,128)(2,1)S(1)}, u32[]{:S(2)}, u32[]{:S(2)}) %collective-permute-start.6) | collective-permute-done | bytes 262176 | tf_op jit(solution)/shard_map/ppermute | solution.py:226
  192.4 2.0 %pad_maximum_fusion = (bf16[3,512,512]{2,1,0:T(8,128)(2,1)}, bf16[3,512,512]{2,1,0:T(8,128)(2,1)}) fusion(bf16[1,512,512]{2,1,0:T(8,128)(2,1)S(1)} %get-tuple-element.62, bf16[1,512,512]{2,1,0:T(8,128)(2,1)S(1)} %get-tuple-element.60, bf16[1,512,512]{2,1,0:T(8,128)(2,1)S(1)} %get-tuple-element.58, bf16[1,512,512]{2,1,0:T(8,128)(2,1)S(1)} %get-tuple-element.61, ...), kind=kLoop, calls=%fused_computation | loop fusion | flops 3145728 | bytes 6291456 | tf_op jit(solution)/shard_map/stack | solution.py:313
  (158 shorter events, 63.4 us)
Async XLA Ops:
  55.7 18.9 %all-to-all-start.2 = ((bf16[32,16,512]{2,1,0:T(8,128)(2,1)}), bf16[32,16,512]{2,1,0:T(8,128)(2,1)}, u32[]{:S(2)}, u32[]{:S(2)}) async-start(bf16[32,16,512]{2,1,0:T(8,128)(2,1)} %bitcast.31), calls=%async_computation.2 | async-start | bytes 1048576 | tf_op jit(solution)/shard_map/all_to_all | solution.py:211
  83.2 18.9 %all-to-all-start.3 = ((bf16[32,16,512]{2,1,0:T(8,128)(2,1)}), bf16[32,16,512]{2,1,0:T(8,128)(2,1)}, u32[]{:S(2)}, u32[]{:S(2)}) async-start(bf16[32,16,512]{2,1,0:T(8,128)(2,1)} %bitcast.29), calls=%async_computation.3 | async-start | bytes 1048576 | tf_op jit(solution)/shard_map/all_to_all | solution.py:211
  89.8 27.4 %collective-permute-start.17 = (bf16[256,512]{1,0:T(8,128)(2,1)}, bf16[256,512]{1,0:T(8,128)(2,1)}, u32[]{:S(2)}, u32[]{:S(2)}) collective-permute-start(bf16[256,512]{1,0:T(8,128)(2,1)} %dynamic-slice_convert_fusion), channel_id=1, source_target_pairs={{0,2},{1,5},{2,0},{3,7},{4,6},{5,1},{6,4},{7,3},{8,10},{9,13},{10,... | collective-permute-start | bytes 786440 | tf_op jit(solution)/shard_map/ppermute | solution.py:226
  108.8 23.5 %all-to-all-start.4 = ((bf16[32,16,512]{2,1,0:T(8,128)(2,1)}), bf16[32,16,512]{2,1,0:T(8,128)(2,1)}, u32[]{:S(2)}, u32[]{:S(2)}) async-start(bf16[32,16,512]{2,1,0:T(8,128)(2,1)} %bitcast.30), calls=%async_computation.4 | async-start | bytes 1048576 | tf_op jit(solution)/shard_map/all_to_all | solution.py:211
  117.2 10.7 %collective-permute-start.8 = (bf16[512,512]{1,0:T(8,128)(2,1)}, bf16[512,512]{1,0:T(8,128)(2,1)}, u32[]{:S(2)}, u32[]{:S(2)}) collective-permute-start(bf16[512,512]{1,0:T(8,128)(2,1)} %get-tuple-element.50), channel_id=1, source_target_pairs={{0,1},{1,0},{2,3},{3,2},{4,5},{5,4},{6,7},{7,6},{8,9},{9,8},{10,11... | collective-permute-start | bytes 1572872 | tf_op jit(solution)/shard_map/ppermute | solution.py:226
  119.3 5.9 %collective-permute-start.18 = (bf16[128,512]{1,0:T(8,128)(2,1)S(1)}, bf16[128,512]{1,0:T(8,128)(2,1)}, u32[]{:S(2)}, u32[]{:S(2)}) collective-permute-start(bf16[128,512]{1,0:T(8,128)(2,1)S(1)} %dynamic-slice_convert_fusion.3), channel_id=1, source_target_pairs={{0,4},{1,3},{2,6},{3,1},{4,0},{5,7},{6,2},{7,5},{8,12},{9,11},{10,... | collective-permute-start | bytes 393224 | tf_op jit(solution)/shard_map/ppermute | solution.py:226
  126.2 12.5 %collective-permute-start.19 = (bf16[128,512]{1,0:T(8,128)(2,1)S(1)}, bf16[128,512]{1,0:T(8,128)(2,1)}, u32[]{:S(2)}, u32[]{:S(2)}) collective-permute-start(bf16[128,512]{1,0:T(8,128)(2,1)S(1)} %add_convert_fusion.1), channel_id=1, source_target_pairs={{0,8},{8,0},{16,24},{24,16},{1,9},{9,1},{17,25},{25,17},{2,10},{10... | collective-permute-start | bytes 393224 | tf_op jit(solution)/shard_map/ppermute | solution.py:242
  131.1 11.2 %collective-permute-start.9 = (bf16[256,512]{1,0:T(8,128)(2,1)}, bf16[256,512]{1,0:T(8,128)(2,1)}, u32[]{:S(2)}, u32[]{:S(2)}) collective-permute-start(bf16[256,512]{1,0:T(8,128)(2,1)} %dynamic-slice_convert_fusion.1), channel_id=1, source_target_pairs={{0,2},{1,5},{2,0},{3,7},{4,6},{5,1},{6,4},{7,3},{8,10},{9,13},{10,... | collective-permute-start | bytes 786440 | tf_op jit(solution)/shard_map/ppermute | solution.py:226
  138.6 6.3 %collective-permute-start = (bf16[512,512]{1,0:T(8,128)(2,1)S(1)}, bf16[512,512]{1,0:T(8,128)(2,1)S(1)}, u32[]{:S(2)}, u32[]{:S(2)}) collective-permute-start(bf16[512,512]{1,0:T(8,128)(2,1)S(1)} %get-tuple-element.46), channel_id=1, source_target_pairs={{0,1},{1,0},{2,3},{3,2},{4,5},{5,4},{6,7},{7,6},{8,9},{9,8},{10,11... | collective-permute-start | bytes 1572872 | tf_op jit(solution)/shard_map/ppermute | solution.py:226
  139.7 9.7 %collective-permute-start.20 = (bf16[128,512]{1,0:T(8,128)(2,1)S(1)}, bf16[128,512]{1,0:T(8,128)(2,1)S(1)}, u32[]{:S(2)}, u32[]{:S(2)}) collective-permute-start(bf16[128,512]{1,0:T(8,128)(2,1)S(1)} %add_convert_fusion), channel_id=1, source_target_pairs={{0,16},{8,24},{16,0},{24,8},{1,17},{9,25},{17,1},{25,9},{2,18},{10... | collective-permute-start | bytes 393224 | tf_op jit(solution)/shard_map/ppermute | solution.py:242
  143.5 7.4 %collective-permute-start.10 = (bf16[128,512]{1,0:T(8,128)(2,1)S(1)}, bf16[128,512]{1,0:T(8,128)(2,1)S(1)}, u32[]{:S(2)}, u32[]{:S(2)}) collective-permute-start(bf16[128,512]{1,0:T(8,128)(2,1)S(1)} %dynamic-slice_convert_fusion.4), channel_id=1, source_target_pairs={{0,4},{1,3},{2,6},{3,1},{4,0},{5,7},{6,2},{7,5},{8,12},{9,11},{10,... | collective-permute-start | bytes 393224 | tf_op jit(solution)/shard_map/ppermute | solution.py:226
  145.1 6.4 %collective-permute-start.1 = (bf16[256,512]{1,0:T(8,128)(2,1)S(1)}, bf16[256,512]{1,0:T(8,128)(2,1)S(1)}, u32[]{:S(2)}, u32[]{:S(2)}) collective-permute-start(bf16[256,512]{1,0:T(8,128)(2,1)S(1)} %dynamic-slice_convert_fusion.2), channel_id=1, source_target_pairs={{0,2},{1,5},{2,0},{3,7},{4,6},{5,1},{6,4},{7,3},{8,10},{9,13},{10,... | collective-permute-start | bytes 786440 | tf_op jit(solution)/shard_map/ppermute | solution.py:226
  149.4 15.8 %collective-permute-start.21 = (bf16[128,512]{1,0:T(8,128)(2,1)S(1)}, bf16[128,512]{1,0:T(8,128)(2,1)S(1)}, u32[]{:S(2)}, u32[]{:S(2)}) collective-permute-start(bf16[128,512]{1,0:T(8,128)(2,1)S(1)} %multiply_convert_fusion), channel_id=1, source_target_pairs={{0,4},{1,3},{2,6},{3,1},{4,0},{5,7},{6,2},{7,5},{8,12},{9,11},{10,... | collective-permute-start | bytes 393224 | tf_op jit(solution)/shard_map/ppermute | solution.py:226
  156.0 7.5 %collective-permute-start.12 = (bf16[128,512]{1,0:T(8,128)(2,1)S(1)}, bf16[128,512]{1,0:T(8,128)(2,1)S(1)}, u32[]{:S(2)}, u32[]{:S(2)}) collective-permute-start(bf16[128,512]{1,0:T(8,128)(2,1)S(1)} %add_convert_fusion.2), channel_id=1, source_target_pairs={{0,16},{8,24},{16,0},{24,8},{1,17},{9,25},{17,1},{25,9},{2,18},{10... | collective-permute-start | bytes 393224 | tf_op jit(solution)/shard_map/ppermute | solution.py:242
  157.3 7.8 %collective-permute-start.3 = (bf16[128,512]{1,0:T(8,128)(2,1)S(1)}, bf16[128,512]{1,0:T(8,128)(2,1)S(1)}, u32[]{:S(2)}, u32[]{:S(2)}) collective-permute-start(bf16[128,512]{1,0:T(8,128)(2,1)S(1)} %add_convert_fusion.5), channel_id=1, source_target_pairs={{0,8},{8,0},{16,24},{24,16},{1,9},{9,1},{17,25},{25,17},{2,10},{10... | collective-permute-start | bytes 393224 | tf_op jit(solution)/shard_map/ppermute | solution.py:242
  163.5 7.1 %collective-permute-start.13 = (bf16[128,512]{1,0:T(8,128)(2,1)S(1)}, bf16[128,512]{1,0:T(8,128)(2,1)S(1)}, u32[]{:S(2)}, u32[]{:S(2)}) collective-permute-start(bf16[128,512]{1,0:T(8,128)(2,1)S(1)} %multiply_convert_fusion.1), channel_id=1, source_target_pairs={{0,4},{1,3},{2,6},{3,1},{4,0},{5,7},{6,2},{7,5},{8,12},{9,11},{10,... | collective-permute-start | bytes 393224 | tf_op jit(solution)/shard_map/ppermute | solution.py:226
  165.1 7.4 %collective-permute-start.4 = (bf16[128,512]{1,0:T(8,128)(2,1)S(1)}, bf16[128,512]{1,0:T(8,128)(2,1)S(1)}, u32[]{:S(2)}, u32[]{:S(2)}) collective-permute-start(bf16[128,512]{1,0:T(8,128)(2,1)S(1)} %add_convert_fusion.4), channel_id=1, source_target_pairs={{0,16},{8,24},{16,0},{24,8},{1,17},{9,25},{17,1},{25,9},{2,18},{10... | collective-permute-start | bytes 393224 | tf_op jit(solution)/shard_map/ppermute | solution.py:242
  165.3 8.9 %collective-permute-start.22 = (bf16[256,512]{1,0:T(8,128)(2,1)S(1)}, bf16[256,512]{1,0:T(8,128)(2,1)S(1)}, u32[]{:S(2)}, u32[]{:S(2)}) collective-permute-start(bf16[256,512]{1,0:T(8,128)(2,1)S(1)} %maximum_select_fusion.5), channel_id=1, source_target_pairs={{0,2},{1,5},{2,0},{3,7},{4,6},{5,1},{6,4},{7,3},{8,10},{9,13},{10,... | collective-permute-start | bytes 786440 | tf_op jit(solution)/shard_map/ppermute | solution.py:226
  167.3 21.6 %all-to-all-start.5 = ((bf16[32,16,512]{2,1,0:T(8,128)(2,1)}), bf16[32,16,512]{2,1,0:T(8,128)(2,1)S(1)}, u32[]{:S(2)}, u32[]{:S(2)}) async-start(bf16[32,16,512]{2,1,0:T(8,128)(2,1)} %bitcast.18), calls=%async_computation.5 | async-start | bytes 1048576 | tf_op jit(solution)/shard_map/all_to_all | solution.py:211
  170.7 11.7 %collective-permute-start.14 = (bf16[256,512]{1,0:T(8,128)(2,1)S(1)}, bf16[256,512]{1,0:T(8,128)(2,1)S(1)}, u32[]{:S(2)}, u32[]{:S(2)}) collective-permute-start(bf16[256,512]{1,0:T(8,128)(2,1)S(1)} %maximum_select_fusion.4), channel_id=1, source_target_pairs={{0,2},{1,5},{2,0},{3,7},{4,6},{5,1},{6,4},{7,3},{8,10},{9,13},{10,... | collective-permute-start | bytes 786440 | tf_op jit(solution)/shard_map/ppermute | solution.py:226
  172.6 8.3 %collective-permute-start.5 = (bf16[128,512]{1,0:T(8,128)(2,1)S(1)}, bf16[128,512]{1,0:T(8,128)(2,1)S(1)}, u32[]{:S(2)}, u32[]{:S(2)}) collective-permute-start(bf16[128,512]{1,0:T(8,128)(2,1)S(1)} %multiply_convert_fusion.2), channel_id=1, source_target_pairs={{0,4},{1,3},{2,6},{3,1},{4,0},{5,7},{6,2},{7,5},{8,12},{9,11},{10,... | collective-permute-start | bytes 393224 | tf_op jit(solution)/shard_map/ppermute | solution.py:226
  174.4 14.5 %collective-permute-start.23 = (bf16[512,512]{1,0:T(8,128)(2,1)S(1)}, bf16[512,512]{1,0:T(8,128)(2,1)S(1)}, u32[]{:S(2)}, u32[]{:S(2)}) collective-permute-start(bf16[512,512]{1,0:T(8,128)(2,1)S(1)} %maximum_select_fusion.2), channel_id=1, source_target_pairs={{0,1},{1,0},{2,3},{3,2},{4,5},{5,4},{6,7},{7,6},{8,9},{9,8},{10,11... | collective-permute-start | bytes 1572872 | tf_op jit(solution)/shard_map/ppermute | solution.py:226
  181.0 6.9 %collective-permute-start.6 = (bf16[256,512]{1,0:T(8,128)(2,1)S(1)}, bf16[256,512]{1,0:T(8,128)(2,1)S(1)}, u32[]{:S(2)}, u32[]{:S(2)}) collective-permute-start(bf16[256,512]{1,0:T(8,128)(2,1)S(1)} %maximum_select_fusion.3), channel_id=1, source_target_pairs={{0,2},{1,5},{2,0},{3,7},{4,6},{5,1},{6,4},{7,3},{8,10},{9,13},{10,... | collective-permute-start | bytes 786440 | tf_op jit(solution)/shard_map/ppermute | solution.py:226
  182.6 7.4 %collective-permute-start.15 = (bf16[512,512]{1,0:T(8,128)(2,1)S(1)}, bf16[512,512]{1,0:T(8,128)(2,1)}, u32[]{:S(2)}, u32[]{:S(2)}) collective-permute-start(bf16[512,512]{1,0:T(8,128)(2,1)S(1)} %maximum_select_fusion.1), channel_id=1, source_target_pairs={{0,1},{1,0},{2,3},{3,2},{4,5},{5,4},{6,7},{7,6},{8,9},{9,8},{10,11... | collective-permute-start | bytes 1572872 | tf_op jit(solution)/shard_map/ppermute | solution.py:226
  (45 other events, 210.1 us)

commit v2 on v1

v2 whole, which is shorter than its diff:
```python
import functools
import math

import jax
import jax.numpy as jnp
from jax import lax
from jax.experimental import pallas as pl
from jax.experimental.pallas import tpu as pltpu
from jax.sharding import PartitionSpec as P


AXES = ("gx", "gy")
SMEM = pl.BlockSpec(memory_space=pltpu.SMEM)
HBM = pl.BlockSpec(memory_space=pltpu.HBM)
ANY = pl.BlockSpec(memory_space=pl.ANY)


def mm(a, b):
    return jnp.dot(a, b, preferred_element_type=jnp.float32)


def mm_tn(a, b):
    return lax.dot_general(a, b, (((0,), (0,)), ((), ())), preferred_element_type=jnp.float32)


def mm_nt(a, b):
    return lax.dot_general(a, b, (((1,), (1,)), ((), ())), preferred_element_type=jnp.float32)


def iota(shape, dim):
    return lax.broadcasted_iota(jnp.int32, shape, dim)


def ones_where(mask):
    return jnp.where(mask, 1.0, 0.0).astype(jnp.bfloat16)


def pick_rows(col, table):
    hot = ones_where(iota((col.shape[0], table.shape[0]), 1) == col)
    return mm(hot, table).astype(jnp.bfloat16)


def return_rows(row, arrived, nodes):
    hot = ones_where(iota((nodes, row.shape[1]), 0) == row)
    return mm(hot, arrived)


class Copies:
    def __init__(self, sems):
        self.sems, self.used, self.stores = sems, 0, []

    def start(self, source, target):
        copy = pltpu.make_async_copy(source, target, self.sems.at[self.used])
        self.used += 1
        copy.start()
        return copy

    def store(self, source, target):
        self.stores.append(self.start(source, target))

    def finish(self):
        for copy in self.stores:
            copy.wait()


def first_kernel(idx, cnt, x, row_out, col_out, send_out, idx_v, cnt_v, x_v, row_v, col_v, send_v, sems):
    go = Copies(sems)
    loads = [go.start(idx, idx_v), go.start(cnt, cnt_v), go.start(x, x_v)]
    for load in loads[:2]:
        load.wait()
    _, peers, slots = idx.shape
    total = peers * slots
    eye = iota((peers, peers), 0) == iota((peers, peers), 1)
    counts = jnp.broadcast_to(cnt_v[...].astype(jnp.float32), (peers, peers))
    count_col = jnp.sum(jnp.where(eye, counts, 0.0), axis=1, keepdims=True)
    live = iota((peers, slots), 1).astype(jnp.float32) < count_col
    code = jnp.where(live, idx_v[0].astype(jnp.float32) + 1.0, 0.0).astype(jnp.bfloat16)
    start_t = iota((total, peers), 1) * slots
    place_t = iota((total, peers), 0)
    inside_t = ones_where((place_t >= start_t) & (place_t < start_t + slots))
    here = (iota((total, slots), 0) & (slots - 1)) == iota((total, slots), 1)
    col = jnp.sum(jnp.where(here, mm(inside_t, code), 0.0), axis=1, keepdims=True) - 1.0
    col = col.astype(jnp.int32)
    col_v[...] = col
    go.store(col_v, col_out)
    spread = ones_where((iota((slots, total), 1) & (slots - 1)) == iota((slots, total), 0))
    start = iota((peers, total), 0) * slots
    place = iota((peers, total), 1)
    inside = (place >= start) & (place < start + slots)
    row = jnp.sum(jnp.where(inside, mm(code, spread), 0.0), axis=0, keepdims=True) - 1.0
    row_v[...] = row.astype(jnp.int32)
    go.store(row_v, row_out)
    loads[2].wait()
    send_v[...] = pick_rows(col, x_v[...])
    go.store(send_v, send_out)
    go.finish()


def aggregate_into(agg_v, ext_v, cols, val_v):
    tiles, blocks, tile, _ = val_v.shape
    for r in range(tiles):
        total = mm(val_v[r, 0], ext_v[cols[r, 0]])
        for b in range(1, blocks):
            total += mm(val_v[r, b], ext_v[cols[r, b]])
        agg_v[r * tile : (r + 1) * tile, :] = total.astype(jnp.bfloat16)


def own_rows(ext_v, own):
    return ext_v[:own].reshape(own * ext_v.shape[1], ext_v.shape[2])


def forward_loads(go, layer, hid, arr, val, ws, wn, ext_v, val_v, ws_v, wn_v):
    own = hid.shape[0]
    return [
        go.start(hid, ext_v.at[pl.ds(0, own)]),
        go.start(ws.at[layer], ws_v),
        go.start(arr, ext_v.at[pl.ds(own, arr.shape[0])]),
        go.start(val, val_v),
        go.start(wn.at[layer], wn_v),
    ]


def pre_activation(loads, cols, own, ext_v, val_v, ws_v, wn_v, agg_v):
    loads[0].wait()
    loads[1].wait()
    pre = mm(own_rows(ext_v, own), ws_v[...])
    loads[2].wait()
    loads[3].wait()
    aggregate_into(agg_v, ext_v, cols, val_v)
    loads[4].wait()
    return pre + mm(agg_v[...], wn_v[...])


def middle_kernel(
    layer, cols, hid, arr, val, ws, wn, col, agg_out, slope_out, next_out, send_out,
    ext_v, val_v, ws_v, wn_v, col_v, agg_v, slope_v, next_v, send_v, sems,
):
    go = Copies(sems)
    loads = forward_loads(go, layer, hid, arr, val, ws, wn, ext_v, val_v, ws_v, wn_v)
    col_load = go.start(col, col_v)
    pre = pre_activation(loads, cols, hid.shape[0], ext_v, val_v, ws_v, wn_v, agg_v)
    go.store(agg_v, agg_out)
    sigma = jax.nn.sigmoid(pre)
    hidden = (pre * sigma).astype(jnp.bfloat16)
    next_v[...] = hidden
    go.store(next_v, next_out)
    slope_v[...] = sigma * (1.0 + pre * (1.0 - sigma))
    go.store(slope_v, slope_out)
    col_load.wait()
    send_v[...] = pick_rows(col_v[...], hidden)
    go.store(send_v, send_out)
    go.finish()


def spread_back(go, delta, cols, val_v, ws_v, wn_load, wn_v, halo_out, base_out, halo_v, base_v, acc_v):
    tiles, blocks, tile, _ = val_v.shape
    own = tiles
    acc_v[...] = jnp.zeros_like(acc_v)
    if wn_load is not None:
        wn_load.wait()
    upstream = mm_nt(delta, wn_v[...]).astype(jnp.bfloat16)
    for r in range(tiles):
        part = upstream[r * tile : (r + 1) * tile, :]
        for b in range(blocks):
            c = cols[r, b]
            acc_v[c] += mm_tn(val_v[r, b], part)
    halo_v[...] = acc_v[own:].astype(jnp.bfloat16)
    go.store(halo_v, halo_out)
    own_part = mm_nt(delta, ws_v[...])
    base_v[...] = own_part + own_rows(acc_v, own)
    go.store(base_v, base_out)


def last_kernel(
    layer, cols, hid, arr, val, ws, wn, cot, agg_out, delta_out, halo_out, base_out,
    ext_v, val_v, ws_v, wn_v, cot_v, agg_v, delta_v, halo_v, base_v, acc_v, sems,
):
    go = Copies(sems)
    loads = forward_loads(go, layer, hid, arr, val, ws, wn, ext_v, val_v, ws_v, wn_v)
    cot_load = go.start(cot, cot_v)
    pre = pre_activation(loads, cols, hid.shape[0], ext_v, val_v, ws_v, wn_v, agg_v)
    go.store(agg_v, agg_out)
    sigma = jax.nn.sigmoid(pre)
    slope = sigma * (1.0 + pre * (1.0 - sigma))
    cot_load.wait()
    delta = (cot_v[...].astype(jnp.float32) * slope).astype(jnp.bfloat16)
    delta_v[...] = delta
    go.store(delta_v, delta_out)
    spread_back(go, delta, cols, val_v, ws_v, None, wn_v, halo_out, base_out, halo_v, base_v, acc_v)
    go.finish()


def backward_kernel(
    layer, cols, arr, before, slope, row, val, ws, wn, delta_out, halo_out, base_out,
    arr_v, before_v, slope_v, row_v, val_v, ws_v, wn_v, delta_v, halo_v, base_v, acc_v, sems,
):
    go = Copies(sems)
    loads = [
        go.start(row, row_v),
        go.start(arr, arr_v),
        go.start(before, before_v),
        go.start(slope, slope_v),
    ]
    wn_load = go.start(wn.at[layer], wn_v)
    late = [go.start(val, val_v), go.start(ws.at[layer], ws_v)]
    for load in loads[:2]:
        load.wait()
    back = return_rows(row_v[...], arr_v[...], before.shape[0])
    for load in loads[2:]:
        load.wait()
    grad = (before_v[...] + back).astype(jnp.bfloat16)
    delta = (grad.astype(jnp.float32) * slope_v[...]).astype(jnp.bfloat16)
    delta_v[...] = delta
    go.store(delta_v, delta_out)
    for load in late:
        load.wait()
    spread_back(go, delta, cols, val_v, ws_v, wn_load, wn_v, halo_out, base_out, halo_v, base_v, acc_v)
    go.finish()


def final_kernel(arr, before, row, grad_out, arr_v, before_v, row_v, grad_v, sems):
    go = Copies(sems)
    loads = [go.start(row, row_v), go.start(arr, arr_v), go.start(before, before_v)]
    for load in loads:
        load.wait()
    back = return_rows(row_v[...], arr_v[...], before.shape[0])
    grad_v[...] = (before_v[...] + back).astype(jnp.bfloat16)
    go.store(grad_v, grad_out)
    go.finish()


def weight_kernel(core, hid, agg, delta, keep_out, give_out, hid_v, agg_v, delta_v, keep_v, give_v, sems):
    go = Copies(sems)
    mine, other = core[0], 1 - core[0]
    both = (hid_v, agg_v)
    loads = [go.start(delta, delta_v), go.start(hid, hid_v), go.start(agg, agg_v)]
    for load in loads:
        load.wait()
    delta_now = delta_v[...]

    def product(side, target):
        for n, source in enumerate(both):

            @pl.when(side == n)
            def _(source=source):
                target[...] = mm_tn(source[...], delta_now).astype(jnp.bfloat16)

    product(other, give_v)
    go.store(give_v, give_out)
    product(mine, keep_v)
    go.store(keep_v, keep_out)
    go.finish()


def place_kernel(layer, blocks, where, mine, other, *rest):
    self_out, neigh_out, mine_v, other_v, sems = rest[-5:]
    go = Copies(sems)
    loads = [go.start(mine, mine_v), go.start(other, other_v)]
    size = mine.shape[0] // blocks
    for load in loads:
        load.wait()

    def store(source, target, start, first):
        copies = []
        for j in range(blocks):
            to = pl.multiple_of((start ^ j) * size, size)
            copies.append(
                pltpu.make_async_copy(
                    source.at[pl.ds(j * size, size)],
                    target.at[layer, pl.ds(to, size)],
                    sems.at[first + j],
                )
            )
        for copy in copies:
            copy.start()
        for copy in copies:
            copy.wait()

    for core in range(2):

        @pl.when(where[0] == core)
        def _(core=core):
            outs = (self_out, neigh_out)
            store(mine_v, outs[core], where[1], 2)
            store(other_v, outs[1 - core], where[2], 2 + blocks)


def per_device(
    features, cotangent, self_weight, neigh_weight, block_val, block_col, send_idx, send_count
):
    outer = lax.axis_size("gx")
    inner = lax.axis_size("gy")
    devices = outer * inner
    nodes, width = features.shape
    tile = block_val.shape[2]
    layers = self_weight.shape[0]
    slots = send_idx.shape[2]
    halo = devices * slots
    own, far = nodes // tile, halo // tile
    scale = 1.0 / math.sqrt(nodes * devices)
    bf16, f32, i32 = jnp.bfloat16, jnp.float32, jnp.int32

    def call(body, args, outs, scratch, flops=0, alias=None, sems=0, loose=()):
        moved = sum(math.prod(o.shape) * o.dtype.itemsize for o in (*outs, *args))
        count = len(args) + len(outs) + sems
        return pl.pallas_call(
            body,
            in_specs=[
                SMEM if a.ndim == 1 or a is block_col else ANY if n in loose else HBM
                for n, a in enumerate(args)
            ],
            out_specs=[HBM for _ in outs],
            out_shape=[jax.ShapeDtypeStruct(o.shape, o.dtype) for o in outs],
            scratch_shapes=[*scratch, pltpu.SemaphoreType.DMA((count,))],
            input_output_aliases=alias or {},
            cost_estimate=pl.CostEstimate(
                flops=flops, bytes_accessed=moved, transcendentals=0
            ),
            compiler_params=pltpu.CompilerParams(vmem_limit_bytes=62 << 20),
        )(*args)

    rows = pltpu.VMEM((nodes, width), bf16)
    rows32 = pltpu.VMEM((nodes, width), f32)
    tiles = pltpu.VMEM((own, tile, width), bf16)
    halo_tiles = pltpu.VMEM((far, tile, width), bf16)
    halo_rows = pltpu.VMEM((halo, width), bf16)
    ext = pltpu.VMEM((own + far, tile, width), bf16)
    acc = pltpu.VMEM((own + far, tile, width), f32)
    blocks = pltpu.VMEM(block_val.shape, bf16)
    matrix = pltpu.VMEM((width, width), bf16)
    row_list = pltpu.VMEM((1, halo), i32)
    col_list = pltpu.VMEM((halo, 1), i32)
    big = 8 * nodes * width * width

    def exchange(array):
        sent = array.reshape(devices, slots, width)
        return lax.all_to_all(sent, AXES, 0, 0, tiled=True)

    position = lax.axis_index("gy")
    core = position & 1
    core_arg = core.reshape(1)

    bits = list(range(1, inner.bit_length() - 1))
    turn = bits[len(bits) // 2 :] + bits[: len(bits) // 2]
    gx_bits = list(range(outer.bit_length() - 1))
    pieces = 1 << len(bits)

    def flip(array, even, odd):
        perm = [(j, j ^ (1 << (odd if j & 1 else even))) for j in range(inner)]
        return lax.ppermute(array, "gy", perm)

    def bit_of(even, odd):
        return jnp.where(core == 0, (position >> even) & 1, (position >> odd) & 1)

    def reach(order):
        index = jnp.int32(0)
        for bit in order:
            index = index * 2 + ((position >> bit) & 1)
        return index

    mine_at = jnp.where(core == 0, reach(bits), reach(turn))
    other_at = jnp.where(core == 0, reach(turn), reach(bits))
    where = jnp.stack([core, mine_at, other_at]).astype(i32)

    def reduce_all(keep, give):
        parts = [[keep, 0], [flip(give, 0, 0), 0]]
        size = keep.shape[0]

        def rows_at(extra, count):
            total = None
            for array, at in parts:
                piece = lax.dynamic_slice(array, (at + extra, 0), (count, width)).astype(f32)
                total = piece if total is None else total + piece
            return total

        for even, odd in zip(bits, turn):
            size //= 2
            b = bit_of(even, odd)
            theirs = rows_at((1 - b) * size, size).astype(bf16)
            got = flip(theirs, even, odd)
            for part in parts:
                part[1] = part[1] + b * size
            parts.append([got, 0])
        total = rows_at(0, size)
        for bit in gx_bits:
            mine = total.astype(bf16)
            perm = [(j, j ^ (1 << bit)) for j in range(outer)]
            total = mine.astype(f32) + lax.ppermute(mine, "gx", perm).astype(f32)
        piece = (total * scale).astype(bf16)
        for even, odd in zip(bits[::-1], turn[::-1]):
            piece = jnp.concatenate([piece, flip(piece, even, odd)])
        return piece, flip(piece, 0, 0)

    row, col, send = call(
        first_kernel,
        (send_idx, send_count, features),
        (
            jax.ShapeDtypeStruct((1, halo), i32),
            jax.ShapeDtypeStruct((halo, 1), i32),
            jax.ShapeDtypeStruct((halo, width), bf16),
        ),
        (
            pltpu.VMEM(send_idx.shape, i32),
            pltpu.VMEM(send_count.shape, i32),
            rows, row_list, col_list, halo_rows,
        ),
    )
    hidden = features
    hiddens, aggregates, slopes = [features], [], []
    for layer in range(layers - 1):
        arrived = exchange(send)
        aggregate, slope, hidden, send = call(
            functools.partial(middle_kernel, layer),
            (
                block_col, hidden.reshape(own, tile, width), arrived.reshape(far, tile, width),
                block_val, self_weight, neigh_weight, col,
            ),
            (rows, rows32, rows, halo_rows),
            (ext, blocks, matrix, matrix, col_list, rows, rows32, rows, halo_rows),
            big,
            loose=(2,),
        )
        hiddens.append(hidden)
        aggregates.append(aggregate)
        slopes.append(slope)
    arrived = exchange(send)
    aggregate, delta, outgoing, base = call(
        functools.partial(last_kernel, layers - 1),
        (
            block_col, hidden.reshape(own, tile, width), arrived.reshape(far, tile, width),
            block_val, self_weight, neigh_weight, cotangent,
        ),
        (rows, rows, halo_tiles, rows32),
        (ext, blocks, matrix, matrix, rows, rows, rows, halo_tiles, rows32, acc),
        2 * big,
        loose=(2,),
    )
    aggregates.append(aggregate)
    outs = ()
    for layer in reversed(range(layers)):
        arrived = exchange(outgoing).reshape(halo, width)
        keep, give = call(
            weight_kernel,
            (core_arg, hiddens[layer], aggregates[layer], delta),
            (matrix, matrix),
            (rows, rows, rows, matrix, matrix),
            4 * nodes * width * width,
        )
        mine, other = reduce_all(keep, give)
        stacked = jax.ShapeDtypeStruct(self_weight.shape, bf16)
        outs = call(
            functools.partial(place_kernel, layer, pieces),
            (where, mine, other, *outs),
            (stacked, stacked),
            (matrix, matrix),
            alias={3: 0, 4: 1} if outs else None,
            sems=2 * pieces,
            loose=(1, 2),
        )
        if layer:
            delta, outgoing, base = call(
                functools.partial(backward_kernel, layer - 1),
                (
                    block_col, arrived, base, slopes[layer - 1], row,
                    block_val, self_weight, neigh_weight,
                ),
                (rows, halo_tiles, rows32),
                (
                    halo_rows, rows32, rows32, row_list, blocks, matrix, matrix,
                    rows, halo_tiles, rows32, acc,
                ),
                big,
                loose=(1,),
            )
    (grad,) = call(
        final_kernel, (arrived, base, row), (rows,), (halo_rows, rows32, row_list, rows), loose=(0,)
    )
    return (*outs, grad)


def solution(mesh):
    return jax.shard_map(
        per_device,
        mesh=mesh,
        in_specs=(
            P(AXES, None),
            P(AXES, None),
            P(),
            P(),
            P(AXES, None, None, None),
            P(AXES, None),
            P(AXES, None, None),
            P(AXES, None),
        ),
        out_specs=(P(), P(), P(AXES, None)),
        check_vma=False,
    )
```

time: 196 us -> 209 us (1.066)
  Pallas kernels: 16 us -> 45.6 us
  local copies, waits for them, and re-layouts: 29.7 us -> 3.81 us
  blocking collectives: 41.1 us -> 60.9 us
  other arithmetic: 13.8 us -> 4.94 us
  starting transfers between devices: 38.3 us -> 33.7 us
  waiting for transfers between devices: 54.3 us -> 57.9 us
    pallas_call x10 -> x13, Pallas kernels: 16 us -> 45.6 us  [call(): pl.pallas_call(body, in_specs=[SMEM if a.ndim == 1 or a is block_col else...]
    unnamed x83 -> x19, local copies, waits for them, and re-layouts: 28.1 us -> 3.81 us
    all_to_all x2 -> x3, blocking collectives: 41.1 us -> 60.9 us  [exchange(): return lax.all_to_all(sent, AXES, 0, 0, tiled=True)]
    all_to_all x4 -> x3, waiting for transfers between devices: 26.4 us -> 15.2 us  [exchange(): return lax.all_to_all(sent, AXES, 0, 0, tiled=True)]
    ppermute x6, waiting for transfers between devices: 11.4 us -> 19.8 us  [reduce_all(): total = mine.astype(f32) + lax.ppermute(mine, 'gx', perm).astype(f32)]
    ppermute x18, waiting for transfers between devices: 16.6 us -> 22.9 us  [flip(): return lax.ppermute(array, 'gy', perm)]
    add x6 -> x0, other arithmetic: 5.46 us -> none  [the longest x3 3.18 us: reduce_all(): total = keep + flip(give, 0, 0).astype(f32)]
    another operation x4 -> x1, other arithmetic: 4.46 us -> 0.56 us  [per_device(): where = jnp.stack([core, mine_at, other_at]).astype(i32)]
  transfers between devices with their start and end apart: 28 -> 27, of which waited for: 11 -> 14; matrix products, arithmetic and copies ran while one was open for 6% -> 2% of each run, Pallas kernels for 4% -> 13%
where the time goes in v2:
time: 209 us; the launch traced here: 208 us
  blocking collectives  60.9 us (29%)
  waiting for transfers between devices  57.9 us (28%)
  Pallas kernels  45.6 us (22%)
  starting transfers between devices  33.7 us (16%)
  other arithmetic  4.94 us (2%)
  local copies, waits for them, and re-layouts  3.81 us (2%)
    all_to_all x3, blocking collectives, exchange(): return lax.all_to_all(sent, AXES, 0, 0, tiled=True)  60.9 us
    pallas_call x13, Pallas kernels, call(): pl.pallas_call(body, in_specs=[SMEM if a.ndim == 1 or a is block_col else...  45.6 us
    ppermute x18, waiting for transfers between devices, flip(): return lax.ppermute(array, 'gy', perm)  22.9 us
    ppermute x6, waiting for transfers between devices, reduce_all(): total = mine.astype(f32) + lax.ppermute(mine, 'gx', perm).astype(f32)  19.8 us
    ppermute x18, starting transfers between devices, flip(): return lax.ppermute(array, 'gy', perm)  16 us
    all_to_all x3, waiting for transfers between devices, exchange(): return lax.all_to_all(sent, AXES, 0, 0, tiled=True)  15.2 us
    all_to_all x3, starting transfers between devices, exchange(): return lax.all_to_all(sent, AXES, 0, 0, tiled=True)  10.9 us
    ppermute x6, starting transfers between devices, reduce_all(): total = mine.astype(f32) + lax.ppermute(mine, 'gx', perm).astype(f32)  6.82 us
  transfers between devices with their start and end apart: 27, of which 14 were waited for; matrix products, arithmetic and copies ran while one was open for 2% of the time, Pallas kernels for 13%

profile of v2, /device:TPU:0, one launch (start us, length us, event | category | flops | bytes accessed | tf_op | source)
XLA Modules:
  0.0 208.1 jit_solution(13071914239733233777)
XLA Ops:
  4.2 23.1 %all_to_all.30 = bf16[32,16,512]{2,1,0:T(8,128)(2,1)} all-to-all(bf16[32,16,512]{2,1,0:T(8,128)(2,1)} %bitcast.29), channel_id=1, replica_groups=mesh['gx'=4,'gy'=8] {'gx','gy'}, dimensions={0} | all-to-all | bytes 1048576 | tf_op jit(solution)/shard_map/all_to_all | solution.py:337
  27.3 4.2 %shard_map.104 = (bf16[256,512]{1,0:T(8,128)(2,1)}, f32[256,512]{1,0:T(8,128)}, bf16[256,512]{1,0:T(8,128)(2,1)}, bf16[512,512]{1,0:T(8,128)(2,1)}) custom-call(s32[2,4]{1,0:T(2,128)} %cols.9, bf16[2,128,512]{2,1,0:T(8,128)(2,1)} %bitcast.24, bf16[4,128,512]{2,1,0:T(8,128)(2,1)} %bitcast.22, bf16[2,4,128,128]{3,2,1,0:T(8,128)(2,1)} %val.9, ...), custom_call_target="tpu_custom_call" | custom-call | flops 536870912 | bytes 5769248 | tf_op jit(solution)/shard_map/pallas_call | solution.py:306
  31.5 18.9 %all_to_all.31 = bf16[32,16,512]{2,1,0:T(8,128)(2,1)} all-to-all(bf16[32,16,512]{2,1,0:T(8,128)(2,1)} %bitcast.28), channel_id=1, replica_groups=mesh['gx'=4,'gy'=8] {'gx','gy'}, dimensions={0} | all-to-all | bytes 1048576 | tf_op jit(solution)/shard_map/all_to_all | solution.py:337
  50.5 4.2 %shard_map.105 = (bf16[256,512]{1,0:T(8,128)(2,1)}, f32[256,512]{1,0:T(8,128)}, bf16[256,512]{1,0:T(8,128)(2,1)}, bf16[512,512]{1,0:T(8,128)(2,1)}) custom-call(s32[2,4]{1,0:T(2,128)} %cols.9, bf16[2,128,512]{2,1,0:T(8,128)(2,1)} %bitcast.30, bf16[4,128,512]{2,1,0:T(8,128)(2,1)} %bitcast.21, bf16[2,4,128,128]{3,2,1,0:T(8,128)(2,1)} %val.9, ...), custom_call_target="tpu_custom_call" | custom-call | flops 536870912 | bytes 5769248 | tf_op jit(solution)/shard_map/pallas_call | solution.py:306
  54.7 18.9 %all_to_all.32 = bf16[32,16,512]{2,1,0:T(8,128)(2,1)} all-to-all(bf16[32,16,512]{2,1,0:T(8,128)(2,1)} %bitcast.27), channel_id=1, replica_groups=mesh['gx'=4,'gy'=8] {'gx','gy'}, dimensions={0} | all-to-all | bytes 1048576 | tf_op jit(solution)/shard_map/all_to_all | solution.py:337
  73.7 4.9 %shard_map.106 = (bf16[256,512]{1,0:T(8,128)(2,1)}, bf16[256,512]{1,0:T(8,128)(2,1)}, bf16[4,128,512]{2,1,0:T(8,128)(2,1)}, f32[256,512]{1,0:T(8,128)}) custom-call(s32[2,4]{1,0:T(2,128)} %cols.9, bf16[2,128,512]{2,1,0:T(8,128)(2,1)} %bitcast.31, bf16[4,128,512]{2,1,0:T(8,128)(2,1)} %bitcast.23, bf16[2,4,128,128]{3,2,1,0:T(8,128)(2,1)} %val.9, ...), custom_call_target="tpu_custom_call" | custom-call | flops 1073741824 | bytes 6029344 | tf_op jit(solution)/shard_map/pallas_call | solution.py:306
  78.6 2.9 %all-to-all-start.3 = ((bf16[32,16,512]{2,1,0:T(8,128)(2,1)}), bf16[32,16,512]{2,1,0:T(8,128)(2,1)S(1)}, u32[]{:S(2)}, u32[]{:S(2)}) async-start(bf16[32,16,512]{2,1,0:T(8,128)(2,1)} %bitcast.26), calls=%async_computation.3 | async-start | bytes 1048576 | tf_op jit(solution)/shard_map/all_to_all | solution.py:337
  81.5 2.6 %shard_map.111 = (bf16[512,512]{1,0:T(8,128)(2,1)}, bf16[512,512]{1,0:T(8,128)(2,1)}) custom-call(s32[1]{0:T(128)} %bitcast.core, bf16[256,512]{1,0:T(8,128)(2,1)} %get-tuple-element.41.hid, bf16[256,512]{1,0:T(8,128)(2,1)} %get-tuple-element.57.agg, bf16[256,512]{1,0:T(8,128)(2,1)} %get-tuple-element.58.delta), custom_call_target="tpu_custom_call" | custom-call | flops 268435456 | bytes 1835012 | tf_op jit(solution)/shard_map/pallas_call | solution.py:306
  84.5 12.7 %all-to-all-done.3 = bf16[32,16,512]{2,1,0:T(8,128)(2,1)S(1)} async-done(((bf16[32,16,512]{2,1,0:T(8,128)(2,1)}), bf16[32,16,512]{2,1,0:T(8,128)(2,1)S(1)}, u32[]{:S(2)}, u32[]{:S(2)}) %all-to-all-start.3) | async-done | bytes 524320 | tf_op jit(solution)/shard_map/all_to_all | solution.py:337
  97.9 4.5 %shard_map.107 = (bf16[256,512]{1,0:T(8,128)(2,1)}, bf16[4,128,512]{2,1,0:T(8,128)(2,1)}, f32[256,512]{1,0:T(8,128)}) custom-call(s32[2,4]{1,0:T(2,128)} %cols.9, bf16[512,512]{1,0:T(8,128)(2,1)} %bitcast.20, f32[256,512]{1,0:T(8,128)} %get-tuple-element.44.before, f32[256,512]{1,0:T(8,128)} %get-tuple-element.45.slope, s32[1,512]{1,0:T(1,128)} %get-tuple-element.46.row, ...), custom_call_target="tpu_custom_call" | custom-call | flops 536870912 | bytes 6293536 | tf_op jit(solution)/shard_map/pallas_call | solution.py:306
  102.5 3.0 %all-to-all-start.4 = ((bf16[32,16,512]{2,1,0:T(8,128)(2,1)}), bf16[32,16,512]{2,1,0:T(8,128)(2,1)S(1)}, u32[]{:S(2)}, u32[]{:S(2)}) async-start(bf16[32,16,512]{2,1,0:T(8,128)(2,1)} %bitcast.25), calls=%async_computation.4 | async-start | bytes 1048576 | tf_op jit(solution)/shard_map/all_to_all | solution.py:337
  107.4 7.9 %collective-permute-done.17 = bf16[256,512]{1,0:T(8,128)(2,1)S(1)} collective-permute-done((bf16[256,512]{1,0:T(8,128)(2,1)S(1)}, bf16[256,512]{1,0:T(8,128)(2,1)S(1)}, u32[]{:S(2)}, u32[]{:S(2)}) %collective-permute-start.17) | collective-permute-done | bytes 262176 | tf_op jit(solution)/shard_map/ppermute | solution.py:350
  121.9 4.4 %shard_map.108 = (bf16[256,512]{1,0:T(8,128)(2,1)}, bf16[4,128,512]{2,1,0:T(8,128)(2,1)}, f32[256,512]{1,0:T(8,128)}) custom-call(s32[2,4]{1,0:T(2,128)} %cols.9, bf16[512,512]{1,0:T(8,128)(2,1)} %bitcast.18, f32[256,512]{1,0:T(8,128)} %get-tuple-element.48.before, f32[256,512]{1,0:T(8,128)} %get-tuple-element.49.slope, s32[1,512]{1,0:T(1,128)} %get-tuple-element.46.row, ...), custom_call_target="tpu_custom_call" | custom-call | flops 536870912 | bytes 6293536 | tf_op jit(solution)/shard_map/pallas_call | solution.py:306
  126.3 2.9 %shard_map.109 = (bf16[512,512]{1,0:T(8,128)(2,1)}, bf16[512,512]{1,0:T(8,128)(2,1)}) custom-call(s32[1]{0:T(128)} %bitcast.core, bf16[256,512]{1,0:T(8,128)(2,1)} %hid.1, bf16[256,512]{1,0:T(8,128)(2,1)} %get-tuple-element.38.agg, bf16[256,512]{1,0:T(8,128)(2,1)} %get-tuple-element.50.delta), custom_call_target="tpu_custom_call" | custom-call | flops 268435456 | bytes 1835012 | tf_op jit(solution)/shard_map/pallas_call | solution.py:306
  130.7 4.7 %collective-permute-done.19 = bf16[128,512]{1,0:T(8,128)(2,1)S(1)} collective-permute-done((bf16[128,512]{1,0:T(8,128)(2,1)S(1)}, bf16[128,512]{1,0:T(8,128)(2,1)S(1)}, u32[]{:S(2)}, u32[]{:S(2)}) %collective-permute-start.19) | collective-permute-done | bytes 131104 | tf_op jit(solution)/shard_map/ppermute | solution.py:388
  140.6 3.5 %collective-permute-done.20 = bf16[128,512]{1,0:T(8,128)(2,1)S(1)} collective-permute-done((bf16[128,512]{1,0:T(8,128)(2,1)S(1)}, bf16[128,512]{1,0:T(8,128)(2,1)S(1)}, u32[]{:S(2)}, u32[]{:S(2)}) %collective-permute-start.20) | collective-permute-done | bytes 131104 | tf_op jit(solution)/shard_map/ppermute | solution.py:388
  158.8 3.3 %collective-permute-done.3 = bf16[128,512]{1,0:T(8,128)(2,1)S(1)} collective-permute-done((bf16[128,512]{1,0:T(8,128)(2,1)S(1)}, bf16[128,512]{1,0:T(8,128)(2,1)S(1)}, u32[]{:S(2)}, u32[]{:S(2)}) %collective-permute-start.3) | collective-permute-done | bytes 131104 | tf_op jit(solution)/shard_map/ppermute | solution.py:388
  162.5 7.0 %collective-permute-done.12 = bf16[128,512]{1,0:T(8,128)(2,1)S(1)} collective-permute-done((bf16[128,512]{1,0:T(8,128)(2,1)S(1)}, bf16[128,512]{1,0:T(8,128)(2,1)S(1)}, u32[]{:S(2)}, u32[]{:S(2)}) %collective-permute-start.12) | collective-permute-done | bytes 131104 | tf_op jit(solution)/shard_map/ppermute | solution.py:388
  172.3 3.7 %collective-permute-done.13 = bf16[128,512]{1,0:T(8,128)(2,1)S(1)} collective-permute-done((bf16[128,512]{1,0:T(8,128)(2,1)S(1)}, bf16[128,512]{1,0:T(8,128)(2,1)S(1)}, u32[]{:S(2)}, u32[]{:S(2)}) %collective-permute-start.13) | collective-permute-done | bytes 131104 | tf_op jit(solution)/shard_map/ppermute | solution.py:350
  177.0 5.1 %all-to-all-start.5 = ((bf16[32,16,512]{2,1,0:T(8,128)(2,1)}), bf16[32,16,512]{2,1,0:T(8,128)(2,1)S(1)}, u32[]{:S(2)}, u32[]{:S(2)}) async-start(bf16[32,16,512]{2,1,0:T(8,128)(2,1)} %bitcast.16), calls=%async_computation.5 | async-start | bytes 1048576 | tf_op jit(solution)/shard_map/all_to_all | solution.py:337
  184.7 7.2 %collective-permute-done.6 = bf16[256,512]{1,0:T(8,128)(2,1)S(1)} collective-permute-done((bf16[256,512]{1,0:T(8,128)(2,1)S(1)}, bf16[256,512]{1,0:T(8,128)(2,1)S(1)}, u32[]{:S(2)}, u32[]{:S(2)}) %collective-permute-start.6) | collective-permute-done | bytes 262176 | tf_op jit(solution)/shard_map/ppermute | solution.py:350
  192.7 3.5 %shard_map.112 = (bf16[3,512,512]{2,1,0:T(8,128)(2,1)}, bf16[3,512,512]{2,1,0:T(8,128)(2,1)}) custom-call(s32[3]{0:T(128)} %pad_add_fusion.where, bf16[512,512]{1,0:T(8,128)(2,1)} %copy-done.5, bf16[512,512]{1,0:T(8,128)(2,1)} %collective-permute-done.23.other), custom_call_target="tpu_custom_call" | custom-call | bytes 4194316 | tf_op jit(solution)/shard_map/pallas_call | solution.py:306
  200.8 3.6 %shard_map.113 = (bf16[3,512,512]{2,1,0:T(8,128)(2,1)}, bf16[3,512,512]{2,1,0:T(8,128)(2,1)}) custom-call(s32[3]{0:T(128)} %pad_add_fusion.where, bf16[512,512]{1,0:T(8,128)(2,1)} %copy-done.2, bf16[512,512]{1,0:T(8,128)(2,1)} %collective-permute-done.15.other, ...), custom_call_target="tpu_custom_call", output_to_operand_aliasing={{0}: (3, {}), {1}: (4, {})} | custom-call | bytes 7340044 | tf_op jit(solution)/shard_map/pallas_call | solution.py:306
  204.4 3.6 %shard_map.114 = (bf16[3,512,512]{2,1,0:T(8,128)(2,1)}, bf16[3,512,512]{2,1,0:T(8,128)(2,1)}) custom-call(s32[3]{0:T(128)} %pad_add_fusion.where, bf16[512,512]{1,0:T(8,128)(2,1)} %copy-done.3, bf16[512,512]{1,0:T(8,128)(2,1)} %collective-permute-done.7.other, ...), custom_call_target="tpu_custom_call", output_to_operand_aliasing={{0}: (3, {}), {1}: (4, {})} | custom-call | bytes 7340044 | tf_op jit(solution)/shard_map/pallas_call | solution.py:306
  (87 shorter events, 46.6 us)
Async XLA Ops:
  78.6 18.5 %all-to-all-start.3 = ((bf16[32,16,512]{2,1,0:T(8,128)(2,1)}), bf16[32,16,512]{2,1,0:T(8,128)(2,1)S(1)}, u32[]{:S(2)}, u32[]{:S(2)}) async-start(bf16[32,16,512]{2,1,0:T(8,128)(2,1)} %bitcast.26), calls=%async_computation.3 | async-start | bytes 1048576 | tf_op jit(solution)/shard_map/all_to_all | solution.py:337
  84.1 21.3 %collective-permute-start.16 = (bf16[512,512]{1,0:T(8,128)(2,1)}, bf16[512,512]{1,0:T(8,128)(2,1)S(1)}, u32[]{:S(2)}, u32[]{:S(2)}) collective-permute-start(bf16[512,512]{1,0:T(8,128)(2,1)} %get-tuple-element.60), channel_id=1, source_target_pairs={{0,1},{1,0},{2,3},{3,2},{4,5},{5,4},{6,7},{7,6},{8,9},{9,8},{10,11... | collective-permute-start | bytes 1572872 | tf_op jit(solution)/shard_map/ppermute | solution.py:350
  102.5 18.6 %all-to-all-start.4 = ((bf16[32,16,512]{2,1,0:T(8,128)(2,1)}), bf16[32,16,512]{2,1,0:T(8,128)(2,1)S(1)}, u32[]{:S(2)}, u32[]{:S(2)}) async-start(bf16[32,16,512]{2,1,0:T(8,128)(2,1)} %bitcast.25), calls=%async_computation.4 | async-start | bytes 1048576 | tf_op jit(solution)/shard_map/all_to_all | solution.py:337
  105.6 9.7 %collective-permute-start.17 = (bf16[256,512]{1,0:T(8,128)(2,1)S(1)}, bf16[256,512]{1,0:T(8,128)(2,1)S(1)}, u32[]{:S(2)}, u32[]{:S(2)}) collective-permute-start(bf16[256,512]{1,0:T(8,128)(2,1)S(1)} %add_convert_fusion), channel_id=1, source_target_pairs={{0,2},{1,5},{2,0},{3,7},{4,6},{5,1},{6,4},{7,3},{8,10},{9,13},{10,... | collective-permute-start | bytes 786440 | tf_op jit(solution)/shard_map/ppermute | solution.py:350
  116.0 13.3 %collective-permute-start.18 = (bf16[128,512]{1,0:T(8,128)(2,1)}, bf16[128,512]{1,0:T(8,128)(2,1)S(1)}, u32[]{:S(2)}, u32[]{:S(2)}) collective-permute-start(bf16[128,512]{1,0:T(8,128)(2,1)} %add_convert_fusion.5), channel_id=1, source_target_pairs={{0,4},{1,3},{2,6},{3,1},{4,0},{5,7},{6,2},{7,5},{8,12},{9,11},{10,... | collective-permute-start | bytes 393224 | tf_op jit(solution)/shard_map/ppermute | solution.py:350
  120.0 17.4 %collective-permute-start.8 = (bf16[512,512]{1,0:T(8,128)(2,1)}, bf16[512,512]{1,0:T(8,128)(2,1)}, u32[]{:S(2)}, u32[]{:S(2)}) collective-permute-start(bf16[512,512]{1,0:T(8,128)(2,1)} %get-tuple-element.56), channel_id=1, source_target_pairs={{0,1},{1,0},{2,3},{3,2},{4,5},{5,4},{6,7},{7,6},{8,9},{9,8},{10,11... | collective-permute-start | bytes 1572872 | tf_op jit(solution)/shard_map/ppermute | solution.py:350
  129.2 9.7 %collective-permute-start = (bf16[512,512]{1,0:T(8,128)(2,1)}, bf16[512,512]{1,0:T(8,128)(2,1)S(1)}, u32[]{:S(2)}, u32[]{:S(2)}) collective-permute-start(bf16[512,512]{1,0:T(8,128)(2,1)} %get-tuple-element.52), channel_id=1, source_target_pairs={{0,1},{1,0},{2,3},{3,2},{4,5},{5,4},{6,7},{7,6},{8,9},{9,8},{10,11... | collective-permute-start | bytes 1572872 | tf_op jit(solution)/shard_map/ppermute | solution.py:350
  129.4 5.9 %collective-permute-start.19 = (bf16[128,512]{1,0:T(8,128)(2,1)S(1)}, bf16[128,512]{1,0:T(8,128)(2,1)S(1)}, u32[]{:S(2)}, u32[]{:S(2)}) collective-permute-start(bf16[128,512]{1,0:T(8,128)(2,1)S(1)} %add_convert_fusion.4), channel_id=1, source_target_pairs={{0,8},{8,0},{16,24},{24,16},{1,9},{9,1},{17,25},{25,17},{2,10},{10... | collective-permute-start | bytes 393224 | tf_op jit(solution)/shard_map/ppermute | solution.py:388
  135.4 8.8 %collective-permute-start.20 = (bf16[128,512]{1,0:T(8,128)(2,1)S(1)}, bf16[128,512]{1,0:T(8,128)(2,1)S(1)}, u32[]{:S(2)}, u32[]{:S(2)}) collective-permute-start(bf16[128,512]{1,0:T(8,128)(2,1)S(1)} %add_convert_fusion.3), channel_id=1, source_target_pairs={{0,16},{8,24},{16,0},{24,8},{1,17},{9,25},{17,1},{25,9},{2,18},{10... | collective-permute-start | bytes 393224 | tf_op jit(solution)/shard_map/ppermute | solution.py:388
  138.4 7.0 %collective-permute-start.9 = (bf16[256,512]{1,0:T(8,128)(2,1)S(1)}, bf16[256,512]{1,0:T(8,128)(2,1)S(1)}, u32[]{:S(2)}, u32[]{:S(2)}) collective-permute-start(bf16[256,512]{1,0:T(8,128)(2,1)S(1)} %add_convert_fusion.1), channel_id=1, source_target_pairs={{0,2},{1,5},{2,0},{3,7},{4,6},{5,1},{6,4},{7,3},{8,10},{9,13},{10,... | collective-permute-start | bytes 786440 | tf_op jit(solution)/shard_map/ppermute | solution.py:350
  138.9 10.8 %collective-permute-start.1 = (bf16[256,512]{1,0:T(8,128)(2,1)S(1)}, bf16[256,512]{1,0:T(8,128)(2,1)S(1)}, u32[]{:S(2)}, u32[]{:S(2)}) collective-permute-start(bf16[256,512]{1,0:T(8,128)(2,1)S(1)} %add_convert_fusion.2), channel_id=1, source_target_pairs={{0,2},{1,5},{2,0},{3,7},{4,6},{5,1},{6,4},{7,3},{8,10},{9,13},{10,... | collective-permute-start | bytes 786440 | tf_op jit(solution)/shard_map/ppermute | solution.py:350
  149.3 34.7 %collective-permute-start.22 = (bf16[256,512]{1,0:T(8,128)(2,1)S(1)}, bf16[256,512]{1,0:T(8,128)(2,1)S(1)}, u32[]{:S(2)}, u32[]{:S(2)}) collective-permute-start(bf16[256,512]{1,0:T(8,128)(2,1)S(1)} %pad_maximum_fusion.5), channel_id=1, source_target_pairs={{0,2},{1,5},{2,0},{3,7},{4,6},{5,1},{6,4},{7,3},{8,10},{9,13},{10,... | collective-permute-start | bytes 786440 | tf_op jit(solution)/shard_map/ppermute | solution.py:350
  149.8 6.2 %collective-permute-start.2 = (bf16[128,512]{1,0:T(8,128)(2,1)S(1)}, bf16[128,512]{1,0:T(8,128)(2,1)S(1)}, u32[]{:S(2)}, u32[]{:S(2)}) collective-permute-start(bf16[128,512]{1,0:T(8,128)(2,1)S(1)} %add_convert_fusion.11), channel_id=1, source_target_pairs={{0,4},{1,3},{2,6},{3,1},{4,0},{5,7},{6,2},{7,5},{8,12},{9,11},{10,... | collective-permute-start | bytes 393224 | tf_op jit(solution)/shard_map/ppermute | solution.py:350
  156.1 6.0 %collective-permute-start.3 = (bf16[128,512]{1,0:T(8,128)(2,1)S(1)}, bf16[128,512]{1,0:T(8,128)(2,1)S(1)}, u32[]{:S(2)}, u32[]{:S(2)}) collective-permute-start(bf16[128,512]{1,0:T(8,128)(2,1)S(1)} %add_convert_fusion.10), channel_id=1, source_target_pairs={{0,8},{8,0},{16,24},{24,16},{1,9},{9,1},{17,25},{25,17},{2,10},{10... | collective-permute-start | bytes 393224 | tf_op jit(solution)/shard_map/ppermute | solution.py:388
  158.1 11.3 %collective-permute-start.12 = (bf16[128,512]{1,0:T(8,128)(2,1)S(1)}, bf16[128,512]{1,0:T(8,128)(2,1)S(1)}, u32[]{:S(2)}, u32[]{:S(2)}) collective-permute-start(bf16[128,512]{1,0:T(8,128)(2,1)S(1)} %add_convert_fusion.6), channel_id=1, source_target_pairs={{0,16},{8,24},{16,0},{24,8},{1,17},{9,25},{17,1},{25,9},{2,18},{10... | collective-permute-start | bytes 393224 | tf_op jit(solution)/shard_map/ppermute | solution.py:388
  162.2 8.7 %collective-permute-start.4 = (bf16[128,512]{1,0:T(8,128)(2,1)S(1)}, bf16[128,512]{1,0:T(8,128)(2,1)S(1)}, u32[]{:S(2)}, u32[]{:S(2)}) collective-permute-start(bf16[128,512]{1,0:T(8,128)(2,1)S(1)} %add_convert_fusion.9), channel_id=1, source_target_pairs={{0,16},{8,24},{16,0},{24,8},{1,17},{9,25},{17,1},{25,9},{2,18},{10... | collective-permute-start | bytes 393224 | tf_op jit(solution)/shard_map/ppermute | solution.py:388
  169.5 6.4 %collective-permute-start.13 = (bf16[128,512]{1,0:T(8,128)(2,1)S(1)}, bf16[128,512]{1,0:T(8,128)(2,1)S(1)}, u32[]{:S(2)}, u32[]{:S(2)}) collective-permute-start(bf16[128,512]{1,0:T(8,128)(2,1)S(1)} %multiply_convert_fusion.1), channel_id=1, source_target_pairs={{0,4},{1,3},{2,6},{3,1},{4,0},{5,7},{6,2},{7,5},{8,12},{9,11},{10,... | collective-permute-start | bytes 393224 | tf_op jit(solution)/shard_map/ppermute | solution.py:350
  170.9 11.2 %collective-permute-start.5 = (bf16[128,512]{1,0:T(8,128)(2,1)S(1)}, bf16[128,512]{1,0:T(8,128)(2,1)S(1)}, u32[]{:S(2)}, u32[]{:S(2)}) collective-permute-start(bf16[128,512]{1,0:T(8,128)(2,1)S(1)} %multiply_convert_fusion.2), channel_id=1, source_target_pairs={{0,4},{1,3},{2,6},{3,1},{4,0},{5,7},{6,2},{7,5},{8,12},{9,11},{10,... | collective-permute-start | bytes 393224 | tf_op jit(solution)/shard_map/ppermute | solution.py:350
  176.0 8.1 %collective-permute-start.14 = (bf16[256,512]{1,0:T(8,128)(2,1)S(1)}, bf16[256,512]{1,0:T(8,128)(2,1)S(1)}, u32[]{:S(2)}, u32[]{:S(2)}) collective-permute-start(bf16[256,512]{1,0:T(8,128)(2,1)S(1)} %pad_maximum_fusion.4), channel_id=1, source_target_pairs={{0,2},{1,5},{2,0},{3,7},{4,6},{5,1},{6,4},{7,3},{8,10},{9,13},{10,... | collective-permute-start | bytes 786440 | tf_op jit(solution)/shard_map/ppermute | solution.py:350
  177.0 20.7 %all-to-all-start.5 = ((bf16[32,16,512]{2,1,0:T(8,128)(2,1)}), bf16[32,16,512]{2,1,0:T(8,128)(2,1)S(1)}, u32[]{:S(2)}, u32[]{:S(2)}) async-start(bf16[32,16,512]{2,1,0:T(8,128)(2,1)} %bitcast.16), calls=%async_computation.5 | async-start | bytes 1048576 | tf_op jit(solution)/shard_map/all_to_all | solution.py:337
  182.2 9.8 %collective-permute-start.6 = (bf16[256,512]{1,0:T(8,128)(2,1)S(1)}, bf16[256,512]{1,0:T(8,128)(2,1)S(1)}, u32[]{:S(2)}, u32[]{:S(2)}) collective-permute-start(bf16[256,512]{1,0:T(8,128)(2,1)S(1)} %pad_maximum_fusion.3), channel_id=1, source_target_pairs={{0,2},{1,5},{2,0},{3,7},{4,6},{5,1},{6,4},{7,3},{8,10},{9,13},{10,... | collective-permute-start | bytes 786440 | tf_op jit(solution)/shard_map/ppermute | solution.py:350
  184.0 8.6 %collective-permute-start.23 = (bf16[512,512]{1,0:T(8,128)(2,1)S(1)}, bf16[512,512]{1,0:T(8,128)(2,1)}, u32[]{:S(2)}, u32[]{:S(2)}) collective-permute-start(bf16[512,512]{1,0:T(8,128)(2,1)S(1)} %pad_maximum_fusion.2.mine), channel_id=1, source_target_pairs={{0,1},{1,0},{2,3},{3,2},{4,5},{5,4},{6,7},{7,6},{8,9},{9,8},{10,11... | collective-permute-start | bytes 1572872 | tf_op jit(solution)/shard_map/ppermute | solution.py:350
  184.2 16.6 %collective-permute-start.15 = (bf16[512,512]{1,0:T(8,128)(2,1)S(1)}, bf16[512,512]{1,0:T(8,128)(2,1)}, u32[]{:S(2)}, u32[]{:S(2)}) collective-permute-start(bf16[512,512]{1,0:T(8,128)(2,1)S(1)} %pad_maximum_fusion.1.mine), channel_id=1, source_target_pairs={{0,1},{1,0},{2,3},{3,2},{4,5},{5,4},{6,7},{7,6},{8,9},{9,8},{10,11... | collective-permute-start | bytes 1572872 | tf_op jit(solution)/shard_map/ppermute | solution.py:350
  192.0 12.4 %collective-permute-start.7 = (bf16[512,512]{1,0:T(8,128)(2,1)S(1)}, bf16[512,512]{1,0:T(8,128)(2,1)}, u32[]{:S(2)}, u32[]{:S(2)}) collective-permute-start(bf16[512,512]{1,0:T(8,128)(2,1)S(1)} %pad_maximum_fusion.mine), channel_id=1, source_target_pairs={{0,1},{1,0},{2,3},{3,2},{4,5},{5,4},{6,7},{7,6},{8,9},{9,8},{10,11... | collective-permute-start | bytes 1572872 | tf_op jit(solution)/shard_map/ppermute | solution.py:350
  (12 other events, 83.4 us)

commit v3 on v0

v3 whole, which is shorter than its diff:
```python
import functools
import math

import jax
import jax.numpy as jnp
from jax import lax
from jax.experimental import pallas as pl
from jax.experimental.pallas import tpu as pltpu
from jax.sharding import PartitionSpec as P


AXES = ("gx", "gy")


def mm(a, b):
    return jnp.dot(a, b, preferred_element_type=jnp.float32)


def mm_tn(a, b):
    return lax.dot_general(a, b, (((0,), (0,)), ((), ())), preferred_element_type=jnp.float32)


def mm_nt(a, b):
    return lax.dot_general(a, b, (((1,), (1,)), ((), ())), preferred_element_type=jnp.float32)


def iota(shape, dim):
    return lax.broadcasted_iota(jnp.int32, shape, dim)


def ones_where(mask):
    return jnp.where(mask, 1.0, 0.0).astype(jnp.bfloat16)


def pick_rows(col, table):
    hot = ones_where(iota((col.shape[0], table.shape[0]), 1) == col)
    return mm(hot, table).astype(jnp.bfloat16)


def return_rows(row, arrived, nodes):
    hot = ones_where(iota((nodes, row.shape[1]), 0) == row)
    return mm(hot, arrived)


class Copies:
    def __init__(self, sems):
        self.sems, self.used, self.stores = sems, 0, []

    def start(self, source, target):
        copy = pltpu.make_async_copy(source, target, self.sems.at[self.used])
        self.used += 1
        copy.start()
        return copy

    def store(self, source, target):
        self.stores.append(self.start(source, target))

    def finish(self):
        for copy in self.stores:
            copy.wait()


def first_kernel(idx, cnt, table, row_out, col_out, send_out, idx_v, cnt_v, table_v, send_v, sems):
    go = Copies(sems)
    loads = [go.start(idx, idx_v), go.start(cnt, cnt_v), go.start(table, table_v)]
    _, slots, peers = idx.shape
    total = peers * slots
    start_t = iota((total, peers), 1) * slots
    place_t = iota((total, peers), 0)
    inside_t = ones_where((place_t >= start_t) & (place_t < start_t + slots))
    here_t = (iota((total, slots), 0) & (slots - 1)) == iota((total, slots), 1)
    loads[0].wait()
    loads[1].wait()
    live = iota((slots, peers), 0) < jnp.broadcast_to(cnt_v[...], (slots, peers))
    code = jnp.where(live, idx_v[0] + 1, 0).astype(jnp.float32).astype(jnp.bfloat16)
    col = jnp.sum(jnp.where(here_t, mm_nt(inside_t, code), 0.0), axis=1, keepdims=True) - 1.0
    col = col.astype(jnp.int32)
    col_out[...] = col
    loads[2].wait()
    send_v[...] = pick_rows(col, table_v[...])
    go.store(send_v, send_out)
    start = iota((peers, total), 0) * slots
    place = iota((peers, total), 1)
    inside = ones_where((place >= start) & (place < start + slots))
    here = (iota((slots, total), 1) & (slots - 1)) == iota((slots, total), 0)
    row = jnp.sum(jnp.where(here, mm(code, inside), 0.0), axis=0, keepdims=True) - 1.0
    row_out[...] = row.astype(jnp.int32)
    go.finish()


def load_kernel(layer, *refs):
    count = (len(refs) - 1) // 2
    go = Copies(refs[-1])
    for n, (source, target) in enumerate(zip(refs[:count], refs[count:-1])):
        go.store(source.at[layer] if n < 2 else source, target)
    go.finish()


def pre_activation(cols, hid, arr, val, ws, wn, agg_v, ext_v):
    tiles, blocks, tile, _ = val.shape
    own = hid.shape[0] // tile
    for t in range(own):
        ext_v[t] = hid[t * tile : (t + 1) * tile, :]
    for t in range(arr.shape[0] // tile):
        ext_v[own + t] = arr[t * tile : (t + 1) * tile, :]
    for r in range(tiles):
        total = mm(val[r, 0], ext_v[cols[r, 0]])
        for b in range(1, blocks):
            total += mm(val[r, b], ext_v[cols[r, b]])
        agg_v[r * tile : (r + 1) * tile, :] = total.astype(jnp.bfloat16)
    return mm(hid[...], ws[...]) + mm(agg_v[...], wn[...])


def middle_kernel(
    cols, hid, arr, val, ws, wn, col, agg_out, slope_out, next_out, next_near, send_out,
    ext_v, agg_v, slope_v, send_v, sems,
):
    go = Copies(sems)
    pre = pre_activation(cols, hid, arr, val, ws, wn, agg_v, ext_v)
    go.store(agg_v, agg_out)
    sigma = jax.nn.sigmoid(pre)
    hidden = (pre * sigma).astype(jnp.bfloat16)
    next_near[...] = hidden
    go.store(next_near, next_out)
    slope_v[...] = sigma * (1.0 + pre * (1.0 - sigma))
    go.store(slope_v, slope_out)
    send_v[...] = pick_rows(col[...], hidden)
    go.store(send_v, send_out)
    go.finish()


def spread_back(go, delta, cols, val, ws, wn, halo_out, base_out, halo_v, base_v, acc_v):
    tiles, blocks, tile, _ = val.shape
    own = base_out.shape[0] // tile
    acc_v[...] = jnp.zeros_like(acc_v)
    upstream = mm_nt(delta, wn[...]).astype(jnp.bfloat16)
    for r in range(tiles):
        part = upstream[r * tile : (r + 1) * tile, :]
        for b in range(blocks):
            acc_v[cols[r, b]] += mm_tn(val[r, b], part)
    for t in range(halo_out.shape[0] // tile):
        halo_v[t * tile : (t + 1) * tile, :] = acc_v[own + t].astype(jnp.bfloat16)
    go.store(halo_v, halo_out)
    own_part = mm_nt(delta, ws[...])
    for t in range(own):
        at = slice(t * tile, (t + 1) * tile)
        base_v[at, :] = own_part[at, :] + acc_v[t]
    go.store(base_v, base_out)


def last_kernel(
    cols, hid, arr, val, ws, wn, cot, agg_out, delta_out, halo_out, base_out,
    ext_v, agg_v, delta_v, halo_v, base_v, acc_v, sems,
):
    go = Copies(sems)
    pre = pre_activation(cols, hid, arr, val, ws, wn, agg_v, ext_v)
    go.store(agg_v, agg_out)
    sigma = jax.nn.sigmoid(pre)
    slope = sigma * (1.0 + pre * (1.0 - sigma))
    delta = (cot[...].astype(jnp.float32) * slope).astype(jnp.bfloat16)
    delta_v[...] = delta
    go.store(delta_v, delta_out)
    spread_back(go, delta, cols, val, ws, wn, halo_out, base_out, halo_v, base_v, acc_v)
    go.finish()


def delta_of(loads, arr, row, before_v, slope_v):
    back = return_rows(row[...], arr[...], before_v.shape[0])
    for load in loads:
        load.wait()
    grad = (before_v[...] + back).astype(jnp.bfloat16)
    return (grad.astype(jnp.float32) * slope_v[...]).astype(jnp.bfloat16)


def backward_kernel(
    cols, arr, before, slope, row, val, ws, wn, delta_out, halo_out, base_out,
    before_v, slope_v, delta_v, halo_v, base_v, acc_v, sems,
):
    go = Copies(sems)
    loads = [go.start(before, before_v), go.start(slope, slope_v)]
    delta = delta_of(loads, arr, row, before_v, slope_v)
    delta_v[...] = delta
    go.store(delta_v, delta_out)
    spread_back(go, delta, cols, val, ws, wn, halo_out, base_out, halo_v, base_v, acc_v)
    go.finish()


def spread_kernel(cols, delta, val, ws, wn, halo_out, base_out, halo_v, base_v, acc_v, sems):
    go = Copies(sems)
    spread_back(go, delta[...], cols, val, ws, wn, halo_out, base_out, halo_v, base_v, acc_v)
    go.finish()


def final_kernel(arr, before, row, grad_out, before_v, grad_v, sems):
    go = Copies(sems)
    load = go.start(before, before_v)
    back = return_rows(row[...], arr[...], before.shape[0])
    load.wait()
    grad_v[...] = (before_v[...] + back).astype(jnp.bfloat16)
    go.store(grad_v, grad_out)
    go.finish()


def products(core, hid_v, agg_v, delta, pairs):
    for side, target in ((1 - core, pairs[0]), (core, pairs[1])):
        for n, source in enumerate((hid_v, agg_v)):

            @pl.when(side == n)
            def _(source=source, target=target):
                target[...] = mm_tn(source[...], delta).astype(jnp.bfloat16)


def weight_kernel(core, hid, agg, delta, keep_out, give, hid_v, agg_v, delta_v, keep_v, sems):
    go = Copies(sems)
    loads = [go.start(delta, delta_v), go.start(hid, hid_v), go.start(agg, agg_v)]
    for load in loads:
        load.wait()
    products(core[0], hid_v, agg_v, delta_v[...], (give, keep_v))
    go.store(keep_v, keep_out)
    go.finish()


def top_kernel(
    core, hid, agg, arr, before, slope, row, delta_near, keep_out, give,
    before_v, slope_v, hid_v, agg_v, keep_v, sems,
):
    go = Copies(sems)
    loads = [go.start(before, before_v), go.start(slope, slope_v)]
    late = [go.start(hid, hid_v), go.start(agg, agg_v)]
    delta = delta_of(loads, arr, row, before_v, slope_v)
    delta_near[...] = delta
    for load in late:
        load.wait()
    products(core[0], hid_v, agg_v, delta, (give, keep_v))
    go.store(keep_v, keep_out)
    go.finish()


def quarters_kernel(chip, keep, got, *rest):
    count = len(rest) - 4
    outs, (keep_v, got_v, out_v, sems) = rest[:count], rest[count:]
    go = Copies(sems)
    size = keep.shape[0] // count
    loads = []
    for m in range(count):
        at = pl.multiple_of((chip[0] ^ m) * size, size)
        here = pl.ds(m * size, size)
        loads.append(go.start(keep.at[pl.ds(at, size)], keep_v.at[here]))
        loads.append(go.start(got.at[pl.ds(at, size)], got_v.at[here]))
    for m in range(count):
        loads[2 * m].wait()
        loads[2 * m + 1].wait()
        here = pl.ds(m * size, size)
        total = keep_v[here, :].astype(jnp.float32) + got_v[here, :].astype(jnp.float32)
        out_v[here, :] = total.astype(jnp.bfloat16)
        go.store(out_v.at[here], outs[m])
    go.finish()


def place_kernel(layers, count, where, *refs):
    mine, other = refs[:count], refs[count : 2 * count]
    self_out, neigh_out, sems = refs[-3:]
    size = mine[0].shape[0] // len(layers)
    for core, outs in enumerate(((self_out, neigh_out), (neigh_out, self_out))):

        @pl.when(where[0] == core)
        def _(outs=outs):
            copies = []
            for m, source in enumerate((*mine, *other)):
                to = pl.multiple_of((where[1] ^ (m % count)) * size, size)
                for n, layer in enumerate(layers):
                    copies.append(
                        pltpu.make_async_copy(
                            source.at[pl.ds(n * size, size)],
                            outs[m // count].at[layer, pl.ds(to, size)],
                            sems.at[len(copies)],
                        )
                    )
            for copy in copies:
                copy.start()
            for copy in copies:
                copy.wait()


def per_device(
    features, cotangent, self_weight, neigh_weight, block_val, block_col, send_idx, send_count
):
    outer = lax.axis_size("gx")
    inner = lax.axis_size("gy")
    devices = outer * inner
    nodes, width = features.shape
    tile = block_val.shape[2]
    layers = self_weight.shape[0]
    slots = send_idx.shape[2]
    halo = devices * slots
    ext_tiles = (nodes + halo) // tile
    scale = 1.0 / math.sqrt(nodes * devices)
    bf16, f32, i32 = jnp.bfloat16, jnp.float32, jnp.int32
    near, away, scalars = pltpu.VMEM, pltpu.HBM, pltpu.SMEM

    def call(body, args, outs, scratch=(), sems=None, flops=0, alias=None):
        moved = sum(math.prod(o[0]) * jnp.dtype(o[1]).itemsize for o in outs)
        operands = [
            a if space is scalars else pltpu.with_memory_space_constraint(a, space)
            for a, space in args
        ]
        sems = len(args) + len(outs) if sems is None else sems
        return pl.pallas_call(
            body,
            in_specs=[pl.BlockSpec(memory_space=space) for _, space in args],
            out_specs=[pl.BlockSpec(memory_space=o[2]) for o in outs],
            out_shape=[o[2](o[0], o[1]) for o in outs],
            scratch_shapes=[*(pltpu.VMEM(*s) for s in scratch), pltpu.SemaphoreType.DMA((sems,))],
            input_output_aliases=alias or {},
            cost_estimate=pl.CostEstimate(
                flops=flops, bytes_accessed=2 * moved, transcendentals=0
            ),
            compiler_params=pltpu.CompilerParams(vmem_limit_bytes=16 << 20),
        )(*operands)

    rows, rows32 = ((nodes, width), bf16), ((nodes, width), f32)
    square, halo_rows = ((width, width), bf16), ((halo, width), bf16)
    ext, acc = ((ext_tiles, tile, width), bf16), ((ext_tiles, tile, width), f32)
    big = 8 * nodes * width * width

    def exchange(array):
        sent = array.reshape(devices, slots, width)
        return lax.all_to_all(sent, AXES, 0, 0, tiled=True).reshape(halo, width)

    position = lax.axis_index("gy")
    core, chip = position & 1, position >> 1
    core_arg = core.reshape(1)
    chips = inner // 2
    gx_bits = list(range(outer.bit_length() - 1))

    def flip(array, mask):
        return lax.ppermute(array, "gy", [(j, j ^ mask) for j in range(inner)])

    def chip_sum(keep, give):
        got = flip(give, 1)
        mine, *others = call(
            quarters_kernel,
            ((chip.reshape(1), scalars), (keep, away), (got, near)),
            (((width // chips, width), bf16, near),) * chips,
            (square, square, square),
            3 * chips,
        )
        total = mine.astype(f32)
        for m, other in enumerate(others, 1):
            arrival = flip(other, 2 * m)
            total = total + arrival.astype(f32)
        for bit in gx_bits:
            mine = total.astype(bf16)
            perm = [(j, j ^ (1 << bit)) for j in range(outer)]
            total = mine.astype(f32) + lax.ppermute(mine, "gx", perm).astype(f32)
        return (total * scale).astype(bf16)

    def gather(piece):
        mine, other = [piece], []
        for m in range(1, chips):
            mine.append(flip(piece, 2 * m))
        for m in range(chips):
            other.append(flip(mine[m], 1))
        return mine, other

    where = jnp.stack([core, chip]).astype(i32)

    def place(group, mine, other, outs):
        return call(
            functools.partial(place_kernel, group, chips),
            ((where, scalars), *((a, near) for a in (*mine, *other)), *((o, away) for o in outs)),
            ((self_weight.shape, bf16, away),) * 2,
            (),
            2 * chips * len(group),
            alias={1 + 2 * chips: 0, 2 + 2 * chips: 1} if outs else None,
        )

    def load(layer, *others):
        arrays = (self_weight, neigh_weight, *others)
        return call(
            functools.partial(load_kernel, layer),
            [(a, away) for a in arrays],
            [(a.shape[1:] if n < 2 else a.shape, a.dtype, near) for n, a in enumerate(arrays)],
        )

    cols = (block_col, scalars)
    row, col, send = call(
        first_kernel,
        ((send_idx.transpose(0, 2, 1), away), (send_count, away), (features, away)),
        (((1, halo), i32, near), ((halo, 1), i32, near), (*halo_rows, away)),
        (
            ((1, slots, devices), i32), ((1, devices), i32), rows, halo_rows,
        ),
    )
    arrived = exchange(send)
    ws, wn, hidden, val = load(0, features, block_val)
    hiddens, aggregates, slopes = [features], [], []
    for layer in range(layers - 1):
        aggregate, slope, kept, hidden, send = call(
            middle_kernel,
            (
                cols, (hidden, near), (arrived, near), (val, near), (ws, near), (wn, near),
                (col, near),
            ),
            ((*rows, away), (*rows32, away), (*rows, away), (*rows, near), (*halo_rows, away)),
            (ext, rows, rows32, halo_rows),
            flops=big,
        )
        hiddens.append(kept)
        aggregates.append(aggregate)
        slopes.append(slope)
        arrived = exchange(send)
        last = layer + 2 == layers
        ws, wn, *cot = load(layer + 1, *((cotangent,) if last else ()))
    aggregate, delta, outgoing, base = call(
        last_kernel,
        (
            cols, (hidden, near), (arrived, near), (val, near), (ws, near), (wn, near),
            (cot[0], near),
        ),
        ((*rows, away), (*rows, away), (*halo_rows, away), (*rows32, away)),
        (ext, rows, rows, halo_rows, rows32, acc),
        flops=2 * big,
    )
    aggregates.append(aggregate)
    sums = []
    for layer in reversed(range(layers)):
        below = layer - 1
        if layer:
            keep, give = call(
                weight_kernel,
                (
                    (core_arg, scalars), (hiddens[layer], away), (aggregates[layer], away),
                    (delta, away),
                ),
                ((*square, away), (*square, near)),
                (rows, rows, rows, square),
                flops=big // 2,
            )
        sums.append(chip_sum(keep, give))
        arrived = exchange(outgoing)
        if layer:
            ws, wn = load(below)
        if below > 0:
            delta, outgoing, base = call(
                backward_kernel,
                (
                    cols, (arrived, near), (base, away), (slopes[below], away), (row, near),
                    (val, near), (ws, near), (wn, near),
                ),
                ((*rows, away), (*halo_rows, away), (*rows32, away)),
                (rows32, rows32, rows, halo_rows, rows32, acc),
                flops=big,
            )
        elif below == 0:
            delta, keep, give = call(
                top_kernel,
                (
                    (core_arg, scalars), (hiddens[0], away), (aggregates[0], away),
                    (arrived, near), (base, away), (slopes[0], away), (row, near),
                ),
                ((*rows, near), (*square, away), (*square, near)),
                (rows32, rows32, rows, rows, square),
                flops=big,
            )
            outgoing, base = call(
                spread_kernel,
                (cols, (delta, near), (val, near), (ws, near), (wn, near)),
                ((*halo_rows, away), (*rows32, away)),
                (halo_rows, rows32, acc),
                flops=big,
            )
    (grad,) = call(
        final_kernel, ((arrived, near), (base, away), (row, near)), ((*rows, away),), (rows32, rows)
    )
    mine, other = gather(jnp.concatenate(sums[:-1]))
    outs = place(tuple(reversed(range(1, layers))), mine, other, ())
    mine, other = gather(sums[-1])
    outs = place((0,), mine, other, outs)
    return (*outs, grad)


def solution(mesh):
    return jax.shard_map(
        per_device,
        mesh=mesh,
        in_specs=(
            P(AXES, None),
            P(AXES, None),
            P(),
            P(),
            P(AXES, None, None, None),
            P(AXES, None),
            P(AXES, None, None),
            P(AXES, None),
        ),
        out_specs=(P(), P(), P(AXES, None)),
        check_vma=False,
    )
```

time: 402 us -> 188 us (0.47)
  waiting for transfers between devices: 186 us -> 74.6 us
  blocking collectives: 72.8 us -> 18.6 us
  Pallas kernels: 0 us -> 41.4 us
  matrix products: 39.5 us -> 0 us
  local copies, waits for them, and re-layouts: 34.6 us -> 0.01 us
  other arithmetic: 19.4 us -> 1.45 us
  starting transfers between devices: 32.8 us -> 49.7 us
  between operations: 14.7 us -> 1.01 us
    psum x1 -> x0, waiting for transfers between devices: 118 us -> none  [per_device(): self_sum, neigh_sum = lax.psum((self_term, neigh_term), ('gx', 'gy'))]
    all_to_all x4 -> x1, blocking collectives: 72.8 us -> 18.6 us  [exchange(): return lax.all_to_all(sent, AXES, 0, 0, tiled=True).reshape(halo, width)]
    pallas_call x0 -> x19, Pallas kernels: none -> 41.4 us  [call(): pl.pallas_call(body, in_specs=[pl.BlockSpec(memory_space=space) for _, sp...]
    dot_general x27 -> x0, matrix products: 39.5 us -> none  [the longest x3 8 us: spread_back(): jnp.einsum('cn,njd->cjd', onehot, contrib.reshape(-1, tile, width), preci...]
    ppermute x0 -> x32, waiting for transfers between devices: none -> 31.8 us  [the longest x26 16.6 us: flip(): return lax.ppermute(array, 'gy', [(j, j ^ mask) for j in range(inner)])]
    ppermute x0 -> x32, starting transfers between devices: none -> 29.5 us  [the longest x26 19.6 us: flip(): return lax.ppermute(array, 'gy', [(j, j ^ mask) for j in range(inner)])]
    all_to_all x8 -> x5, waiting for transfers between devices: 68.3 us -> 42.8 us  [exchange(): return lax.all_to_all(sent, AXES, 0, 0, tiled=True).reshape(halo, width)]
    all_to_all x8 -> x5, starting transfers between devices: 32.8 us -> 20.1 us  [exchange(): return lax.all_to_all(sent, AXES, 0, 0, tiled=True).reshape(halo, width)]
  transfers between devices with their start and end apart: 9 -> 37, of which waited for: 9 -> 11; matrix products, arithmetic and copies ran while one was open for 7% -> 1% of each run, Pallas kernels for 0% -> 13%
where the time goes in v3:
time: 188 us; the launch traced here: 187 us
  waiting for transfers between devices  74.6 us (40%)
  starting transfers between devices  49.7 us (26%)
  Pallas kernels  41.4 us (22%)
  blocking collectives  18.6 us (10%)
    all_to_all x5, waiting for transfers between devices, exchange(): return lax.all_to_all(sent, AXES, 0, 0, tiled=True).reshape(halo, width)  42.8 us
    pallas_call x19, Pallas kernels, call(): pl.pallas_call(body, in_specs=[pl.BlockSpec(memory_space=space) for _, sp...  41.4 us
    all_to_all x5, starting transfers between devices, exchange(): return lax.all_to_all(sent, AXES, 0, 0, tiled=True).reshape(halo, width)  20.1 us
    ppermute x26, starting transfers between devices, flip(): return lax.ppermute(array, 'gy', [(j, j ^ mask) for j in range(inner)])  19.6 us
    all_to_all x1, blocking collectives, exchange(): return lax.all_to_all(sent, AXES, 0, 0, tiled=True).reshape(halo, width)  18.6 us
    ppermute x26, waiting for transfers between devices, flip(): return lax.ppermute(array, 'gy', [(j, j ^ mask) for j in range(inner)])  16.6 us
    ppermute x6, waiting for transfers between devices, chip_sum(): total = mine.astype(f32) + lax.ppermute(mine, 'gx', perm).astype(f32)  15.1 us
    ppermute x6, starting transfers between devices, chip_sum(): total = mine.astype(f32) + lax.ppermute(mine, 'gx', perm).astype(f32)  9.95 us
  transfers between devices with their start and end apart: 37, of which 11 were waited for; matrix products, arithmetic and copies ran while one was open for 1% of the time, Pallas kernels for 13%

profile of v3, /device:TPU:0, one launch (start us, length us, event | category | flops | bytes accessed | tf_op | source)
XLA Modules:
  0.0 186.7 jit_solution(606423281574290220)
XLA Ops:
  2.8 7.3 %all-to-all-start = ((bf16[32,16,512]{2,1,0:T(8,128)(2,1)}), bf16[32,16,512]{2,1,0:T(8,128)(2,1)S(1)}, u32[]{:S(2)}, u32[]{:S(2)}) async-start(bf16[32,16,512]{2,1,0:T(8,128)(2,1)} %bitcast.25), calls=%async_computation | async-start | bytes 1048576 | tf_op jit(solution)/shard_map/all_to_all | solution.py:328
  11.5 14.2 %all-to-all-done = bf16[32,16,512]{2,1,0:T(8,128)(2,1)S(1)} async-done(((bf16[32,16,512]{2,1,0:T(8,128)(2,1)}), bf16[32,16,512]{2,1,0:T(8,128)(2,1)S(1)}, u32[]{:S(2)}, u32[]{:S(2)}) %all-to-all-start) | async-done | bytes 524320 | tf_op jit(solution)/shard_map/all_to_all | solution.py:328
  25.7 2.6 %shard_map.105 = (bf16[256,512]{1,0:T(8,128)(2,1)}, f32[256,512]{1,0:T(8,128)}, bf16[256,512]{1,0:T(8,128)(2,1)}, bf16[256,512]{1,0:T(8,128)(2,1)S(1)}, bf16[512,512]{1,0:T(8,128)(2,1)}) custom-call(s32[2,4]{1,0:T(2,128)S(1)} %copy-done, bf16[256,512]{1,0:T(8,128)(2,1)S(1)} %get-tuple-element.59.hid, bf16[512,512]{1,0:T(8,128)(2,1)S(1)} %bitcast.17, ...), custom_call_target="tpu_custom_call" | custom-call | flops 536870912 | bytes 3670016 | tf_op jit(solution)/shard_map/pallas_call | solution.py:308
  28.4 3.0 %all-to-all-start.1 = ((bf16[32,16,512]{2,1,0:T(8,128)(2,1)}), bf16[32,16,512]{2,1,0:T(8,128)(2,1)S(1)}, u32[]{:S(2)}, u32[]{:S(2)}) async-start(bf16[32,16,512]{2,1,0:T(8,128)(2,1)} %bitcast.23), calls=%async_computation.1 | async-start | bytes 1048576 | tf_op jit(solution)/shard_map/all_to_all | solution.py:328
  32.6 14.4 %all-to-all-done.1 = bf16[32,16,512]{2,1,0:T(8,128)(2,1)S(1)} async-done(((bf16[32,16,512]{2,1,0:T(8,128)(2,1)}), bf16[32,16,512]{2,1,0:T(8,128)(2,1)S(1)}, u32[]{:S(2)}, u32[]{:S(2)}) %all-to-all-start.1) | async-done | bytes 524320 | tf_op jit(solution)/shard_map/all_to_all | solution.py:328
  47.0 2.7 %shard_map.107 = (bf16[256,512]{1,0:T(8,128)(2,1)}, f32[256,512]{1,0:T(8,128)}, bf16[256,512]{1,0:T(8,128)(2,1)}, bf16[256,512]{1,0:T(8,128)(2,1)S(1)}, bf16[512,512]{1,0:T(8,128)(2,1)}) custom-call(s32[2,4]{1,0:T(2,128)S(1)} %copy-done, bf16[256,512]{1,0:T(8,128)(2,1)S(1)} %get-tuple-element.66.hid, bf16[512,512]{1,0:T(8,128)(2,1)S(1)} %bitcast.18, ...), custom_call_target="tpu_custom_call" | custom-call | flops 536870912 | bytes 3670016 | tf_op jit(solution)/shard_map/pallas_call | solution.py:308
  49.7 3.0 %all-to-all-start.2 = ((bf16[32,16,512]{2,1,0:T(8,128)(2,1)}), bf16[32,16,512]{2,1,0:T(8,128)(2,1)S(1)}, u32[]{:S(2)}, u32[]{:S(2)}) async-start(bf16[32,16,512]{2,1,0:T(8,128)(2,1)} %bitcast.24), calls=%async_computation.2 | async-start | bytes 1048576 | tf_op jit(solution)/shard_map/all_to_all | solution.py:328
  54.0 14.3 %all-to-all-done.2 = bf16[32,16,512]{2,1,0:T(8,128)(2,1)S(1)} async-done(((bf16[32,16,512]{2,1,0:T(8,128)(2,1)}), bf16[32,16,512]{2,1,0:T(8,128)(2,1)S(1)}, u32[]{:S(2)}, u32[]{:S(2)}) %all-to-all-start.2) | async-done | bytes 524320 | tf_op jit(solution)/shard_map/all_to_all | solution.py:328
  68.3 3.4 %shard_map.109 = (bf16[256,512]{1,0:T(8,128)(2,1)}, bf16[256,512]{1,0:T(8,128)(2,1)}, bf16[512,512]{1,0:T(8,128)(2,1)}, f32[256,512]{1,0:T(8,128)}) custom-call(s32[2,4]{1,0:T(2,128)S(1)} %copy-done, bf16[256,512]{1,0:T(8,128)(2,1)S(1)} %get-tuple-element.70.hid, bf16[512,512]{1,0:T(8,128)(2,1)S(1)} %bitcast.20, ...), custom_call_target="tpu_custom_call" | custom-call | flops 1073741824 | bytes 3145728 | tf_op jit(solution)/shard_map/pallas_call | solution.py:308
  71.7 18.6 %all_to_all.30 = bf16[32,16,512]{2,1,0:T(8,128)(2,1)S(1)} all-to-all(bf16[32,16,512]{2,1,0:T(8,128)(2,1)} %bitcast.26), channel_id=1, replica_groups=mesh['gx'=4,'gy'=8] {'gx','gy'}, dimensions={0} | all-to-all | bytes 1048576 | tf_op jit(solution)/shard_map/all_to_all | solution.py:328
  90.3 3.8 %shard_map.110 = (bf16[256,512]{1,0:T(8,128)(2,1)}, bf16[512,512]{1,0:T(8,128)(2,1)}, f32[256,512]{1,0:T(8,128)}) custom-call(s32[2,4]{1,0:T(2,128)S(1)} %copy-done, bf16[512,512]{1,0:T(8,128)(2,1)S(1)} %bitcast.19, f32[256,512]{1,0:T(8,128)} %get-tuple-element.76.before, f32[256,512]{1,0:T(8,128)} %get-tuple-element.77.slope, ...), custom_call_target="tpu_custom_call" | custom-call | flops 536870912 | bytes 2621440 | tf_op jit(solution)/shard_map/pallas_call | solution.py:308
  94.1 3.0 %all-to-all-start.4 = ((bf16[32,16,512]{2,1,0:T(8,128)(2,1)}), bf16[32,16,512]{2,1,0:T(8,128)(2,1)S(1)}, u32[]{:S(2)}, u32[]{:S(2)}) async-start(bf16[32,16,512]{2,1,0:T(8,128)(2,1)} %bitcast.22), calls=%async_computation.4 | async-start | bytes 1048576 | tf_op jit(solution)/shard_map/all_to_all | solution.py:328
  97.1 2.6 %shard_map.113 = (bf16[512,512]{1,0:T(8,128)(2,1)}, bf16[512,512]{1,0:T(8,128)(2,1)S(1)}) custom-call(s32[1]{0:T(128)} %bitcast.core, bf16[256,512]{1,0:T(8,128)(2,1)} %get-tuple-element.88.hid, bf16[256,512]{1,0:T(8,128)(2,1)} %get-tuple-element.89.agg, bf16[256,512]{1,0:T(8,128)(2,1)} %get-tuple-element.90.delta), custom_call_target="tpu_custom_call" | custom-call | flops 268435456 | bytes 2097152 | tf_op jit(solution)/shard_map/pallas_call | solution.py:308
  100.0 2.6 %shard_map.115 = (bf16[512,512]{1,0:T(8,128)(2,1)}, bf16[512,512]{1,0:T(8,128)(2,1)S(1)}) custom-call(s32[1]{0:T(128)} %bitcast.core, bf16[256,512]{1,0:T(8,128)(2,1)} %get-tuple-element.97.hid, bf16[256,512]{1,0:T(8,128)(2,1)} %get-tuple-element.98.agg, bf16[256,512]{1,0:T(8,128)(2,1)} %get-tuple-element.99.delta), custom_call_target="tpu_custom_call" | custom-call | flops 268435456 | bytes 2097152 | tf_op jit(solution)/shard_map/pallas_call | solution.py:308
  108.4 3.6 %collective-permute-done.14 = bf16[128,512]{1,0:T(8,128)(2,1)S(1)} collective-permute-done((bf16[128,512]{1,0:T(8,128)(2,1)S(1)}, bf16[128,512]{1,0:T(8,128)(2,1)S(1)}, u32[]{:S(2)}, u32[]{:S(2)}) %collective-permute-start.14) | collective-permute-done | bytes 131104 | tf_op jit(solution)/shard_map/ppermute | solution.py:337
  112.0 3.8 %collective-permute-done.15 = bf16[128,512]{1,0:T(8,128)(2,1)S(1)} collective-permute-done((bf16[128,512]{1,0:T(8,128)(2,1)S(1)}, bf16[128,512]{1,0:T(8,128)(2,1)S(1)}, u32[]{:S(2)}, u32[]{:S(2)}) %collective-permute-start.15) | collective-permute-done | bytes 131104 | tf_op jit(solution)/shard_map/ppermute | solution.py:337
  123.9 2.9 %shard_map.111 = (bf16[256,512]{1,0:T(8,128)(2,1)S(1)}, bf16[512,512]{1,0:T(8,128)(2,1)}, bf16[512,512]{1,0:T(8,128)(2,1)S(1)}) custom-call(s32[1]{0:T(128)} %bitcast.core, bf16[256,512]{1,0:T(8,128)(2,1)} %hid.1, bf16[256,512]{1,0:T(8,128)(2,1)} %get-tuple-element.65.agg, bf16[512,512]{1,0:T(8,128)(2,1)S(1)} %bitcast.16, ...), custom_call_target="tpu_custom_call" | custom-call | flops 536870912 | bytes 2621440 | tf_op jit(solution)/shard_map/pallas_call | solution.py:308
  131.1 5.7 %collective-permute-done.18 = bf16[128,512]{1,0:T(8,128)(2,1)S(1)} collective-permute-done((bf16[128,512]{1,0:T(8,128)(2,1)S(1)}, bf16[128,512]{1,0:T(8,128)(2,1)S(1)}, u32[]{:S(2)}, u32[]{:S(2)}) %collective-permute-start.18) | collective-permute-done | bytes 131104 | tf_op jit(solution)/shard_map/ppermute | solution.py:355
  142.3 2.5 %shard_map.120 = (bf16[512,512]{1,0:T(8,128)(2,1)}, f32[256,512]{1,0:T(8,128)}) custom-call(s32[2,4]{1,0:T(2,128)S(1)} %copy-done, bf16[256,512]{1,0:T(8,128)(2,1)S(1)} %get-tuple-element.110.delta, bf16[2,4,128,128]{3,2,1,0:T(8,128)(2,1)S(1)} %get-tuple-element.61.val, bf16[512,512]{1,0:T(8,128)(2,1)S(1)} %get-tuple-element.111.ws, ...), custom_call_target="tpu_custom_call" | custom-call | flops 536870912 | bytes 2097152 | tf_op jit(solution)/shard_map/pallas_call | solution.py:308
  144.8 3.8 %all-to-all-start.5 = ((bf16[32,16,512]{2,1,0:T(8,128)(2,1)}), bf16[32,16,512]{2,1,0:T(8,128)(2,1)S(1)}, u32[]{:S(2)}, u32[]{:S(2)}) async-start(bf16[32,16,512]{2,1,0:T(8,128)(2,1)} %bitcast.21), calls=%async_computation.5 | async-start | bytes 1048576 | tf_op jit(solution)/shard_map/all_to_all | solution.py:328
  154.2 7.4 %collective-permute-done.4 = bf16[128,512]{1,0:T(8,128)(2,1)S(1)} collective-permute-done((bf16[128,512]{1,0:T(8,128)(2,1)S(1)}, bf16[128,512]{1,0:T(8,128)(2,1)S(1)}, u32[]{:S(2)}, u32[]{:S(2)}) %collective-permute-start.4) | collective-permute-done | bytes 131104 | tf_op jit(solution)/shard_map/ppermute | solution.py:355
  161.7 3.5 %collective-permute-start.5 = (bf16[128,512]{1,0:T(8,128)(2,1)S(1)}, bf16[128,512]{1,0:T(8,128)(2,1)S(1)}, u32[]{:S(2)}, u32[]{:S(2)}) collective-permute-start(bf16[128,512]{1,0:T(8,128)(2,1)S(1)} %add_convert_fusion.4), channel_id=1, source_target_pairs={{0,16},{8,24},{16,0},{24,8},{1,17},{9,25},{17,1},{25,9},{2,18},{10... | collective-permute-start | bytes 393224 | tf_op jit(solution)/shard_map/ppermute | solution.py:355
  165.8 3.4 %collective-permute-done.27.refs_3_ = bf16[256,512]{1,0:T(8,128)(2,1)S(1)} collective-permute-done((bf16[256,512]{1,0:T(8,128)(2,1)S(1)}, bf16[256,512]{1,0:T(8,128)(2,1)S(1)}, u32[]{:S(2)}, u32[]{:S(2)}) %collective-permute-start.27) | collective-permute-done | bytes 262176 | tf_op jit(solution)/shard_map/ppermute | solution.py:337
  176.8 3.8 %collective-permute-done.7.refs_2_ = bf16[128,512]{1,0:T(8,128)(2,1)S(1)} collective-permute-done((bf16[128,512]{1,0:T(8,128)(2,1)S(1)}, bf16[128,512]{1,0:T(8,128)(2,1)S(1)}, u32[]{:S(2)}, u32[]{:S(2)}) %collective-permute-start.7) | collective-permute-done | bytes 131104 | tf_op jit(solution)/shard_map/ppermute | solution.py:337
  (83 shorter events, 49.7 us)
Async XLA Ops:
  2.8 23.0 %all-to-all-start = ((bf16[32,16,512]{2,1,0:T(8,128)(2,1)}), bf16[32,16,512]{2,1,0:T(8,128)(2,1)S(1)}, u32[]{:S(2)}, u32[]{:S(2)}) async-start(bf16[32,16,512]{2,1,0:T(8,128)(2,1)} %bitcast.25), calls=%async_computation | async-start | bytes 1048576 | tf_op jit(solution)/shard_map/all_to_all | solution.py:328
  28.4 18.6 %all-to-all-start.1 = ((bf16[32,16,512]{2,1,0:T(8,128)(2,1)}), bf16[32,16,512]{2,1,0:T(8,128)(2,1)S(1)}, u32[]{:S(2)}, u32[]{:S(2)}) async-start(bf16[32,16,512]{2,1,0:T(8,128)(2,1)} %bitcast.23), calls=%async_computation.1 | async-start | bytes 1048576 | tf_op jit(solution)/shard_map/all_to_all | solution.py:328
  49.7 18.6 %all-to-all-start.2 = ((bf16[32,16,512]{2,1,0:T(8,128)(2,1)}), bf16[32,16,512]{2,1,0:T(8,128)(2,1)S(1)}, u32[]{:S(2)}, u32[]{:S(2)}) async-start(bf16[32,16,512]{2,1,0:T(8,128)(2,1)} %bitcast.24), calls=%async_computation.2 | async-start | bytes 1048576 | tf_op jit(solution)/shard_map/all_to_all | solution.py:328
  94.1 29.8 %all-to-all-start.4 = ((bf16[32,16,512]{2,1,0:T(8,128)(2,1)}), bf16[32,16,512]{2,1,0:T(8,128)(2,1)S(1)}, u32[]{:S(2)}, u32[]{:S(2)}) async-start(bf16[32,16,512]{2,1,0:T(8,128)(2,1)} %bitcast.22), calls=%async_computation.4 | async-start | bytes 1048576 | tf_op jit(solution)/shard_map/all_to_all | solution.py:328
  102.7 15.9 %collective-permute-start.19 = (bf16[512,512]{1,0:T(8,128)(2,1)S(1)}, bf16[512,512]{1,0:T(8,128)(2,1)S(1)}, u32[]{:S(2)}, u32[]{:S(2)}) collective-permute-start(bf16[512,512]{1,0:T(8,128)(2,1)S(1)} %get-tuple-element.101), channel_id=1, source_target_pairs={{0,1},{1,0},{2,3},{3,2},{4,5},{5,4},{6,7},{7,6},{8,9},{9,8},{10,11... | collective-permute-start | bytes 1572872 | tf_op jit(solution)/shard_map/ppermute | solution.py:337
  106.6 9.1 %collective-permute-start.15 = (bf16[128,512]{1,0:T(8,128)(2,1)S(1)}, bf16[128,512]{1,0:T(8,128)(2,1)S(1)}, u32[]{:S(2)}, u32[]{:S(2)}) collective-permute-start(bf16[128,512]{1,0:T(8,128)(2,1)S(1)} %get-tuple-element.95), channel_id=1, source_target_pairs={{0,4},{1,5},{2,6},{3,7},{4,0},{5,1},{6,2},{7,3},{8,12},{9,13},{10,... | collective-permute-start | bytes 393224 | tf_op jit(solution)/shard_map/ppermute | solution.py:337
  115.9 11.1 %collective-permute-start.17 = (bf16[128,512]{1,0:T(8,128)(2,1)S(1)}, bf16[128,512]{1,0:T(8,128)(2,1)S(1)}, u32[]{:S(2)}, u32[]{:S(2)}) collective-permute-start(bf16[128,512]{1,0:T(8,128)(2,1)S(1)} %add_convert_fusion.3), channel_id=1, source_target_pairs={{0,8},{8,0},{16,24},{24,16},{1,9},{9,1},{17,25},{25,17},{2,10},{10... | collective-permute-start | bytes 393224 | tf_op jit(solution)/shard_map/ppermute | solution.py:355
  120.4 8.7 %collective-permute-start.20 = (bf16[128,512]{1,0:T(8,128)(2,1)S(1)}, bf16[128,512]{1,0:T(8,128)(2,1)S(1)}, u32[]{:S(2)}, u32[]{:S(2)}) collective-permute-start(bf16[128,512]{1,0:T(8,128)(2,1)S(1)} %get-tuple-element.103), channel_id=1, source_target_pairs={{0,2},{1,3},{2,0},{3,1},{4,6},{5,7},{6,4},{7,5},{8,10},{9,11},{10,... | collective-permute-start | bytes 393224 | tf_op jit(solution)/shard_map/ppermute | solution.py:337
  126.9 9.9 %collective-permute-start = (bf16[512,512]{1,0:T(8,128)(2,1)S(1)}, bf16[512,512]{1,0:T(8,128)(2,1)S(1)}, u32[]{:S(2)}, u32[]{:S(2)}) collective-permute-start(bf16[512,512]{1,0:T(8,128)(2,1)S(1)} %get-tuple-element.83), channel_id=1, source_target_pairs={{0,1},{1,0},{2,3},{3,2},{4,5},{5,4},{6,7},{7,6},{8,9},{9,8},{10,11... | collective-permute-start | bytes 1572872 | tf_op jit(solution)/shard_map/ppermute | solution.py:337
  127.0 9.8 %collective-permute-start.18 = (bf16[128,512]{1,0:T(8,128)(2,1)S(1)}, bf16[128,512]{1,0:T(8,128)(2,1)S(1)}, u32[]{:S(2)}, u32[]{:S(2)}) collective-permute-start(bf16[128,512]{1,0:T(8,128)(2,1)S(1)} %add_convert_fusion.2), channel_id=1, source_target_pairs={{0,16},{8,24},{16,0},{24,8},{1,17},{9,25},{17,1},{25,9},{2,18},{10... | collective-permute-start | bytes 393224 | tf_op jit(solution)/shard_map/ppermute | solution.py:355
  130.1 12.2 %collective-permute-start.23 = (bf16[128,512]{1,0:T(8,128)(2,1)S(1)}, bf16[128,512]{1,0:T(8,128)(2,1)S(1)}, u32[]{:S(2)}, u32[]{:S(2)}) collective-permute-start(bf16[128,512]{1,0:T(8,128)(2,1)S(1)} %add_convert_fusion.1), channel_id=1, source_target_pairs={{0,8},{8,0},{16,24},{24,16},{1,9},{9,1},{17,25},{25,17},{2,10},{10... | collective-permute-start | bytes 393224 | tf_op jit(solution)/shard_map/ppermute | solution.py:355
  138.7 10.0 %collective-permute-start.1 = (bf16[128,512]{1,0:T(8,128)(2,1)S(1)}, bf16[128,512]{1,0:T(8,128)(2,1)S(1)}, u32[]{:S(2)}, u32[]{:S(2)}) collective-permute-start(bf16[128,512]{1,0:T(8,128)(2,1)S(1)} %get-tuple-element.85), channel_id=1, source_target_pairs={{0,2},{1,3},{2,0},{3,1},{4,6},{5,7},{6,4},{7,5},{8,10},{9,11},{10,... | collective-permute-start | bytes 393224 | tf_op jit(solution)/shard_map/ppermute | solution.py:337
  139.7 9.0 %collective-permute-start.2 = (bf16[128,512]{1,0:T(8,128)(2,1)S(1)}, bf16[128,512]{1,0:T(8,128)(2,1)S(1)}, u32[]{:S(2)}, u32[]{:S(2)}) collective-permute-start(bf16[128,512]{1,0:T(8,128)(2,1)S(1)} %get-tuple-element.86), channel_id=1, source_target_pairs={{0,4},{1,5},{2,6},{3,7},{4,0},{5,1},{6,2},{7,3},{8,12},{9,13},{10,... | collective-permute-start | bytes 393224 | tf_op jit(solution)/shard_map/ppermute | solution.py:337
  142.3 8.3 %collective-permute-start.24 = (bf16[128,512]{1,0:T(8,128)(2,1)S(1)}, bf16[128,512]{1,0:T(8,128)(2,1)S(1)}, u32[]{:S(2)}, u32[]{:S(2)}) collective-permute-start(bf16[128,512]{1,0:T(8,128)(2,1)S(1)} %add_convert_fusion), channel_id=1, source_target_pairs={{0,16},{8,24},{16,0},{24,8},{1,17},{9,25},{17,1},{25,9},{2,18},{10... | collective-permute-start | bytes 393224 | tf_op jit(solution)/shard_map/ppermute | solution.py:355
  144.8 38.4 %all-to-all-start.5 = ((bf16[32,16,512]{2,1,0:T(8,128)(2,1)}), bf16[32,16,512]{2,1,0:T(8,128)(2,1)S(1)}, u32[]{:S(2)}, u32[]{:S(2)}) async-start(bf16[32,16,512]{2,1,0:T(8,128)(2,1)} %bitcast.21), calls=%async_computation.5 | async-start | bytes 1048576 | tf_op jit(solution)/shard_map/all_to_all | solution.py:328
  148.8 12.9 %collective-permute-start.4 = (bf16[128,512]{1,0:T(8,128)(2,1)S(1)}, bf16[128,512]{1,0:T(8,128)(2,1)S(1)}, u32[]{:S(2)}, u32[]{:S(2)}) collective-permute-start(bf16[128,512]{1,0:T(8,128)(2,1)S(1)} %add_convert_fusion.5), channel_id=1, source_target_pairs={{0,8},{8,0},{16,24},{24,16},{1,9},{9,1},{17,25},{25,17},{2,10},{10... | collective-permute-start | bytes 393224 | tf_op jit(solution)/shard_map/ppermute | solution.py:355
  150.7 14.6 %collective-permute-start.25 = (bf16[256,512]{1,0:T(8,128)(2,1)S(1)}, bf16[256,512]{1,0:T(8,128)(2,1)S(1)}, u32[]{:S(2)}, u32[]{:S(2)}) collective-permute-start(bf16[256,512]{1,0:T(8,128)(2,1)S(1)} %pad_maximum_fusion.refs_0_), channel_id=1, source_target_pairs={{0,2},{1,3},{2,0},{3,1},{4,6},{5,7},{6,4},{7,5},{8,10},{9,11},{10,... | collective-permute-start | bytes 786440 | tf_op jit(solution)/shard_map/ppermute | solution.py:337
  152.2 13.6 %collective-permute-start.26 = (bf16[256,512]{1,0:T(8,128)(2,1)S(1)}, bf16[256,512]{1,0:T(8,128)(2,1)S(1)}, u32[]{:S(2)}, u32[]{:S(2)}) collective-permute-start(bf16[256,512]{1,0:T(8,128)(2,1)S(1)} %pad_maximum_fusion.refs_0_), channel_id=1, source_target_pairs={{0,4},{1,5},{2,6},{3,7},{4,0},{5,1},{6,2},{7,3},{8,12},{9,13},{10,... | collective-permute-start | bytes 786440 | tf_op jit(solution)/shard_map/ppermute | solution.py:337
  153.7 15.6 %collective-permute-start.27 = (bf16[256,512]{1,0:T(8,128)(2,1)S(1)}, bf16[256,512]{1,0:T(8,128)(2,1)S(1)}, u32[]{:S(2)}, u32[]{:S(2)}) collective-permute-start(bf16[256,512]{1,0:T(8,128)(2,1)S(1)} %pad_maximum_fusion.refs_0_), channel_id=1, source_target_pairs={{0,6},{1,7},{2,4},{3,5},{4,2},{5,3},{6,0},{7,1},{8,14},{9,15},{10,... | collective-permute-start | bytes 786440 | tf_op jit(solution)/shard_map/ppermute | solution.py:337
  161.7 9.6 %collective-permute-start.5 = (bf16[128,512]{1,0:T(8,128)(2,1)S(1)}, bf16[128,512]{1,0:T(8,128)(2,1)S(1)}, u32[]{:S(2)}, u32[]{:S(2)}) collective-permute-start(bf16[128,512]{1,0:T(8,128)(2,1)S(1)} %add_convert_fusion.4), channel_id=1, source_target_pairs={{0,16},{8,24},{16,0},{24,8},{1,17},{9,25},{17,1},{25,9},{2,18},{10... | collective-permute-start | bytes 393224 | tf_op jit(solution)/shard_map/ppermute | solution.py:355
  165.2 9.1 %collective-permute-start.29 = (bf16[256,512]{1,0:T(8,128)(2,1)S(1)}, bf16[256,512]{1,0:T(8,128)(2,1)S(1)}, u32[]{:S(2)}, u32[]{:S(2)}) collective-permute-start(bf16[256,512]{1,0:T(8,128)(2,1)S(1)} %collective-permute-done.25.refs_1_), channel_id=1, source_target_pairs={{0,1},{1,0},{2,3},{3,2},{4,5},{5,4},{6,7},{7,6},{8,9},{9,8},{10,11... | collective-permute-start | bytes 786440 | tf_op jit(solution)/shard_map/ppermute | solution.py:337
  165.8 9.1 %collective-permute-start.30 = (bf16[256,512]{1,0:T(8,128)(2,1)S(1)}, bf16[256,512]{1,0:T(8,128)(2,1)S(1)}, u32[]{:S(2)}, u32[]{:S(2)}) collective-permute-start(bf16[256,512]{1,0:T(8,128)(2,1)S(1)} %collective-permute-done.26.refs_2_), channel_id=1, source_target_pairs={{0,1},{1,0},{2,3},{3,2},{4,5},{5,4},{6,7},{7,6},{8,9},{9,8},{10,11... | collective-permute-start | bytes 786440 | tf_op jit(solution)/shard_map/ppermute | solution.py:337
  169.3 12.0 %collective-permute-start.31 = (bf16[256,512]{1,0:T(8,128)(2,1)S(1)}, bf16[256,512]{1,0:T(8,128)(2,1)S(1)}, u32[]{:S(2)}, u32[]{:S(2)}) collective-permute-start(bf16[256,512]{1,0:T(8,128)(2,1)S(1)} %collective-permute-done.27.refs_3_), channel_id=1, source_target_pairs={{0,1},{1,0},{2,3},{3,2},{4,5},{5,4},{6,7},{7,6},{8,9},{9,8},{10,11... | collective-permute-start | bytes 786440 | tf_op jit(solution)/shard_map/ppermute | solution.py:337
  174.9 10.3 %collective-permute-start.9 = (bf16[128,512]{1,0:T(8,128)(2,1)S(1)}, bf16[128,512]{1,0:T(8,128)(2,1)S(1)}, u32[]{:S(2)}, u32[]{:S(2)}) collective-permute-start(bf16[128,512]{1,0:T(8,128)(2,1)S(1)} %multiply_convert_fusion.2.refs_0_), channel_id=1, source_target_pairs={{0,1},{1,0},{2,3},{3,2},{4,5},{5,4},{6,7},{7,6},{8,9},{9,8},{10,11... | collective-permute-start | bytes 393224 | tf_op jit(solution)/shard_map/ppermute | solution.py:337
  (14 other events, 101.1 us)

commit v4 on v3

--- a/solution.py
+++ b/solution.py
@@ -174,20 +174,13 @@
 
 def backward_kernel(
     cols, arr, before, slope, row, val, ws, wn, delta_out, halo_out, base_out,
-    before_v, slope_v, delta_v, halo_v, base_v, acc_v, sems,
+    before_v, slope_v, halo_v, base_v, acc_v, sems,
 ):
     go = Copies(sems)
     loads = [go.start(before, before_v), go.start(slope, slope_v)]
     delta = delta_of(loads, arr, row, before_v, slope_v)
-    delta_v[...] = delta
-    go.store(delta_v, delta_out)
+    delta_out[...] = delta
     spread_back(go, delta, cols, val, ws, wn, halo_out, base_out, halo_v, base_v, acc_v)
-    go.finish()
-
-
-def spread_kernel(cols, delta, val, ws, wn, halo_out, base_out, halo_v, base_v, acc_v, sems):
-    go = Copies(sems)
-    spread_back(go, delta[...], cols, val, ws, wn, halo_out, base_out, halo_v, base_v, acc_v)
     go.finish()
 
 
@@ -210,51 +203,24 @@
                 target[...] = mm_tn(source[...], delta).astype(jnp.bfloat16)
 
 
-def weight_kernel(core, hid, agg, delta, keep_out, give, hid_v, agg_v, delta_v, keep_v, sems):
+def weight_kernel(core, hid, agg, delta, keep, give, hid_v, agg_v, delta_v, sems):
     go = Copies(sems)
     loads = [go.start(delta, delta_v), go.start(hid, hid_v), go.start(agg, agg_v)]
     for load in loads:
         load.wait()
-    products(core[0], hid_v, agg_v, delta_v[...], (give, keep_v))
-    go.store(keep_v, keep_out)
-    go.finish()
-
-
-def top_kernel(
-    core, hid, agg, arr, before, slope, row, delta_near, keep_out, give,
-    before_v, slope_v, hid_v, agg_v, keep_v, sems,
-):
-    go = Copies(sems)
-    loads = [go.start(before, before_v), go.start(slope, slope_v)]
-    late = [go.start(hid, hid_v), go.start(agg, agg_v)]
-    delta = delta_of(loads, arr, row, before_v, slope_v)
-    delta_near[...] = delta
-    for load in late:
-        load.wait()
-    products(core[0], hid_v, agg_v, delta, (give, keep_v))
-    go.store(keep_v, keep_out)
-    go.finish()
-
-
-def quarters_kernel(chip, keep, got, *rest):
-    count = len(rest) - 4
-    outs, (keep_v, got_v, out_v, sems) = rest[:count], rest[count:]
-    go = Copies(sems)
-    size = keep.shape[0] // count
-    loads = []
-    for m in range(count):
-        at = pl.multiple_of((chip[0] ^ m) * size, size)
-        here = pl.ds(m * size, size)
-        loads.append(go.start(keep.at[pl.ds(at, size)], keep_v.at[here]))
-        loads.append(go.start(got.at[pl.ds(at, size)], got_v.at[here]))
-    for m in range(count):
-        loads[2 * m].wait()
-        loads[2 * m + 1].wait()
-        here = pl.ds(m * size, size)
-        total = keep_v[here, :].astype(jnp.float32) + got_v[here, :].astype(jnp.float32)
-        out_v[here, :] = total.astype(jnp.bfloat16)
-        go.store(out_v.at[here], outs[m])
-    go.finish()
+    products(core[0], hid_v, agg_v, delta_v[...], (give, keep))
+
+
+def near_weight_kernel(core, hid, agg, delta, keep, give, sems):
+    products(core[0], hid, agg, delta[...], (give, keep))
+
+
+def quarters_kernel(chip, keep, got, *outs):
+    size = outs[0].shape[0]
+    for m, out in enumerate(outs[:-1]):
+        at = pl.ds(pl.multiple_of((chip[0] ^ m) * size, size), size)
+        total = keep[at, :].astype(jnp.float32) + got[at, :].astype(jnp.float32)
+        out[...] = total.astype(jnp.bfloat16)
 
 
 def place_kernel(layers, count, where, *refs):
@@ -340,10 +306,8 @@
         got = flip(give, 1)
         mine, *others = call(
             quarters_kernel,
-            ((chip.reshape(1), scalars), (keep, away), (got, near)),
+            ((chip.reshape(1), scalars), (keep, near), (got, near)),
             (((width // chips, width), bf16, near),) * chips,
-            (square, square, square),
-            3 * chips,
         )
         total = mine.astype(f32)
         for m, other in enumerate(others, 1):
@@ -423,51 +387,36 @@
         flops=2 * big,
     )
     aggregates.append(aggregate)
-    sums = []
+    sums, delta_at = [], away
     for layer in reversed(range(layers)):
         below = layer - 1
         if layer:
-            keep, give = call(
-                weight_kernel,
-                (
-                    (core_arg, scalars), (hiddens[layer], away), (aggregates[layer], away),
-                    (delta, away),
-                ),
-                ((*square, away), (*square, near)),
-                (rows, rows, rows, square),
-                flops=big // 2,
-            )
+            sources = ((hiddens[layer], away), (aggregates[layer], away), (delta, delta_at))
+        else:
+            sources = ((hid, near), (agg, near), (delta, near))
+        keep, give = call(
+            weight_kernel if layer else near_weight_kernel,
+            ((core_arg, scalars), *sources),
+            ((*square, near), (*square, near)),
+            (rows, rows, rows) if layer else (),
+            flops=big // 2,
+        )
         sums.append(chip_sum(keep, give))
         arrived = exchange(outgoing)
         if layer:
-            ws, wn = load(below)
-        if below > 0:
+            last = (hiddens[0], aggregates[0]) if below == 0 else ()
+            ws, wn, *more = load(below, *last)
+            if more:
+                hid, agg = more
+            delta_at = near
             delta, outgoing, base = call(
                 backward_kernel,
                 (
                     cols, (arrived, near), (base, away), (slopes[below], away), (row, near),
                     (val, near), (ws, near), (wn, near),
                 ),
-                ((*rows, away), (*halo_rows, away), (*rows32, away)),
-                (rows32, rows32, rows, halo_rows, rows32, acc),
-                flops=big,
-            )
-        elif below == 0:
-            delta, keep, give = call(
-                top_kernel,
-                (
-                    (core_arg, scalars), (hiddens[0], away), (aggregates[0], away),
-                    (arrived, near), (base, away), (slopes[0], away), (row, near),
-                ),
-                ((*rows, near), (*square, away), (*square, near)),
-                (rows32, rows32, rows, rows, square),
-                flops=big,
-            )
-            outgoing, base = call(
-                spread_kernel,
-                (cols, (delta, near), (val, near), (ws, near), (wn, near)),
-                ((*halo_rows, away), (*rows32, away)),
-                (halo_rows, rows32, acc),
+                ((*rows, near), (*halo_rows, away), (*rows32, away)),
+                (rows32, rows32, halo_rows, rows32, acc),
                 flops=big,
             )
     (grad,) = call(

time: 188 us -> 185 us (0.984)
  Pallas kernels: 41.4 us -> 34.8 us
  waiting for transfers between devices: 74.6 us -> 78.7 us
  starting transfers between devices: 49.7 us -> 47.3 us
    pallas_call x19, Pallas kernels: 41.4 us -> 34.8 us  [call(): pl.pallas_call(body, in_specs=[pl.BlockSpec(memory_space=space) for _, sp...]
    ppermute x6, starting transfers between devices: 9.95 us -> 7.11 us  [chip_sum(): total = mine.astype(f32) + lax.ppermute(mine, 'gx', perm).astype(f32)]
    ppermute x26, waiting for transfers between devices: 16.6 us -> 19.2 us  [flip(): return lax.ppermute(array, 'gy', [(j, j ^ mask) for j in range(inner)])]
  transfers between devices with their start and end apart: 37 -> 37, of which waited for: 11 -> 14; matrix products, arithmetic and copies ran while one was open for 1% -> 1% of each run, Pallas kernels for 13% -> 10%
where the time goes in v4:
time: 185 us; the launch traced here: 184 us
  waiting for transfers between devices  78.7 us (43%)
  starting transfers between devices  47.3 us (26%)
  Pallas kernels  34.8 us (19%)
  blocking collectives  18.6 us (10%)
  other arithmetic  2.15 us (1%)
    all_to_all x5, waiting for transfers between devices, exchange(): return lax.all_to_all(sent, AXES, 0, 0, tiled=True).reshape(halo, width)  42.8 us
    pallas_call x19, Pallas kernels, call(): pl.pallas_call(body, in_specs=[pl.BlockSpec(memory_space=space) for _, sp...  34.8 us
    all_to_all x5, starting transfers between devices, exchange(): return lax.all_to_all(sent, AXES, 0, 0, tiled=True).reshape(halo, width)  20.3 us
    ppermute x26, starting transfers between devices, flip(): return lax.ppermute(array, 'gy', [(j, j ^ mask) for j in range(inner)])  19.9 us
    ppermute x26, waiting for transfers between devices, flip(): return lax.ppermute(array, 'gy', [(j, j ^ mask) for j in range(inner)])  19.2 us
    all_to_all x1, blocking collectives, exchange(): return lax.all_to_all(sent, AXES, 0, 0, tiled=True).reshape(halo, width)  18.6 us
    ppermute x6, waiting for transfers between devices, chip_sum(): total = mine.astype(f32) + lax.ppermute(mine, 'gx', perm).astype(f32)  16.7 us
    ppermute x6, starting transfers between devices, chip_sum(): total = mine.astype(f32) + lax.ppermute(mine, 'gx', perm).astype(f32)  7.11 us
  transfers between devices with their start and end apart: 37, of which 14 were waited for; matrix products, arithmetic and copies ran while one was open for 1% of the time, Pallas kernels for 10%

profile of v4, /device:TPU:0, one launch (start us, length us, event | category | flops | bytes accessed | tf_op | source)
XLA Modules:
  0.0 184.1 jit_solution(18144722010545952460)
XLA Ops:
  0.6 2.1 %shard_map.104 = (s32[1,512]{1,0:T(1,128)S(1)}, s32[512,1]{1,0:T(8,128)S(1)}, bf16[512,512]{1,0:T(8,128)(2,1)}) custom-call(s32[1,16,32]{2,1,0:T(8,128)} %bitcast.26, s32[1,32]{1,0:T(1,128)} %cnt.1, bf16[256,512]{1,0:T(8,128)(2,1)} %refs_2_.4), custom_call_target="tpu_custom_call" | custom-call | bytes 1056768 | tf_op jit(solution)/shard_map/pallas_call | solution.py:274
  2.8 7.3 %all-to-all-start = ((bf16[32,16,512]{2,1,0:T(8,128)(2,1)}), bf16[32,16,512]{2,1,0:T(8,128)(2,1)S(1)}, u32[]{:S(2)}, u32[]{:S(2)}) async-start(bf16[32,16,512]{2,1,0:T(8,128)(2,1)} %bitcast.24), calls=%async_computation | async-start | bytes 1048576 | tf_op jit(solution)/shard_map/all_to_all | solution.py:294
  11.5 14.2 %all-to-all-done = bf16[32,16,512]{2,1,0:T(8,128)(2,1)S(1)} async-done(((bf16[32,16,512]{2,1,0:T(8,128)(2,1)}), bf16[32,16,512]{2,1,0:T(8,128)(2,1)S(1)}, u32[]{:S(2)}, u32[]{:S(2)}) %all-to-all-start) | async-done | bytes 524320 | tf_op jit(solution)/shard_map/all_to_all | solution.py:294
  25.7 2.6 %shard_map.105 = (bf16[256,512]{1,0:T(8,128)(2,1)}, f32[256,512]{1,0:T(8,128)}, bf16[256,512]{1,0:T(8,128)(2,1)}, bf16[256,512]{1,0:T(8,128)(2,1)S(1)}, bf16[512,512]{1,0:T(8,128)(2,1)}) custom-call(s32[2,4]{1,0:T(2,128)S(1)} %copy-done, bf16[256,512]{1,0:T(8,128)(2,1)S(1)} %get-tuple-element.61.hid, bf16[512,512]{1,0:T(8,128)(2,1)S(1)} %bitcast.17, ...), custom_call_target="tpu_custom_call" | custom-call | flops 536870912 | bytes 3670016 | tf_op jit(solution)/shard_map/pallas_call | solution.py:274
  28.4 3.0 %all-to-all-start.1 = ((bf16[32,16,512]{2,1,0:T(8,128)(2,1)}), bf16[32,16,512]{2,1,0:T(8,128)(2,1)S(1)}, u32[]{:S(2)}, u32[]{:S(2)}) async-start(bf16[32,16,512]{2,1,0:T(8,128)(2,1)} %bitcast.22), calls=%async_computation.1 | async-start | bytes 1048576 | tf_op jit(solution)/shard_map/all_to_all | solution.py:294
  32.6 14.4 %all-to-all-done.1 = bf16[32,16,512]{2,1,0:T(8,128)(2,1)S(1)} async-done(((bf16[32,16,512]{2,1,0:T(8,128)(2,1)}), bf16[32,16,512]{2,1,0:T(8,128)(2,1)S(1)}, u32[]{:S(2)}, u32[]{:S(2)}) %all-to-all-start.1) | async-done | bytes 524320 | tf_op jit(solution)/shard_map/all_to_all | solution.py:294
  47.0 2.6 %shard_map.108 = (bf16[256,512]{1,0:T(8,128)(2,1)}, f32[256,512]{1,0:T(8,128)}, bf16[256,512]{1,0:T(8,128)(2,1)}, bf16[256,512]{1,0:T(8,128)(2,1)S(1)}, bf16[512,512]{1,0:T(8,128)(2,1)}) custom-call(s32[2,4]{1,0:T(2,128)S(1)} %copy-done, bf16[256,512]{1,0:T(8,128)(2,1)S(1)} %get-tuple-element.70.hid, bf16[512,512]{1,0:T(8,128)(2,1)S(1)} %bitcast.18, ...), custom_call_target="tpu_custom_call" | custom-call | flops 536870912 | bytes 3670016 | tf_op jit(solution)/shard_map/pallas_call | solution.py:274
  49.6 3.0 %all-to-all-start.2 = ((bf16[32,16,512]{2,1,0:T(8,128)(2,1)}), bf16[32,16,512]{2,1,0:T(8,128)(2,1)S(1)}, u32[]{:S(2)}, u32[]{:S(2)}) async-start(bf16[32,16,512]{2,1,0:T(8,128)(2,1)} %bitcast.23), calls=%async_computation.2 | async-start | bytes 1048576 | tf_op jit(solution)/shard_map/all_to_all | solution.py:294
  53.9 14.3 %all-to-all-done.2 = bf16[32,16,512]{2,1,0:T(8,128)(2,1)S(1)} async-done(((bf16[32,16,512]{2,1,0:T(8,128)(2,1)}), bf16[32,16,512]{2,1,0:T(8,128)(2,1)S(1)}, u32[]{:S(2)}, u32[]{:S(2)}) %all-to-all-start.2) | async-done | bytes 524320 | tf_op jit(solution)/shard_map/all_to_all | solution.py:294
  68.2 3.4 %shard_map.110 = (bf16[256,512]{1,0:T(8,128)(2,1)}, bf16[256,512]{1,0:T(8,128)(2,1)}, bf16[512,512]{1,0:T(8,128)(2,1)}, f32[256,512]{1,0:T(8,128)}) custom-call(s32[2,4]{1,0:T(2,128)S(1)} %copy-done, bf16[256,512]{1,0:T(8,128)(2,1)S(1)} %get-tuple-element.74.hid, bf16[512,512]{1,0:T(8,128)(2,1)S(1)} %bitcast.20, ...), custom_call_target="tpu_custom_call" | custom-call | flops 1073741824 | bytes 3145728 | tf_op jit(solution)/shard_map/pallas_call | solution.py:274
  71.6 18.6 %all_to_all.30 = bf16[32,16,512]{2,1,0:T(8,128)(2,1)S(1)} all-to-all(bf16[32,16,512]{2,1,0:T(8,128)(2,1)} %bitcast.25), channel_id=1, replica_groups=mesh['gx'=4,'gy'=8] {'gx','gy'}, dimensions={0} | all-to-all | bytes 1048576 | tf_op jit(solution)/shard_map/all_to_all | solution.py:294
  90.2 3.8 %shard_map.111 = (bf16[256,512]{1,0:T(8,128)(2,1)S(1)}, bf16[512,512]{1,0:T(8,128)(2,1)}, f32[256,512]{1,0:T(8,128)}) custom-call(s32[2,4]{1,0:T(2,128)S(1)} %copy-done, bf16[512,512]{1,0:T(8,128)(2,1)S(1)} %bitcast.19, f32[256,512]{1,0:T(8,128)} %get-tuple-element.80.before, f32[256,512]{1,0:T(8,128)} %get-tuple-element.81.slope, ...), custom_call_target="tpu_custom_call" | custom-call | flops 536870912 | bytes 2621440 | tf_op jit(solution)/shard_map/pallas_call | solution.py:274
  94.7 3.0 %all-to-all-start.4 = ((bf16[32,16,512]{2,1,0:T(8,128)(2,1)}), bf16[32,16,512]{2,1,0:T(8,128)(2,1)S(1)}, u32[]{:S(2)}, u32[]{:S(2)}) async-start(bf16[32,16,512]{2,1,0:T(8,128)(2,1)} %bitcast.21), calls=%async_computation.4 | async-start | bytes 1048576 | tf_op jit(solution)/shard_map/all_to_all | solution.py:294
  97.7 2.6 %shard_map.115 = (bf16[512,512]{1,0:T(8,128)(2,1)S(1)}, bf16[512,512]{1,0:T(8,128)(2,1)}) custom-call(s32[1]{0:T(128)} %bitcast.core, bf16[256,512]{1,0:T(8,128)(2,1)} %get-tuple-element.95.hid, bf16[256,512]{1,0:T(8,128)(2,1)} %get-tuple-element.96.agg, bf16[256,512]{1,0:T(8,128)(2,1)} %get-tuple-element.97.delta), custom_call_target="tpu_custom_call" | custom-call | flops 268435456 | bytes 2097152 | tf_op jit(solution)/shard_map/pallas_call | solution.py:274
  106.5 3.6 %collective-permute-done.14 = bf16[128,512]{1,0:T(8,128)(2,1)S(1)} collective-permute-done((bf16[128,512]{1,0:T(8,128)(2,1)S(1)}, bf16[128,512]{1,0:T(8,128)(2,1)S(1)}, u32[]{:S(2)}, u32[]{:S(2)}) %collective-permute-start.14) | collective-permute-done | bytes 131104 | tf_op jit(solution)/shard_map/ppermute | solution.py:303
  110.1 4.3 %collective-permute-done.15 = bf16[128,512]{1,0:T(8,128)(2,1)S(1)} collective-permute-done((bf16[128,512]{1,0:T(8,128)(2,1)S(1)}, bf16[128,512]{1,0:T(8,128)(2,1)S(1)}, u32[]{:S(2)}, u32[]{:S(2)}) %collective-permute-start.15) | collective-permute-done | bytes 131104 | tf_op jit(solution)/shard_map/ppermute | solution.py:303
  122.6 3.7 %shard_map.112 = (bf16[256,512]{1,0:T(8,128)(2,1)S(1)}, bf16[512,512]{1,0:T(8,128)(2,1)}, f32[256,512]{1,0:T(8,128)}) custom-call(s32[2,4]{1,0:T(2,128)S(1)} %copy-done, bf16[512,512]{1,0:T(8,128)(2,1)S(1)} %bitcast.16, f32[256,512]{1,0:T(8,128)} %get-tuple-element.84.before, f32[256,512]{1,0:T(8,128)} %get-tuple-element.85.slope, ...), custom_call_target="tpu_custom_call" | custom-call | flops 536870912 | bytes 2621440 | tf_op jit(solution)/shard_map/pallas_call | solution.py:274
  128.2 2.0 %collective-permute-start.18 = (bf16[128,512]{1,0:T(8,128)(2,1)S(1)}, bf16[128,512]{1,0:T(8,128)(2,1)S(1)}, u32[]{:S(2)}, u32[]{:S(2)}) collective-permute-start(bf16[128,512]{1,0:T(8,128)(2,1)S(1)} %add_convert_fusion.2), channel_id=1, source_target_pairs={{0,16},{8,24},{16,0},{24,8},{1,17},{9,25},{17,1},{25,9},{2,18},{10... | collective-permute-start | bytes 393224 | tf_op jit(solution)/shard_map/ppermute | solution.py:319
  131.5 6.4 %collective-permute-done.18 = bf16[128,512]{1,0:T(8,128)(2,1)S(1)} collective-permute-done((bf16[128,512]{1,0:T(8,128)(2,1)S(1)}, bf16[128,512]{1,0:T(8,128)(2,1)S(1)}, u32[]{:S(2)}, u32[]{:S(2)}) %collective-permute-start.18) | collective-permute-done | bytes 131104 | tf_op jit(solution)/shard_map/ppermute | solution.py:319
  141.8 4.0 %all-to-all-start.5 = ((bf16[32,16,512]{2,1,0:T(8,128)(2,1)}), bf16[32,16,512]{2,1,0:T(8,128)(2,1)S(1)}, u32[]{:S(2)}, u32[]{:S(2)}) async-start(bf16[32,16,512]{2,1,0:T(8,128)(2,1)} %bitcast.13), calls=%async_computation.5 | async-start | bytes 1048576 | tf_op jit(solution)/shard_map/all_to_all | solution.py:294
  153.3 7.2 %collective-permute-done.4 = bf16[128,512]{1,0:T(8,128)(2,1)S(1)} collective-permute-done((bf16[128,512]{1,0:T(8,128)(2,1)S(1)}, bf16[128,512]{1,0:T(8,128)(2,1)S(1)}, u32[]{:S(2)}, u32[]{:S(2)}) %collective-permute-start.4) | collective-permute-done | bytes 131104 | tf_op jit(solution)/shard_map/ppermute | solution.py:319
  162.9 4.0 %collective-permute-done.26.refs_2_ = bf16[256,512]{1,0:T(8,128)(2,1)S(1)} collective-permute-done((bf16[256,512]{1,0:T(8,128)(2,1)S(1)}, bf16[256,512]{1,0:T(8,128)(2,1)S(1)}, u32[]{:S(2)}, u32[]{:S(2)}) %collective-permute-start.26) | collective-permute-done | bytes 262176 | tf_op jit(solution)/shard_map/ppermute | solution.py:303
  168.7 2.2 %collective-permute-start.8 = (bf16[128,512]{1,0:T(8,128)(2,1)S(1)}, bf16[128,512]{1,0:T(8,128)(2,1)S(1)}, u32[]{:S(2)}, u32[]{:S(2)}) collective-permute-start(bf16[128,512]{1,0:T(8,128)(2,1)S(1)} %multiply_convert_fusion.2.refs_0_), channel_id=1, source_target_pairs={{0,6},{1,7},{2,4},{3,5},{4,2},{5,3},{6,0},{7,1},{8,14},{9,15},{10,... | collective-permute-start | bytes 393224 | tf_op jit(solution)/shard_map/ppermute | solution.py:303
  172.3 3.7 %collective-permute-done.8.refs_3_ = bf16[128,512]{1,0:T(8,128)(2,1)S(1)} collective-permute-done((bf16[128,512]{1,0:T(8,128)(2,1)S(1)}, bf16[128,512]{1,0:T(8,128)(2,1)S(1)}, u32[]{:S(2)}, u32[]{:S(2)}) %collective-permute-start.8) | collective-permute-done | bytes 131104 | tf_op jit(solution)/shard_map/ppermute | solution.py:303
  (95 shorter events, 47.1 us)
Async XLA Ops:
  2.8 23.0 %all-to-all-start = ((bf16[32,16,512]{2,1,0:T(8,128)(2,1)}), bf16[32,16,512]{2,1,0:T(8,128)(2,1)S(1)}, u32[]{:S(2)}, u32[]{:S(2)}) async-start(bf16[32,16,512]{2,1,0:T(8,128)(2,1)} %bitcast.24), calls=%async_computation | async-start | bytes 1048576 | tf_op jit(solution)/shard_map/all_to_all | solution.py:294
  28.4 18.6 %all-to-all-start.1 = ((bf16[32,16,512]{2,1,0:T(8,128)(2,1)}), bf16[32,16,512]{2,1,0:T(8,128)(2,1)S(1)}, u32[]{:S(2)}, u32[]{:S(2)}) async-start(bf16[32,16,512]{2,1,0:T(8,128)(2,1)} %bitcast.22), calls=%async_computation.1 | async-start | bytes 1048576 | tf_op jit(solution)/shard_map/all_to_all | solution.py:294
  49.6 18.6 %all-to-all-start.2 = ((bf16[32,16,512]{2,1,0:T(8,128)(2,1)}), bf16[32,16,512]{2,1,0:T(8,128)(2,1)S(1)}, u32[]{:S(2)}, u32[]{:S(2)}) async-start(bf16[32,16,512]{2,1,0:T(8,128)(2,1)} %bitcast.23), calls=%async_computation.2 | async-start | bytes 1048576 | tf_op jit(solution)/shard_map/all_to_all | solution.py:294
  94.7 27.9 %all-to-all-start.4 = ((bf16[32,16,512]{2,1,0:T(8,128)(2,1)}), bf16[32,16,512]{2,1,0:T(8,128)(2,1)S(1)}, u32[]{:S(2)}, u32[]{:S(2)}) async-start(bf16[32,16,512]{2,1,0:T(8,128)(2,1)} %bitcast.21), calls=%async_computation.4 | async-start | bytes 1048576 | tf_op jit(solution)/shard_map/all_to_all | solution.py:294
  102.4 16.4 %collective-permute-start.19 = (bf16[512,512]{1,0:T(8,128)(2,1)S(1)}, bf16[512,512]{1,0:T(8,128)(2,1)S(1)}, u32[]{:S(2)}, u32[]{:S(2)}) collective-permute-start(bf16[512,512]{1,0:T(8,128)(2,1)S(1)} %get-tuple-element.108), channel_id=1, source_target_pairs={{0,1},{1,0},{2,3},{3,2},{4,5},{5,4},{6,7},{7,6},{8,9},{9,8},{10,11... | collective-permute-start | bytes 1572872 | tf_op jit(solution)/shard_map/ppermute | solution.py:303
  104.8 9.6 %collective-permute-start.15 = (bf16[128,512]{1,0:T(8,128)(2,1)S(1)}, bf16[128,512]{1,0:T(8,128)(2,1)S(1)}, u32[]{:S(2)}, u32[]{:S(2)}) collective-permute-start(bf16[128,512]{1,0:T(8,128)(2,1)S(1)} %get-tuple-element.102), channel_id=1, source_target_pairs={{0,4},{1,5},{2,6},{3,7},{4,0},{5,1},{6,2},{7,3},{8,12},{9,13},{10,... | collective-permute-start | bytes 393224 | tf_op jit(solution)/shard_map/ppermute | solution.py:303
  106.2 8.2 %collective-permute-start.16 = (bf16[128,512]{1,0:T(8,128)(2,1)S(1)}, bf16[128,512]{1,0:T(8,128)(2,1)S(1)}, u32[]{:S(2)}, u32[]{:S(2)}) collective-permute-start(bf16[128,512]{1,0:T(8,128)(2,1)S(1)} %get-tuple-element.103), channel_id=1, source_target_pairs={{0,6},{1,7},{2,4},{3,5},{4,2},{5,3},{6,0},{7,1},{8,14},{9,15},{10,... | collective-permute-start | bytes 393224 | tf_op jit(solution)/shard_map/ppermute | solution.py:303
  115.1 12.0 %collective-permute-start.17 = (bf16[128,512]{1,0:T(8,128)(2,1)}, bf16[128,512]{1,0:T(8,128)(2,1)}, u32[]{:S(2)}, u32[]{:S(2)}) collective-permute-start(bf16[128,512]{1,0:T(8,128)(2,1)} %add_convert_fusion.3), channel_id=1, source_target_pairs={{0,8},{8,0},{16,24},{24,16},{1,9},{9,1},{17,25},{25,17},{2,10},{10... | collective-permute-start | bytes 393224 | tf_op jit(solution)/shard_map/ppermute | solution.py:319
  119.0 11.2 %collective-permute-start.20 = (bf16[128,512]{1,0:T(8,128)(2,1)S(1)}, bf16[128,512]{1,0:T(8,128)(2,1)S(1)}, u32[]{:S(2)}, u32[]{:S(2)}) collective-permute-start(bf16[128,512]{1,0:T(8,128)(2,1)S(1)} %get-tuple-element.110), channel_id=1, source_target_pairs={{0,2},{1,3},{2,0},{3,1},{4,6},{5,7},{6,4},{7,5},{8,10},{9,11},{10,... | collective-permute-start | bytes 393224 | tf_op jit(solution)/shard_map/ppermute | solution.py:303
  120.2 10.0 %collective-permute-start.21 = (bf16[128,512]{1,0:T(8,128)(2,1)S(1)}, bf16[128,512]{1,0:T(8,128)(2,1)S(1)}, u32[]{:S(2)}, u32[]{:S(2)}) collective-permute-start(bf16[128,512]{1,0:T(8,128)(2,1)S(1)} %get-tuple-element.111), channel_id=1, source_target_pairs={{0,4},{1,5},{2,6},{3,7},{4,0},{5,1},{6,2},{7,3},{8,12},{9,13},{10,... | collective-permute-start | bytes 393224 | tf_op jit(solution)/shard_map/ppermute | solution.py:303
  120.9 9.3 %collective-permute-start.22 = (bf16[128,512]{1,0:T(8,128)(2,1)S(1)}, bf16[128,512]{1,0:T(8,128)(2,1)S(1)}, u32[]{:S(2)}, u32[]{:S(2)}) collective-permute-start(bf16[128,512]{1,0:T(8,128)(2,1)S(1)} %get-tuple-element.112), channel_id=1, source_target_pairs={{0,6},{1,7},{2,4},{3,5},{4,2},{5,3},{6,0},{7,1},{8,14},{9,15},{10,... | collective-permute-start | bytes 393224 | tf_op jit(solution)/shard_map/ppermute | solution.py:303
  127.1 10.8 %collective-permute-start = (bf16[512,512]{1,0:T(8,128)(2,1)S(1)}, bf16[512,512]{1,0:T(8,128)(2,1)S(1)}, u32[]{:S(2)}, u32[]{:S(2)}) collective-permute-start(bf16[512,512]{1,0:T(8,128)(2,1)S(1)} %get-tuple-element.90), channel_id=1, source_target_pairs={{0,1},{1,0},{2,3},{3,2},{4,5},{5,4},{6,7},{7,6},{8,9},{9,8},{10,11... | collective-permute-start | bytes 1572872 | tf_op jit(solution)/shard_map/ppermute | solution.py:303
  128.2 9.7 %collective-permute-start.18 = (bf16[128,512]{1,0:T(8,128)(2,1)S(1)}, bf16[128,512]{1,0:T(8,128)(2,1)S(1)}, u32[]{:S(2)}, u32[]{:S(2)}) collective-permute-start(bf16[128,512]{1,0:T(8,128)(2,1)S(1)} %add_convert_fusion.2), channel_id=1, source_target_pairs={{0,16},{8,24},{16,0},{24,8},{1,17},{9,25},{17,1},{25,9},{2,18},{10... | collective-permute-start | bytes 393224 | tf_op jit(solution)/shard_map/ppermute | solution.py:319
  130.3 11.4 %collective-permute-start.23 = (bf16[128,512]{1,0:T(8,128)(2,1)S(1)}, bf16[128,512]{1,0:T(8,128)(2,1)S(1)}, u32[]{:S(2)}, u32[]{:S(2)}) collective-permute-start(bf16[128,512]{1,0:T(8,128)(2,1)S(1)} %add_convert_fusion.1), channel_id=1, source_target_pairs={{0,8},{8,0},{16,24},{24,16},{1,9},{9,1},{17,25},{25,17},{2,10},{10... | collective-permute-start | bytes 393224 | tf_op jit(solution)/shard_map/ppermute | solution.py:319
  141.8 38.8 %all-to-all-start.5 = ((bf16[32,16,512]{2,1,0:T(8,128)(2,1)}), bf16[32,16,512]{2,1,0:T(8,128)(2,1)S(1)}, u32[]{:S(2)}, u32[]{:S(2)}) async-start(bf16[32,16,512]{2,1,0:T(8,128)(2,1)} %bitcast.13), calls=%async_computation.5 | async-start | bytes 1048576 | tf_op jit(solution)/shard_map/all_to_all | solution.py:294
  147.4 13.1 %collective-permute-start.4 = (bf16[128,512]{1,0:T(8,128)(2,1)S(1)}, bf16[128,512]{1,0:T(8,128)(2,1)S(1)}, u32[]{:S(2)}, u32[]{:S(2)}) collective-permute-start(bf16[128,512]{1,0:T(8,128)(2,1)S(1)} %add_convert_fusion.5), channel_id=1, source_target_pairs={{0,8},{8,0},{16,24},{24,16},{1,9},{9,1},{17,25},{25,17},{2,10},{10... | collective-permute-start | bytes 393224 | tf_op jit(solution)/shard_map/ppermute | solution.py:319
  149.7 12.7 %collective-permute-start.27 = (bf16[256,512]{1,0:T(8,128)(2,1)S(1)}, bf16[256,512]{1,0:T(8,128)(2,1)S(1)}, u32[]{:S(2)}, u32[]{:S(2)}) collective-permute-start(bf16[256,512]{1,0:T(8,128)(2,1)S(1)} %pad_maximum_fusion.refs_0_), channel_id=1, source_target_pairs={{0,6},{1,7},{2,4},{3,5},{4,2},{5,3},{6,0},{7,1},{8,14},{9,15},{10,... | collective-permute-start | bytes 786440 | tf_op jit(solution)/shard_map/ppermute | solution.py:303
  150.7 16.2 %collective-permute-start.26 = (bf16[256,512]{1,0:T(8,128)(2,1)S(1)}, bf16[256,512]{1,0:T(8,128)(2,1)S(1)}, u32[]{:S(2)}, u32[]{:S(2)}) collective-permute-start(bf16[256,512]{1,0:T(8,128)(2,1)S(1)} %pad_maximum_fusion.refs_0_), channel_id=1, source_target_pairs={{0,4},{1,5},{2,6},{3,7},{4,0},{5,1},{6,2},{7,3},{8,12},{9,13},{10,... | collective-permute-start | bytes 786440 | tf_op jit(solution)/shard_map/ppermute | solution.py:303
  152.2 14.8 %collective-permute-start.25 = (bf16[256,512]{1,0:T(8,128)(2,1)S(1)}, bf16[256,512]{1,0:T(8,128)(2,1)S(1)}, u32[]{:S(2)}, u32[]{:S(2)}) collective-permute-start(bf16[256,512]{1,0:T(8,128)(2,1)S(1)} %pad_maximum_fusion.refs_0_), channel_id=1, source_target_pairs={{0,2},{1,3},{2,0},{3,1},{4,6},{5,7},{6,4},{7,5},{8,10},{9,11},{10,... | collective-permute-start | bytes 786440 | tf_op jit(solution)/shard_map/ppermute | solution.py:303
  160.5 8.2 %collective-permute-start.5 = (bf16[128,512]{1,0:T(8,128)(2,1)S(1)}, bf16[128,512]{1,0:T(8,128)(2,1)S(1)}, u32[]{:S(2)}, u32[]{:S(2)}) collective-permute-start(bf16[128,512]{1,0:T(8,128)(2,1)S(1)} %add_convert_fusion.4), channel_id=1, source_target_pairs={{0,16},{8,24},{16,0},{24,8},{1,17},{9,25},{17,1},{25,9},{2,18},{10... | collective-permute-start | bytes 393224 | tf_op jit(solution)/shard_map/ppermute | solution.py:319
  162.4 8.5 %collective-permute-start.28 = (bf16[256,512]{1,0:T(8,128)(2,1)S(1)}, bf16[256,512]{1,0:T(8,128)(2,1)S(1)}, u32[]{:S(2)}, u32[]{:S(2)}) collective-permute-start(bf16[256,512]{1,0:T(8,128)(2,1)S(1)} %pad_maximum_fusion.refs_0_), channel_id=1, source_target_pairs={{0,1},{1,0},{2,3},{3,2},{4,5},{5,4},{6,7},{7,6},{8,9},{9,8},{10,11... | collective-permute-start | bytes 786440 | tf_op jit(solution)/shard_map/ppermute | solution.py:303
  162.4 9.3 %collective-permute-start.31 = (bf16[256,512]{1,0:T(8,128)(2,1)S(1)}, bf16[256,512]{1,0:T(8,128)(2,1)S(1)}, u32[]{:S(2)}, u32[]{:S(2)}) collective-permute-start(bf16[256,512]{1,0:T(8,128)(2,1)S(1)} %collective-permute-done.27.refs_3_), channel_id=1, source_target_pairs={{0,1},{1,0},{2,3},{3,2},{4,5},{5,4},{6,7},{7,6},{8,9},{9,8},{10,11... | collective-permute-start | bytes 786440 | tf_op jit(solution)/shard_map/ppermute | solution.py:303
  167.0 11.5 %collective-permute-start.29 = (bf16[256,512]{1,0:T(8,128)(2,1)S(1)}, bf16[256,512]{1,0:T(8,128)(2,1)S(1)}, u32[]{:S(2)}, u32[]{:S(2)}) collective-permute-start(bf16[256,512]{1,0:T(8,128)(2,1)S(1)} %collective-permute-done.25.refs_1_), channel_id=1, source_target_pairs={{0,1},{1,0},{2,3},{3,2},{4,5},{5,4},{6,7},{7,6},{8,9},{9,8},{10,11... | collective-permute-start | bytes 786440 | tf_op jit(solution)/shard_map/ppermute | solution.py:303
  172.3 10.1 %collective-permute-start.9 = (bf16[128,512]{1,0:T(8,128)(2,1)S(1)}, bf16[128,512]{1,0:T(8,128)(2,1)S(1)}, u32[]{:S(2)}, u32[]{:S(2)}) collective-permute-start(bf16[128,512]{1,0:T(8,128)(2,1)S(1)} %multiply_convert_fusion.2.refs_0_), channel_id=1, source_target_pairs={{0,1},{1,0},{2,3},{3,2},{4,5},{5,4},{6,7},{7,6},{8,9},{9,8},{10,11... | collective-permute-start | bytes 393224 | tf_op jit(solution)/shard_map/ppermute | solution.py:303
  (20 other events, 118.1 us)

commit v5 on v4

--- a/solution.py
+++ b/solution.py
@@ -223,6 +223,15 @@
         out[...] = total.astype(jnp.bfloat16)
 
 
+def add_kernel(scale, *refs):
+    total = refs[0][...].astype(jnp.float32)
+    for ref in refs[1:-2]:
+        total += ref[...].astype(jnp.float32)
+    if scale is not None:
+        total *= scale
+    refs[-2][...] = total.astype(jnp.bfloat16)
+
+
 def place_kernel(layers, count, where, *refs):
     mine, other = refs[:count], refs[count : 2 * count]
     self_out, neigh_out, sems = refs[-3:]
@@ -302,6 +311,17 @@
     def flip(array, mask):
         return lax.ppermute(array, "gy", [(j, j ^ mask) for j in range(inner)])
 
+    def flip_to(m, array):
+        return flip(array, 2 * m)
+
+    def add(*arrays, scaling=None):
+        (total,) = call(
+            functools.partial(add_kernel, scaling),
+            [(a, near) for a in arrays],
+            ((arrays[0].shape, bf16, near),),
+        )
+        return total
+
     def chip_sum(keep, give):
         got = flip(give, 1)
         mine, *others = call(
@@ -309,15 +329,12 @@
             ((chip.reshape(1), scalars), (keep, near), (got, near)),
             (((width // chips, width), bf16, near),) * chips,
         )
-        total = mine.astype(f32)
-        for m, other in enumerate(others, 1):
-            arrival = flip(other, 2 * m)
-            total = total + arrival.astype(f32)
+        total = add(mine, *(flip_to(m, other) for m, other in enumerate(others, 1)))
         for bit in gx_bits:
-            mine = total.astype(bf16)
             perm = [(j, j ^ (1 << bit)) for j in range(outer)]
-            total = mine.astype(f32) + lax.ppermute(mine, "gx", perm).astype(f32)
-        return (total * scale).astype(bf16)
+            got = lax.ppermute(total, "gx", perm)
+            total = add(total, got, scaling=scale if bit == gx_bits[-1] else None)
+        return total
 
     def gather(piece):
         mine, other = [piece], []
@@ -422,10 +439,10 @@
     (grad,) = call(
         final_kernel, ((arrived, near), (base, away), (row, near)), ((*rows, away),), (rows32, rows)
     )
-    mine, other = gather(jnp.concatenate(sums[:-1]))
-    outs = place(tuple(reversed(range(1, layers))), mine, other, ())
-    mine, other = gather(sums[-1])
-    outs = place((0,), mine, other, outs)
+    outs = ()
+    for layer, piece in zip(reversed(range(layers)), sums):
+        mine, other = gather(piece)
+        outs = place((layer,), mine, other, outs)
     return (*outs, grad)
 
 

time: 185 us -> 190 us (1.027)
  Pallas kernels: 34.8 us -> 40 us
  starting transfers between devices: 47.3 us -> 50.5 us
  waiting for transfers between devices: 78.7 us -> 76.6 us
  other arithmetic: 2.15 us -> 0.07 us
    all_to_all x5, waiting for transfers between devices: 42.8 us -> 50.4 us  [exchange(): return lax.all_to_all(sent, AXES, 0, 0, tiled=True).reshape(halo, width)]
    pallas_call x19 -> x29, Pallas kernels: 34.8 us -> 40 us  [call(): pl.pallas_call(body, in_specs=[pl.BlockSpec(memory_space=space) for _, sp...]
    ppermute x6, waiting for transfers between devices: 16.7 us -> 11.8 us  [chip_sum(): got = lax.ppermute(total, 'gx', perm)]
    ppermute x26 -> x33, waiting for transfers between devices: 19.2 us -> 14.4 us  [flip(): return lax.ppermute(array, 'gy', [(j, j ^ mask) for j in range(inner)])]
    ppermute x26 -> x33, starting transfers between devices: 19.9 us -> 22.5 us  [flip(): return lax.ppermute(array, 'gy', [(j, j ^ mask) for j in range(inner)])]
    convert_element_type x9 -> x0, other arithmetic: 2.06 us -> none  [the longest x6 1.93 us: chip_sum(): mine = total.astype(bf16)]
  transfers between devices with their start and end apart: 37 -> 44, of which waited for: 14 -> 17; matrix products, arithmetic and copies ran while one was open for 1% -> 0% of each run, Pallas kernels for 10% -> 13%
where the time goes in v5:
time: 190 us; the launch traced here: 189 us
  waiting for transfers between devices  76.6 us (40%)
  starting transfers between devices  50.5 us (27%)
  Pallas kernels  40 us (21%)
  blocking collectives  18.6 us (10%)
    all_to_all x5, waiting for transfers between devices, exchange(): return lax.all_to_all(sent, AXES, 0, 0, tiled=True).reshape(halo, width)  50.4 us
    pallas_call x29, Pallas kernels, call(): pl.pallas_call(body, in_specs=[pl.BlockSpec(memory_space=space) for _, sp...  40 us
    ppermute x33, starting transfers between devices, flip(): return lax.ppermute(array, 'gy', [(j, j ^ mask) for j in range(inner)])  22.5 us
    all_to_all x5, starting transfers between devices, exchange(): return lax.all_to_all(sent, AXES, 0, 0, tiled=True).reshape(halo, width)  19.4 us
    all_to_all x1, blocking collectives, exchange(): return lax.all_to_all(sent, AXES, 0, 0, tiled=True).reshape(halo, width)  18.6 us
    ppermute x33, waiting for transfers between devices, flip(): return lax.ppermute(array, 'gy', [(j, j ^ mask) for j in range(inner)])  14.4 us
    ppermute x6, waiting for transfers between devices, chip_sum(): got = lax.ppermute(total, 'gx', perm)  11.8 us
    ppermute x6, starting transfers between devices, chip_sum(): got = lax.ppermute(total, 'gx', perm)  8.57 us
  transfers between devices with their start and end apart: 44, of which 17 were waited for; matrix products, arithmetic and copies ran while one was open for 0% of the time, Pallas kernels for 13%

profile of v5, /device:TPU:0, one launch (start us, length us, event | category | flops | bytes accessed | tf_op | source)
XLA Modules:
  0.0 188.8 jit_solution(88092385233549728)
XLA Ops:
  0.6 2.1 %shard_map.104 = (s32[1,512]{1,0:T(1,128)S(1)}, s32[512,1]{1,0:T(8,128)S(1)}, bf16[512,512]{1,0:T(8,128)(2,1)}) custom-call(s32[1,16,32]{2,1,0:T(8,128)} %bitcast.27, s32[1,32]{1,0:T(1,128)} %cnt.1, bf16[256,512]{1,0:T(8,128)(2,1)} %refs_2_.4), custom_call_target="tpu_custom_call" | custom-call | bytes 1056768 | tf_op jit(solution)/shard_map/pallas_call | solution.py:283
  2.8 7.3 %all-to-all-start = ((bf16[32,16,512]{2,1,0:T(8,128)(2,1)}), bf16[32,16,512]{2,1,0:T(8,128)(2,1)S(1)}, u32[]{:S(2)}, u32[]{:S(2)}) async-start(bf16[32,16,512]{2,1,0:T(8,128)(2,1)} %bitcast.25), calls=%async_computation | async-start | bytes 1048576 | tf_op jit(solution)/shard_map/all_to_all | solution.py:303
  11.5 14.2 %all-to-all-done = bf16[32,16,512]{2,1,0:T(8,128)(2,1)S(1)} async-done(((bf16[32,16,512]{2,1,0:T(8,128)(2,1)}), bf16[32,16,512]{2,1,0:T(8,128)(2,1)S(1)}, u32[]{:S(2)}, u32[]{:S(2)}) %all-to-all-start) | async-done | bytes 524320 | tf_op jit(solution)/shard_map/all_to_all | solution.py:303
  25.7 2.6 %shard_map.105 = (bf16[256,512]{1,0:T(8,128)(2,1)}, f32[256,512]{1,0:T(8,128)}, bf16[256,512]{1,0:T(8,128)(2,1)}, bf16[256,512]{1,0:T(8,128)(2,1)S(1)}, bf16[512,512]{1,0:T(8,128)(2,1)}) custom-call(s32[2,4]{1,0:T(2,128)S(1)} %copy-done.2, bf16[256,512]{1,0:T(8,128)(2,1)S(1)} %get-tuple-element.63.hid, bf16[512,512]{1,0:T(8,128)(2,1)S(1)} %bitcast.17, ...), custom_call_target="tpu_custom_call" | custom-call | flops 536870912 | bytes 3670016 | tf_op jit(solution)/shard_map/pallas_call | solution.py:283
  28.4 3.0 %all-to-all-start.1 = ((bf16[32,16,512]{2,1,0:T(8,128)(2,1)}), bf16[32,16,512]{2,1,0:T(8,128)(2,1)S(1)}, u32[]{:S(2)}, u32[]{:S(2)}) async-start(bf16[32,16,512]{2,1,0:T(8,128)(2,1)} %bitcast.23), calls=%async_computation.1 | async-start | bytes 1048576 | tf_op jit(solution)/shard_map/all_to_all | solution.py:303
  32.6 14.4 %all-to-all-done.1 = bf16[32,16,512]{2,1,0:T(8,128)(2,1)S(1)} async-done(((bf16[32,16,512]{2,1,0:T(8,128)(2,1)}), bf16[32,16,512]{2,1,0:T(8,128)(2,1)S(1)}, u32[]{:S(2)}, u32[]{:S(2)}) %all-to-all-start.1) | async-done | bytes 524320 | tf_op jit(solution)/shard_map/all_to_all | solution.py:303
  47.0 2.6 %shard_map.108 = (bf16[256,512]{1,0:T(8,128)(2,1)}, f32[256,512]{1,0:T(8,128)}, bf16[256,512]{1,0:T(8,128)(2,1)}, bf16[256,512]{1,0:T(8,128)(2,1)S(1)}, bf16[512,512]{1,0:T(8,128)(2,1)}) custom-call(s32[2,4]{1,0:T(2,128)S(1)} %copy-done.2, bf16[256,512]{1,0:T(8,128)(2,1)S(1)} %get-tuple-element.72.hid, bf16[512,512]{1,0:T(8,128)(2,1)S(1)} %bitcast.18, ...), custom_call_target="tpu_custom_call" | custom-call | flops 536870912 | bytes 3670016 | tf_op jit(solution)/shard_map/pallas_call | solution.py:283
  49.6 3.0 %all-to-all-start.2 = ((bf16[32,16,512]{2,1,0:T(8,128)(2,1)}), bf16[32,16,512]{2,1,0:T(8,128)(2,1)S(1)}, u32[]{:S(2)}, u32[]{:S(2)}) async-start(bf16[32,16,512]{2,1,0:T(8,128)(2,1)} %bitcast.24), calls=%async_computation.2 | async-start | bytes 1048576 | tf_op jit(solution)/shard_map/all_to_all | solution.py:303
  53.9 14.3 %all-to-all-done.2 = bf16[32,16,512]{2,1,0:T(8,128)(2,1)S(1)} async-done(((bf16[32,16,512]{2,1,0:T(8,128)(2,1)}), bf16[32,16,512]{2,1,0:T(8,128)(2,1)S(1)}, u32[]{:S(2)}, u32[]{:S(2)}) %all-to-all-start.2) | async-done | bytes 524320 | tf_op jit(solution)/shard_map/all_to_all | solution.py:303
  68.2 3.4 %shard_map.110 = (bf16[256,512]{1,0:T(8,128)(2,1)}, bf16[256,512]{1,0:T(8,128)(2,1)}, bf16[512,512]{1,0:T(8,128)(2,1)}, f32[256,512]{1,0:T(8,128)}) custom-call(s32[2,4]{1,0:T(2,128)S(1)} %copy-done.2, bf16[256,512]{1,0:T(8,128)(2,1)S(1)} %get-tuple-element.76.hid, bf16[512,512]{1,0:T(8,128)(2,1)S(1)} %bitcast.20, ...), custom_call_target="tpu_custom_call" | custom-call | flops 1073741824 | bytes 3145728 | tf_op jit(solution)/shard_map/pallas_call | solution.py:283
  71.6 18.6 %all_to_all.30 = bf16[32,16,512]{2,1,0:T(8,128)(2,1)S(1)} all-to-all(bf16[32,16,512]{2,1,0:T(8,128)(2,1)} %bitcast.26), channel_id=1, replica_groups=mesh['gx'=4,'gy'=8] {'gx','gy'}, dimensions={0} | all-to-all | bytes 1048576 | tf_op jit(solution)/shard_map/all_to_all | solution.py:303
  90.2 3.8 %shard_map.111 = (bf16[256,512]{1,0:T(8,128)(2,1)S(1)}, bf16[512,512]{1,0:T(8,128)(2,1)}, f32[256,512]{1,0:T(8,128)}) custom-call(s32[2,4]{1,0:T(2,128)S(1)} %copy-done.2, bf16[512,512]{1,0:T(8,128)(2,1)S(1)} %bitcast.19, f32[256,512]{1,0:T(8,128)} %get-tuple-element.82.before, f32[256,512]{1,0:T(8,128)} %get-tuple-element.83.slope, ...), custom_call_target="tpu_custom_call" | custom-call | flops 536870912 | bytes 2621440 | tf_op jit(solution)/shard_map/pallas_call | solution.py:283
  94.1 3.0 %all-to-all-start.4 = ((bf16[32,16,512]{2,1,0:T(8,128)(2,1)}), bf16[32,16,512]{2,1,0:T(8,128)(2,1)S(1)}, u32[]{:S(2)}, u32[]{:S(2)}) async-start(bf16[32,16,512]{2,1,0:T(8,128)(2,1)} %bitcast.22), calls=%async_computation.4 | async-start | bytes 1048576 | tf_op jit(solution)/shard_map/all_to_all | solution.py:303
  97.0 2.6 %shard_map.123 = (bf16[512,512]{1,0:T(8,128)(2,1)S(1)}, bf16[512,512]{1,0:T(8,128)(2,1)}) custom-call(s32[1]{0:T(128)} %bitcast.core, bf16[256,512]{1,0:T(8,128)(2,1)} %get-tuple-element.106.hid, bf16[256,512]{1,0:T(8,128)(2,1)} %get-tuple-element.107.agg, bf16[256,512]{1,0:T(8,128)(2,1)} %get-tuple-element.108.delta), custom_call_target="tpu_custom_call" | custom-call | flops 268435456 | bytes 2097152 | tf_op jit(solution)/shard_map/pallas_call | solution.py:283
  100.0 2.6 %shard_map.118 = (bf16[512,512]{1,0:T(8,128)(2,1)S(1)}, bf16[512,512]{1,0:T(8,128)(2,1)}) custom-call(s32[1]{0:T(128)} %bitcast.core, bf16[256,512]{1,0:T(8,128)(2,1)} %get-tuple-element.97.hid, bf16[256,512]{1,0:T(8,128)(2,1)} %get-tuple-element.98.agg, bf16[256,512]{1,0:T(8,128)(2,1)S(1)} %get-tuple-element.99.delta), custom_call_target="tpu_custom_call" | custom-call | flops 268435456 | bytes 2097152 | tf_op jit(solution)/shard_map/pallas_call | solution.py:283
  105.1 7.5 %all-to-all-done.4 = bf16[32,16,512]{2,1,0:T(8,128)(2,1)S(1)} async-done(((bf16[32,16,512]{2,1,0:T(8,128)(2,1)}), bf16[32,16,512]{2,1,0:T(8,128)(2,1)S(1)}, u32[]{:S(2)}, u32[]{:S(2)}) %all-to-all-start.4) | async-done | bytes 524320 | tf_op jit(solution)/shard_map/all_to_all | solution.py:303
  113.7 3.8 %shard_map.112 = (bf16[256,512]{1,0:T(8,128)(2,1)S(1)}, bf16[512,512]{1,0:T(8,128)(2,1)}, f32[256,512]{1,0:T(8,128)}) custom-call(s32[2,4]{1,0:T(2,128)S(1)} %copy-done.2, bf16[512,512]{1,0:T(8,128)(2,1)S(1)} %bitcast.16, f32[256,512]{1,0:T(8,128)} %get-tuple-element.86.before, f32[256,512]{1,0:T(8,128)} %get-tuple-element.87.slope, ...), custom_call_target="tpu_custom_call" | custom-call | flops 536870912 | bytes 2621440 | tf_op jit(solution)/shard_map/pallas_call | solution.py:283
  124.4 3.2 %all-to-all-start.5 = ((bf16[32,16,512]{2,1,0:T(8,128)(2,1)}), bf16[32,16,512]{2,1,0:T(8,128)(2,1)S(1)}, u32[]{:S(2)}, u32[]{:S(2)}) async-start(bf16[32,16,512]{2,1,0:T(8,128)(2,1)} %bitcast.21), calls=%async_computation.5 | async-start | bytes 1048576 | tf_op jit(solution)/shard_map/all_to_all | solution.py:303
  135.2 5.3 %collective-permute-done.30.refs_1_ = bf16[128,512]{1,0:T(8,128)(2,1)S(1)} collective-permute-done((bf16[128,512]{1,0:T(8,128)(2,1)S(1)}, bf16[128,512]{1,0:T(8,128)(2,1)S(1)}, u32[]{:S(2)}, u32[]{:S(2)}) %collective-permute-start.30) | collective-permute-done | bytes 131104 | tf_op jit(solution)/shard_map/ppermute | solution.py:335
  140.5 3.5 %collective-permute-start.31 = (bf16[128,512]{1,0:T(8,128)(2,1)S(1)}, bf16[128,512]{1,0:T(8,128)(2,1)S(1)}, u32[]{:S(2)}, u32[]{:S(2)}) collective-permute-start(bf16[128,512]{1,0:T(8,128)(2,1)S(1)} %shard_map.126.refs_0_), channel_id=1, source_target_pairs={{0,16},{8,24},{16,0},{24,8},{1,17},{9,25},{17,1},{25,9},{2,18},{10... | collective-permute-start | bytes 393224 | tf_op jit(solution)/shard_map/ppermute | solution.py:335
  150.2 2.5 %collective-permute-start.34 = (bf16[128,512]{1,0:T(8,128)(2,1)S(1)}, bf16[128,512]{1,0:T(8,128)(2,1)S(1)}, u32[]{:S(2)}, u32[]{:S(2)}) collective-permute-start(bf16[128,512]{1,0:T(8,128)(2,1)S(1)} %shard_map.127.refs_0_), channel_id=1, source_target_pairs={{0,6},{1,7},{2,4},{3,5},{4,2},{5,3},{6,0},{7,1},{8,14},{9,15},{10,... | collective-permute-start | bytes 393224 | tf_op jit(solution)/shard_map/ppermute | solution.py:312
  154.5 2.8 %collective-permute-done.2.refs_2_ = bf16[128,512]{1,0:T(8,128)(2,1)S(1)} collective-permute-done((bf16[128,512]{1,0:T(8,128)(2,1)S(1)}, bf16[128,512]{1,0:T(8,128)(2,1)S(1)}, u32[]{:S(2)}, u32[]{:S(2)}) %collective-permute-start.2) | collective-permute-done | bytes 131104 | tf_op jit(solution)/shard_map/ppermute | solution.py:312
  169.1 2.3 %collective-permute-done.5.refs_1_ = bf16[128,512]{1,0:T(8,128)(2,1)S(1)} collective-permute-done((bf16[128,512]{1,0:T(8,128)(2,1)S(1)}, bf16[128,512]{1,0:T(8,128)(2,1)S(1)}, u32[]{:S(2)}, u32[]{:S(2)}) %collective-permute-start.5) | collective-permute-done | bytes 131104 | tf_op jit(solution)/shard_map/ppermute | solution.py:335
  176.1 3.3 %collective-permute-done.8.refs_3_ = bf16[128,512]{1,0:T(8,128)(2,1)S(1)} collective-permute-done((bf16[128,512]{1,0:T(8,128)(2,1)S(1)}, bf16[128,512]{1,0:T(8,128)(2,1)S(1)}, u32[]{:S(2)}, u32[]{:S(2)}) %collective-permute-start.8) | collective-permute-done | bytes 131104 | tf_op jit(solution)/shard_map/ppermute | solution.py:312
  (101 shorter events, 56.0 us)
Async XLA Ops:
  2.8 22.9 %all-to-all-start = ((bf16[32,16,512]{2,1,0:T(8,128)(2,1)}), bf16[32,16,512]{2,1,0:T(8,128)(2,1)S(1)}, u32[]{:S(2)}, u32[]{:S(2)}) async-start(bf16[32,16,512]{2,1,0:T(8,128)(2,1)} %bitcast.25), calls=%async_computation | async-start | bytes 1048576 | tf_op jit(solution)/shard_map/all_to_all | solution.py:303
  28.4 18.6 %all-to-all-start.1 = ((bf16[32,16,512]{2,1,0:T(8,128)(2,1)}), bf16[32,16,512]{2,1,0:T(8,128)(2,1)S(1)}, u32[]{:S(2)}, u32[]{:S(2)}) async-start(bf16[32,16,512]{2,1,0:T(8,128)(2,1)} %bitcast.23), calls=%async_computation.1 | async-start | bytes 1048576 | tf_op jit(solution)/shard_map/all_to_all | solution.py:303
  49.6 18.6 %all-to-all-start.2 = ((bf16[32,16,512]{2,1,0:T(8,128)(2,1)}), bf16[32,16,512]{2,1,0:T(8,128)(2,1)S(1)}, u32[]{:S(2)}, u32[]{:S(2)}) async-start(bf16[32,16,512]{2,1,0:T(8,128)(2,1)} %bitcast.24), calls=%async_computation.2 | async-start | bytes 1048576 | tf_op jit(solution)/shard_map/all_to_all | solution.py:303
  94.1 18.6 %all-to-all-start.4 = ((bf16[32,16,512]{2,1,0:T(8,128)(2,1)}), bf16[32,16,512]{2,1,0:T(8,128)(2,1)S(1)}, u32[]{:S(2)}, u32[]{:S(2)}) async-start(bf16[32,16,512]{2,1,0:T(8,128)(2,1)} %bitcast.22), calls=%async_computation.4 | async-start | bytes 1048576 | tf_op jit(solution)/shard_map/all_to_all | solution.py:303
  99.7 19.4 %collective-permute-start.26 = (bf16[512,512]{1,0:T(8,128)(2,1)}, bf16[512,512]{1,0:T(8,128)(2,1)}, u32[]{:S(2)}, u32[]{:S(2)}) collective-permute-start(bf16[512,512]{1,0:T(8,128)(2,1)} %get-tuple-element.110), channel_id=1, source_target_pairs={{0,1},{1,0},{2,3},{3,2},{4,5},{5,4},{6,7},{7,6},{8,9},{9,8},{10,11... | collective-permute-start | bytes 1572872 | tf_op jit(solution)/shard_map/ppermute | solution.py:312
  102.6 28.8 %collective-permute-start.13 = (bf16[512,512]{1,0:T(8,128)(2,1)}, bf16[512,512]{1,0:T(8,128)(2,1)S(1)}, u32[]{:S(2)}, u32[]{:S(2)}) collective-permute-start(bf16[512,512]{1,0:T(8,128)(2,1)} %get-tuple-element.101), channel_id=1, source_target_pairs={{0,1},{1,0},{2,3},{3,2},{4,5},{5,4},{6,7},{7,6},{8,9},{9,8},{10,11... | collective-permute-start | bytes 1572872 | tf_op jit(solution)/shard_map/ppermute | solution.py:312
  119.0 25.7 %collective-permute-start = (bf16[512,512]{1,0:T(8,128)(2,1)}, bf16[512,512]{1,0:T(8,128)(2,1)S(1)}, u32[]{:S(2)}, u32[]{:S(2)}) collective-permute-start(bf16[512,512]{1,0:T(8,128)(2,1)} %get-tuple-element.92), channel_id=1, source_target_pairs={{0,1},{1,0},{2,3},{3,2},{4,5},{5,4},{6,7},{7,6},{8,9},{9,8},{10,11... | collective-permute-start | bytes 1572872 | tf_op jit(solution)/shard_map/ppermute | solution.py:312
  124.4 60.6 %all-to-all-start.5 = ((bf16[32,16,512]{2,1,0:T(8,128)(2,1)}), bf16[32,16,512]{2,1,0:T(8,128)(2,1)S(1)}, u32[]{:S(2)}, u32[]{:S(2)}) async-start(bf16[32,16,512]{2,1,0:T(8,128)(2,1)} %bitcast.21), calls=%async_computation.5 | async-start | bytes 1048576 | tf_op jit(solution)/shard_map/all_to_all | solution.py:303
  130.6 9.8 %collective-permute-start.30 = (bf16[128,512]{1,0:T(8,128)(2,1)S(1)}, bf16[128,512]{1,0:T(8,128)(2,1)S(1)}, u32[]{:S(2)}, u32[]{:S(2)}) collective-permute-start(bf16[128,512]{1,0:T(8,128)(2,1)S(1)} %shard_map.125.refs_0_), channel_id=1, source_target_pairs={{0,8},{8,0},{16,24},{24,16},{1,9},{9,1},{17,25},{25,17},{2,10},{10... | collective-permute-start | bytes 393224 | tf_op jit(solution)/shard_map/ppermute | solution.py:335
  131.6 12.4 %collective-permute-start.14 = (bf16[128,512]{1,0:T(8,128)(2,1)S(1)}, bf16[128,512]{1,0:T(8,128)(2,1)S(1)}, u32[]{:S(2)}, u32[]{:S(2)}) collective-permute-start(bf16[128,512]{1,0:T(8,128)(2,1)S(1)} %get-tuple-element.103), channel_id=1, source_target_pairs={{0,2},{1,3},{2,0},{3,1},{4,6},{5,7},{6,4},{7,5},{8,10},{9,11},{10,... | collective-permute-start | bytes 393224 | tf_op jit(solution)/shard_map/ppermute | solution.py:312
  133.1 11.0 %collective-permute-start.15 = (bf16[128,512]{1,0:T(8,128)(2,1)S(1)}, bf16[128,512]{1,0:T(8,128)(2,1)S(1)}, u32[]{:S(2)}, u32[]{:S(2)}) collective-permute-start(bf16[128,512]{1,0:T(8,128)(2,1)S(1)} %get-tuple-element.104), channel_id=1, source_target_pairs={{0,4},{1,5},{2,6},{3,7},{4,0},{5,1},{6,2},{7,3},{8,12},{9,13},{10,... | collective-permute-start | bytes 393224 | tf_op jit(solution)/shard_map/ppermute | solution.py:312
  135.2 8.9 %collective-permute-start.16 = (bf16[128,512]{1,0:T(8,128)(2,1)S(1)}, bf16[128,512]{1,0:T(8,128)(2,1)S(1)}, u32[]{:S(2)}, u32[]{:S(2)}) collective-permute-start(bf16[128,512]{1,0:T(8,128)(2,1)S(1)} %get-tuple-element.105), channel_id=1, source_target_pairs={{0,6},{1,7},{2,4},{3,5},{4,2},{5,3},{6,0},{7,1},{8,14},{9,15},{10,... | collective-permute-start | bytes 393224 | tf_op jit(solution)/shard_map/ppermute | solution.py:312
  140.5 9.7 %collective-permute-start.31 = (bf16[128,512]{1,0:T(8,128)(2,1)S(1)}, bf16[128,512]{1,0:T(8,128)(2,1)S(1)}, u32[]{:S(2)}, u32[]{:S(2)}) collective-permute-start(bf16[128,512]{1,0:T(8,128)(2,1)S(1)} %shard_map.126.refs_0_), channel_id=1, source_target_pairs={{0,16},{8,24},{16,0},{24,8},{1,17},{9,25},{17,1},{25,9},{2,18},{10... | collective-permute-start | bytes 393224 | tf_op jit(solution)/shard_map/ppermute | solution.py:335
  144.2 8.5 %collective-permute-start.17 = (bf16[128,512]{1,0:T(8,128)(2,1)S(1)}, bf16[128,512]{1,0:T(8,128)(2,1)S(1)}, u32[]{:S(2)}, u32[]{:S(2)}) collective-permute-start(bf16[128,512]{1,0:T(8,128)(2,1)S(1)} %shard_map.120.refs_0_), channel_id=1, source_target_pairs={{0,8},{8,0},{16,24},{24,16},{1,9},{9,1},{17,25},{25,17},{2,10},{10... | collective-permute-start | bytes 393224 | tf_op jit(solution)/shard_map/ppermute | solution.py:335
  144.9 8.4 %collective-permute-start.1 = (bf16[128,512]{1,0:T(8,128)(2,1)S(1)}, bf16[128,512]{1,0:T(8,128)(2,1)S(1)}, u32[]{:S(2)}, u32[]{:S(2)}) collective-permute-start(bf16[128,512]{1,0:T(8,128)(2,1)S(1)} %get-tuple-element.94), channel_id=1, source_target_pairs={{0,2},{1,3},{2,0},{3,1},{4,6},{5,7},{6,4},{7,5},{8,10},{9,11},{10,... | collective-permute-start | bytes 393224 | tf_op jit(solution)/shard_map/ppermute | solution.py:312
  146.5 10.8 %collective-permute-start.2 = (bf16[128,512]{1,0:T(8,128)(2,1)S(1)}, bf16[128,512]{1,0:T(8,128)(2,1)S(1)}, u32[]{:S(2)}, u32[]{:S(2)}) collective-permute-start(bf16[128,512]{1,0:T(8,128)(2,1)S(1)} %get-tuple-element.95), channel_id=1, source_target_pairs={{0,4},{1,5},{2,6},{3,7},{4,0},{5,1},{6,2},{7,3},{8,12},{9,13},{10,... | collective-permute-start | bytes 393224 | tf_op jit(solution)/shard_map/ppermute | solution.py:312
  148.0 9.3 %collective-permute-start.3 = (bf16[128,512]{1,0:T(8,128)(2,1)S(1)}, bf16[128,512]{1,0:T(8,128)(2,1)S(1)}, u32[]{:S(2)}, u32[]{:S(2)}) collective-permute-start(bf16[128,512]{1,0:T(8,128)(2,1)S(1)} %get-tuple-element.96), channel_id=1, source_target_pairs={{0,6},{1,7},{2,4},{3,5},{4,2},{5,3},{6,0},{7,1},{8,14},{9,15},{10,... | collective-permute-start | bytes 393224 | tf_op jit(solution)/shard_map/ppermute | solution.py:312
  150.2 9.1 %collective-permute-start.34 = (bf16[128,512]{1,0:T(8,128)(2,1)S(1)}, bf16[128,512]{1,0:T(8,128)(2,1)S(1)}, u32[]{:S(2)}, u32[]{:S(2)}) collective-permute-start(bf16[128,512]{1,0:T(8,128)(2,1)S(1)} %shard_map.127.refs_0_), channel_id=1, source_target_pairs={{0,6},{1,7},{2,4},{3,5},{4,2},{5,3},{6,0},{7,1},{8,14},{9,15},{10,... | collective-permute-start | bytes 393224 | tf_op jit(solution)/shard_map/ppermute | solution.py:312
  163.2 8.3 %collective-permute-start.5 = (bf16[128,512]{1,0:T(8,128)(2,1)S(1)}, bf16[128,512]{1,0:T(8,128)(2,1)S(1)}, u32[]{:S(2)}, u32[]{:S(2)}) collective-permute-start(bf16[128,512]{1,0:T(8,128)(2,1)S(1)} %shard_map.116.refs_0_), channel_id=1, source_target_pairs={{0,16},{8,24},{16,0},{24,8},{1,17},{9,25},{17,1},{25,9},{2,18},{10... | collective-permute-start | bytes 393224 | tf_op jit(solution)/shard_map/ppermute | solution.py:335
  172.1 7.3 %collective-permute-start.8 = (bf16[128,512]{1,0:T(8,128)(2,1)S(1)}, bf16[128,512]{1,0:T(8,128)(2,1)S(1)}, u32[]{:S(2)}, u32[]{:S(2)}) collective-permute-start(bf16[128,512]{1,0:T(8,128)(2,1)S(1)} %shard_map.117.refs_0_), channel_id=1, source_target_pairs={{0,6},{1,7},{2,4},{3,5},{4,2},{5,3},{6,0},{7,1},{8,14},{9,15},{10,... | collective-permute-start | bytes 393224 | tf_op jit(solution)/shard_map/ppermute | solution.py:312
  173.8 7.6 %collective-permute-start.7 = (bf16[128,512]{1,0:T(8,128)(2,1)S(1)}, bf16[128,512]{1,0:T(8,128)(2,1)S(1)}, u32[]{:S(2)}, u32[]{:S(2)}) collective-permute-start(bf16[128,512]{1,0:T(8,128)(2,1)S(1)} %shard_map.117.refs_0_), channel_id=1, source_target_pairs={{0,4},{1,5},{2,6},{3,7},{4,0},{5,1},{6,2},{7,3},{8,12},{9,13},{10,... | collective-permute-start | bytes 393224 | tf_op jit(solution)/shard_map/ppermute | solution.py:312
  175.6 7.9 %collective-permute-start.23 = (bf16[128,512]{1,0:T(8,128)(2,1)S(1)}, bf16[128,512]{1,0:T(8,128)(2,1)S(1)}, u32[]{:S(2)}, u32[]{:S(2)}) collective-permute-start(bf16[128,512]{1,0:T(8,128)(2,1)S(1)} %collective-permute-done.19.refs_1_), channel_id=1, source_target_pairs={{0,1},{1,0},{2,3},{3,2},{4,5},{5,4},{6,7},{7,6},{8,9},{9,8},{10,11... | collective-permute-start | bytes 393224 | tf_op jit(solution)/shard_map/ppermute | solution.py:312
  175.6 11.4 %collective-permute-start.9 = (bf16[128,512]{1,0:T(8,128)(2,1)S(1)}, bf16[128,512]{1,0:T(8,128)(2,1)S(1)}, u32[]{:S(2)}, u32[]{:S(2)}) collective-permute-start(bf16[128,512]{1,0:T(8,128)(2,1)S(1)} %shard_map.117.refs_0_), channel_id=1, source_target_pairs={{0,1},{1,0},{2,3},{3,2},{4,5},{5,4},{6,7},{7,6},{8,9},{9,8},{10,11... | collective-permute-start | bytes 393224 | tf_op jit(solution)/shard_map/ppermute | solution.py:312
  179.4 7.6 %collective-permute-start.12 = (bf16[128,512]{1,0:T(8,128)(2,1)S(1)}, bf16[128,512]{1,0:T(8,128)(2,1)S(1)}, u32[]{:S(2)}, u32[]{:S(2)}) collective-permute-start(bf16[128,512]{1,0:T(8,128)(2,1)S(1)} %collective-permute-done.8.refs_3_), channel_id=1, source_target_pairs={{0,1},{1,0},{2,3},{3,2},{4,5},{5,4},{6,7},{7,6},{8,9},{9,8},{10,11... | collective-permute-start | bytes 393224 | tf_op jit(solution)/shard_map/ppermute | solution.py:312
  (23 other events, 138.1 us)

commit v6 on v5

--- a/solution.py
+++ b/solution.py
@@ -184,6 +184,22 @@
     go.finish()
 
 
+def top_kernel(
+    core, hid, agg, arr, before, slope, row, delta_out, keep, give, before_v, slope_v, sems
+):
+    go = Copies(sems)
+    loads = [go.start(before, before_v), go.start(slope, slope_v)]
+    delta = delta_of(loads, arr, row, before_v, slope_v)
+    delta_out[...] = delta
+    products(core[0], hid, agg, delta, (give, keep))
+
+
+def spread_kernel(cols, delta, val, ws, wn, halo_out, base_out, halo_v, base_v, acc_v, sems):
+    go = Copies(sems)
+    spread_back(go, delta[...], cols, val, ws, wn, halo_out, base_out, halo_v, base_v, acc_v)
+    go.finish()
+
+
 def final_kernel(arr, before, row, grad_out, before_v, grad_v, sems):
     go = Copies(sems)
     load = go.start(before, before_v)
@@ -209,10 +225,6 @@
     for load in loads:
         load.wait()
     products(core[0], hid_v, agg_v, delta_v[...], (give, keep))
-
-
-def near_weight_kernel(core, hid, agg, delta, keep, give, sems):
-    products(core[0], hid, agg, delta[...], (give, keep))
 
 
 def quarters_kernel(chip, keep, got, *outs):
@@ -408,32 +420,47 @@
     for layer in reversed(range(layers)):
         below = layer - 1
         if layer:
-            sources = ((hiddens[layer], away), (aggregates[layer], away), (delta, delta_at))
-        else:
-            sources = ((hid, near), (agg, near), (delta, near))
-        keep, give = call(
-            weight_kernel if layer else near_weight_kernel,
-            ((core_arg, scalars), *sources),
-            ((*square, near), (*square, near)),
-            (rows, rows, rows) if layer else (),
-            flops=big // 2,
-        )
+            keep, give = call(
+                weight_kernel,
+                (
+                    (core_arg, scalars), (hiddens[layer], away), (aggregates[layer], away),
+                    (delta, delta_at),
+                ),
+                ((*square, near), (*square, near)),
+                (rows, rows, rows),
+                flops=big // 2,
+            )
         sums.append(chip_sum(keep, give))
         arrived = exchange(outgoing)
-        if layer:
-            last = (hiddens[0], aggregates[0]) if below == 0 else ()
-            ws, wn, *more = load(below, *last)
-            if more:
-                hid, agg = more
-            delta_at = near
+        if not layer:
+            break
+        last = (hiddens[0], aggregates[0]) if below == 0 else ()
+        ws, wn, *more = load(below, *last)
+        back = ((arrived, near), (base, away), (slopes[below], away), (row, near))
+        graph = ((val, near), (ws, near), (wn, near))
+        delta_at = near
+        if below:
             delta, outgoing, base = call(
                 backward_kernel,
-                (
-                    cols, (arrived, near), (base, away), (slopes[below], away), (row, near),
-                    (val, near), (ws, near), (wn, near),
-                ),
+                (cols, *back, *graph),
                 ((*rows, near), (*halo_rows, away), (*rows32, away)),
                 (rows32, rows32, halo_rows, rows32, acc),
+                flops=big,
+            )
+        else:
+            delta, keep, give = call(
+                top_kernel,
+                ((core_arg, scalars), *((a, near) for a in more), *back),
+                ((*rows, near), (*square, near), (*square, near)),
+                (rows32, rows32),
+                flops=big,
+            )
+        if not below:
+            outgoing, base = call(
+                spread_kernel,
+                (cols, (delta, near), *graph),
+                ((*halo_rows, away), (*rows32, away)),
+                (halo_rows, rows32, acc),
                 flops=big,
             )
     (grad,) = call(

time: 190 us -> 192 us (1.011)
  local copies, waits for them, and re-layouts: 1.84 us -> 5.32 us
    unnamed x6 -> x14, local copies, waits for them, and re-layouts: 1.84 us -> 5.32 us
    ppermute x33, waiting for transfers between devices: 14.4 us -> 11.5 us  [flip(): return lax.ppermute(array, 'gy', [(j, j ^ mask) for j in range(inner)])]
    ppermute x6, waiting for transfers between devices: 11.8 us -> 14.2 us  [chip_sum(): got = lax.ppermute(total, 'gx', perm)]
  transfers between devices with their start and end apart: 44 -> 44, of which waited for: 17 -> 15; matrix products, arithmetic and copies ran while one was open for 0% -> 0% of each run, Pallas kernels for 13% -> 12%
where the time goes in v6:
time: 192 us; the launch traced here: 191 us
  waiting for transfers between devices  75.3 us (39%)
  starting transfers between devices  50.8 us (26%)
  Pallas kernels  40.1 us (21%)
  blocking collectives  18.6 us (10%)
  local copies, waits for them, and re-layouts  5.32 us (3%)
    all_to_all x5, waiting for transfers between devices, exchange(): return lax.all_to_all(sent, AXES, 0, 0, tiled=True).reshape(halo, width)  49.5 us
    pallas_call x29, Pallas kernels, call(): pl.pallas_call(body, in_specs=[pl.BlockSpec(memory_space=space) for _, sp...  40.1 us
    ppermute x33, starting transfers between devices, flip(): return lax.ppermute(array, 'gy', [(j, j ^ mask) for j in range(inner)])  22.4 us
    all_to_all x5, starting transfers between devices, exchange(): return lax.all_to_all(sent, AXES, 0, 0, tiled=True).reshape(halo, width)  19.4 us
    all_to_all x1, blocking collectives, exchange(): return lax.all_to_all(sent, AXES, 0, 0, tiled=True).reshape(halo, width)  18.6 us
    ppermute x6, waiting for transfers between devices, chip_sum(): got = lax.ppermute(total, 'gx', perm)  14.2 us
    ppermute x33, waiting for transfers between devices, flip(): return lax.ppermute(array, 'gy', [(j, j ^ mask) for j in range(inner)])  11.5 us
    ppermute x6, starting transfers between devices, chip_sum(): got = lax.ppermute(total, 'gx', perm)  9.01 us
  transfers between devices with their start and end apart: 44, of which 15 were waited for; matrix products, arithmetic and copies ran while one was open for 0% of the time, Pallas kernels for 12%

profile of v6, /device:TPU:0, one launch (start us, length us, event | category | flops | bytes accessed | tf_op | source)
XLA Modules:
  0.0 191.4 jit_solution(14729290337471459878)
XLA Ops:
  2.8 7.3 %all-to-all-start = ((bf16[32,16,512]{2,1,0:T(8,128)(2,1)}), bf16[32,16,512]{2,1,0:T(8,128)(2,1)S(1)}, u32[]{:S(2)}, u32[]{:S(2)}) async-start(bf16[32,16,512]{2,1,0:T(8,128)(2,1)} %bitcast.25), calls=%async_computation | async-start | bytes 1048576 | tf_op jit(solution)/shard_map/all_to_all | solution.py:315
  11.5 14.2 %all-to-all-done = bf16[32,16,512]{2,1,0:T(8,128)(2,1)S(1)} async-done(((bf16[32,16,512]{2,1,0:T(8,128)(2,1)}), bf16[32,16,512]{2,1,0:T(8,128)(2,1)S(1)}, u32[]{:S(2)}, u32[]{:S(2)}) %all-to-all-start) | async-done | bytes 524320 | tf_op jit(solution)/shard_map/all_to_all | solution.py:315
  25.7 2.6 %shard_map.105 = (bf16[256,512]{1,0:T(8,128)(2,1)}, f32[256,512]{1,0:T(8,128)}, bf16[256,512]{1,0:T(8,128)(2,1)}, bf16[256,512]{1,0:T(8,128)(2,1)S(1)}, bf16[512,512]{1,0:T(8,128)(2,1)}) custom-call(s32[2,4]{1,0:T(2,128)S(1)} %copy-done, bf16[256,512]{1,0:T(8,128)(2,1)S(1)} %get-tuple-element.63.hid, bf16[512,512]{1,0:T(8,128)(2,1)S(1)} %bitcast.17, ...), custom_call_target="tpu_custom_call" | custom-call | flops 536870912 | bytes 3670016 | tf_op jit(solution)/shard_map/pallas_call | solution.py:295
  28.4 3.0 %all-to-all-start.1 = ((bf16[32,16,512]{2,1,0:T(8,128)(2,1)}), bf16[32,16,512]{2,1,0:T(8,128)(2,1)S(1)}, u32[]{:S(2)}, u32[]{:S(2)}) async-start(bf16[32,16,512]{2,1,0:T(8,128)(2,1)} %bitcast.23), calls=%async_computation.1 | async-start | bytes 1048576 | tf_op jit(solution)/shard_map/all_to_all | solution.py:315
  32.6 14.4 %all-to-all-done.1 = bf16[32,16,512]{2,1,0:T(8,128)(2,1)S(1)} async-done(((bf16[32,16,512]{2,1,0:T(8,128)(2,1)}), bf16[32,16,512]{2,1,0:T(8,128)(2,1)S(1)}, u32[]{:S(2)}, u32[]{:S(2)}) %all-to-all-start.1) | async-done | bytes 524320 | tf_op jit(solution)/shard_map/all_to_all | solution.py:315
  47.0 2.7 %shard_map.108 = (bf16[256,512]{1,0:T(8,128)(2,1)}, f32[256,512]{1,0:T(8,128)}, bf16[256,512]{1,0:T(8,128)(2,1)}, bf16[256,512]{1,0:T(8,128)(2,1)S(1)}, bf16[512,512]{1,0:T(8,128)(2,1)}) custom-call(s32[2,4]{1,0:T(2,128)S(1)} %copy-done, bf16[256,512]{1,0:T(8,128)(2,1)S(1)} %get-tuple-element.72.hid, bf16[512,512]{1,0:T(8,128)(2,1)S(1)} %bitcast.18, ...), custom_call_target="tpu_custom_call" | custom-call | flops 536870912 | bytes 3670016 | tf_op jit(solution)/shard_map/pallas_call | solution.py:295
  49.7 3.0 %all-to-all-start.2 = ((bf16[32,16,512]{2,1,0:T(8,128)(2,1)}), bf16[32,16,512]{2,1,0:T(8,128)(2,1)S(1)}, u32[]{:S(2)}, u32[]{:S(2)}) async-start(bf16[32,16,512]{2,1,0:T(8,128)(2,1)} %bitcast.24), calls=%async_computation.2 | async-start | bytes 1048576 | tf_op jit(solution)/shard_map/all_to_all | solution.py:315
  54.0 14.3 %all-to-all-done.2 = bf16[32,16,512]{2,1,0:T(8,128)(2,1)S(1)} async-done(((bf16[32,16,512]{2,1,0:T(8,128)(2,1)}), bf16[32,16,512]{2,1,0:T(8,128)(2,1)S(1)}, u32[]{:S(2)}, u32[]{:S(2)}) %all-to-all-start.2) | async-done | bytes 524320 | tf_op jit(solution)/shard_map/all_to_all | solution.py:315
  68.2 3.4 %shard_map.110 = (bf16[256,512]{1,0:T(8,128)(2,1)}, bf16[256,512]{1,0:T(8,128)(2,1)}, bf16[512,512]{1,0:T(8,128)(2,1)}, f32[256,512]{1,0:T(8,128)}) custom-call(s32[2,4]{1,0:T(2,128)S(1)} %copy-done, bf16[256,512]{1,0:T(8,128)(2,1)S(1)} %get-tuple-element.76.hid, bf16[512,512]{1,0:T(8,128)(2,1)S(1)} %bitcast.20, ...), custom_call_target="tpu_custom_call" | custom-call | flops 1073741824 | bytes 3145728 | tf_op jit(solution)/shard_map/pallas_call | solution.py:295
  71.6 18.6 %all_to_all.30 = bf16[32,16,512]{2,1,0:T(8,128)(2,1)S(1)} all-to-all(bf16[32,16,512]{2,1,0:T(8,128)(2,1)} %bitcast.26), channel_id=1, replica_groups=mesh['gx'=4,'gy'=8] {'gx','gy'}, dimensions={0} | all-to-all | bytes 1048576 | tf_op jit(solution)/shard_map/all_to_all | solution.py:315
  90.2 3.8 %shard_map.111 = (bf16[256,512]{1,0:T(8,128)(2,1)S(1)}, bf16[512,512]{1,0:T(8,128)(2,1)}, f32[256,512]{1,0:T(8,128)}) custom-call(s32[2,4]{1,0:T(2,128)S(1)} %copy-done, bf16[512,512]{1,0:T(8,128)(2,1)S(1)} %bitcast.19, f32[256,512]{1,0:T(8,128)} %get-tuple-element.82.before, f32[256,512]{1,0:T(8,128)} %get-tuple-element.83.slope, ...), custom_call_target="tpu_custom_call" | custom-call | flops 536870912 | bytes 2621440 | tf_op jit(solution)/shard_map/pallas_call | solution.py:295
  94.0 3.0 %all-to-all-start.4 = ((bf16[32,16,512]{2,1,0:T(8,128)(2,1)}), bf16[32,16,512]{2,1,0:T(8,128)(2,1)S(1)}, u32[]{:S(2)}, u32[]{:S(2)}) async-start(bf16[32,16,512]{2,1,0:T(8,128)(2,1)} %bitcast.22), calls=%async_computation.4 | async-start | bytes 1048576 | tf_op jit(solution)/shard_map/all_to_all | solution.py:315
  97.0 2.6 %shard_map.122 = (bf16[512,512]{1,0:T(8,128)(2,1)S(1)}, bf16[512,512]{1,0:T(8,128)(2,1)}) custom-call(s32[1]{0:T(128)} %bitcast.core, bf16[256,512]{1,0:T(8,128)(2,1)} %get-tuple-element.103.hid, bf16[256,512]{1,0:T(8,128)(2,1)} %get-tuple-element.104.agg, bf16[256,512]{1,0:T(8,128)(2,1)} %get-tuple-element.105.delta), custom_call_target="tpu_custom_call" | custom-call | flops 268435456 | bytes 2097152 | tf_op jit(solution)/shard_map/pallas_call | solution.py:295
  99.9 2.6 %shard_map.117 = (bf16[512,512]{1,0:T(8,128)(2,1)S(1)}, bf16[512,512]{1,0:T(8,128)(2,1)}) custom-call(s32[1]{0:T(128)} %bitcast.core, bf16[256,512]{1,0:T(8,128)(2,1)} %get-tuple-element.94.hid, bf16[256,512]{1,0:T(8,128)(2,1)} %get-tuple-element.95.agg, bf16[256,512]{1,0:T(8,128)(2,1)S(1)} %get-tuple-element.96.delta), custom_call_target="tpu_custom_call" | custom-call | flops 268435456 | bytes 2097152 | tf_op jit(solution)/shard_map/pallas_call | solution.py:295
  105.9 6.7 %all-to-all-done.4 = bf16[32,16,512]{2,1,0:T(8,128)(2,1)S(1)} async-done(((bf16[32,16,512]{2,1,0:T(8,128)(2,1)}), bf16[32,16,512]{2,1,0:T(8,128)(2,1)S(1)}, u32[]{:S(2)}, u32[]{:S(2)}) %all-to-all-start.4) | async-done | bytes 524320 | tf_op jit(solution)/shard_map/all_to_all | solution.py:315
  112.6 2.9 %shard_map.112 = (bf16[256,512]{1,0:T(8,128)(2,1)S(1)}, bf16[512,512]{1,0:T(8,128)(2,1)S(1)}, bf16[512,512]{1,0:T(8,128)(2,1)}) custom-call(s32[1]{0:T(128)} %bitcast.core, bf16[256,512]{1,0:T(8,128)(2,1)S(1)} %get-tuple-element.70.hid, bf16[256,512]{1,0:T(8,128)(2,1)S(1)} %get-tuple-element.71.agg, bf16[512,512]{1,0:T(8,128)(2,1)S(1)} %bitcast.16, ...), custom_call_target="tpu_custom_call" | custom-call | flops 536870912 | bytes 2621440 | tf_op jit(solution)/shard_map/pallas_call | solution.py:295
  124.7 2.4 %shard_map.130 = (bf16[512,512]{1,0:T(8,128)(2,1)}, f32[256,512]{1,0:T(8,128)}) custom-call(s32[2,4]{1,0:T(2,128)S(1)} %copy-done, bf16[256,512]{1,0:T(8,128)(2,1)S(1)} %copy-done.6, bf16[2,4,128,128]{3,2,1,0:T(8,128)(2,1)S(1)} %get-tuple-element.65.val, bf16[512,512]{1,0:T(8,128)(2,1)S(1)} %copy-done.2, bf16[512,512]{1,0:T(8,128)(2,1)S(1)} %copy-done.4), custom_call_target="tpu_custom_call" | custom-call | flops 536870912 | bytes 2097152 | tf_op jit(solution)/shard_map/pallas_call | solution.py:295
  127.1 3.2 %all-to-all-start.5 = ((bf16[32,16,512]{2,1,0:T(8,128)(2,1)}), bf16[32,16,512]{2,1,0:T(8,128)(2,1)S(1)}, u32[]{:S(2)}, u32[]{:S(2)}) async-start(bf16[32,16,512]{2,1,0:T(8,128)(2,1)} %bitcast.21), calls=%async_computation.5 | async-start | bytes 1048576 | tf_op jit(solution)/shard_map/all_to_all | solution.py:315
  135.8 7.3 %collective-permute-done.30.refs_1_ = bf16[128,512]{1,0:T(8,128)(2,1)S(1)} collective-permute-done((bf16[128,512]{1,0:T(8,128)(2,1)S(1)}, bf16[128,512]{1,0:T(8,128)(2,1)S(1)}, u32[]{:S(2)}, u32[]{:S(2)}) %collective-permute-start.30) | collective-permute-done | bytes 131104 | tf_op jit(solution)/shard_map/ppermute | solution.py:347
  143.2 3.5 %collective-permute-start.31 = (bf16[128,512]{1,0:T(8,128)(2,1)S(1)}, bf16[128,512]{1,0:T(8,128)(2,1)S(1)}, u32[]{:S(2)}, u32[]{:S(2)}) collective-permute-start(bf16[128,512]{1,0:T(8,128)(2,1)S(1)} %shard_map.125.refs_0_), channel_id=1, source_target_pairs={{0,16},{8,24},{16,0},{24,8},{1,17},{9,25},{17,1},{25,9},{2,18},{10... | collective-permute-start | bytes 393224 | tf_op jit(solution)/shard_map/ppermute | solution.py:347
  152.9 2.5 %collective-permute-start.34 = (bf16[128,512]{1,0:T(8,128)(2,1)S(1)}, bf16[128,512]{1,0:T(8,128)(2,1)S(1)}, u32[]{:S(2)}, u32[]{:S(2)}) collective-permute-start(bf16[128,512]{1,0:T(8,128)(2,1)S(1)} %shard_map.126.refs_0_), channel_id=1, source_target_pairs={{0,6},{1,7},{2,4},{3,5},{4,2},{5,3},{6,0},{7,1},{8,14},{9,15},{10,... | collective-permute-start | bytes 393224 | tf_op jit(solution)/shard_map/ppermute | solution.py:324
  157.2 2.8 %collective-permute-done.2.refs_2_ = bf16[128,512]{1,0:T(8,128)(2,1)S(1)} collective-permute-done((bf16[128,512]{1,0:T(8,128)(2,1)S(1)}, bf16[128,512]{1,0:T(8,128)(2,1)S(1)}, u32[]{:S(2)}, u32[]{:S(2)}) %collective-permute-start.2) | collective-permute-done | bytes 131104 | tf_op jit(solution)/shard_map/ppermute | solution.py:324
  171.8 2.3 %collective-permute-done.5.refs_1_ = bf16[128,512]{1,0:T(8,128)(2,1)S(1)} collective-permute-done((bf16[128,512]{1,0:T(8,128)(2,1)S(1)}, bf16[128,512]{1,0:T(8,128)(2,1)S(1)}, u32[]{:S(2)}, u32[]{:S(2)}) %collective-permute-start.5) | collective-permute-done | bytes 131104 | tf_op jit(solution)/shard_map/ppermute | solution.py:347
  178.8 3.3 %collective-permute-done.8.refs_3_ = bf16[128,512]{1,0:T(8,128)(2,1)S(1)} collective-permute-done((bf16[128,512]{1,0:T(8,128)(2,1)S(1)}, bf16[128,512]{1,0:T(8,128)(2,1)S(1)}, u32[]{:S(2)}, u32[]{:S(2)}) %collective-permute-start.8) | collective-permute-done | bytes 131104 | tf_op jit(solution)/shard_map/ppermute | solution.py:324
  (109 shorter events, 58.0 us)
Async XLA Ops:
  2.8 22.9 %all-to-all-start = ((bf16[32,16,512]{2,1,0:T(8,128)(2,1)}), bf16[32,16,512]{2,1,0:T(8,128)(2,1)S(1)}, u32[]{:S(2)}, u32[]{:S(2)}) async-start(bf16[32,16,512]{2,1,0:T(8,128)(2,1)} %bitcast.25), calls=%async_computation | async-start | bytes 1048576 | tf_op jit(solution)/shard_map/all_to_all | solution.py:315
  28.4 18.6 %all-to-all-start.1 = ((bf16[32,16,512]{2,1,0:T(8,128)(2,1)}), bf16[32,16,512]{2,1,0:T(8,128)(2,1)S(1)}, u32[]{:S(2)}, u32[]{:S(2)}) async-start(bf16[32,16,512]{2,1,0:T(8,128)(2,1)} %bitcast.23), calls=%async_computation.1 | async-start | bytes 1048576 | tf_op jit(solution)/shard_map/all_to_all | solution.py:315
  49.7 18.6 %all-to-all-start.2 = ((bf16[32,16,512]{2,1,0:T(8,128)(2,1)}), bf16[32,16,512]{2,1,0:T(8,128)(2,1)S(1)}, u32[]{:S(2)}, u32[]{:S(2)}) async-start(bf16[32,16,512]{2,1,0:T(8,128)(2,1)} %bitcast.24), calls=%async_computation.2 | async-start | bytes 1048576 | tf_op jit(solution)/shard_map/all_to_all | solution.py:315
  94.0 18.6 %all-to-all-start.4 = ((bf16[32,16,512]{2,1,0:T(8,128)(2,1)}), bf16[32,16,512]{2,1,0:T(8,128)(2,1)S(1)}, u32[]{:S(2)}, u32[]{:S(2)}) async-start(bf16[32,16,512]{2,1,0:T(8,128)(2,1)} %bitcast.22), calls=%async_computation.4 | async-start | bytes 1048576 | tf_op jit(solution)/shard_map/all_to_all | solution.py:315
  99.6 16.6 %collective-permute-start.26 = (bf16[512,512]{1,0:T(8,128)(2,1)}, bf16[512,512]{1,0:T(8,128)(2,1)}, u32[]{:S(2)}, u32[]{:S(2)}) collective-permute-start(bf16[512,512]{1,0:T(8,128)(2,1)} %get-tuple-element.107), channel_id=1, source_target_pairs={{0,1},{1,0},{2,3},{3,2},{4,5},{5,4},{6,7},{7,6},{8,9},{9,8},{10,11... | collective-permute-start | bytes 1572872 | tf_op jit(solution)/shard_map/ppermute | solution.py:324
  102.5 29.5 %collective-permute-start.13 = (bf16[512,512]{1,0:T(8,128)(2,1)}, bf16[512,512]{1,0:T(8,128)(2,1)S(1)}, u32[]{:S(2)}, u32[]{:S(2)}) collective-permute-start(bf16[512,512]{1,0:T(8,128)(2,1)} %get-tuple-element.98), channel_id=1, source_target_pairs={{0,1},{1,0},{2,3},{3,2},{4,5},{5,4},{6,7},{7,6},{8,9},{9,8},{10,11... | collective-permute-start | bytes 1572872 | tf_op jit(solution)/shard_map/ppermute | solution.py:324
  116.2 30.7 %collective-permute-start = (bf16[512,512]{1,0:T(8,128)(2,1)}, bf16[512,512]{1,0:T(8,128)(2,1)S(1)}, u32[]{:S(2)}, u32[]{:S(2)}) collective-permute-start(bf16[512,512]{1,0:T(8,128)(2,1)} %get-tuple-element.89), channel_id=1, source_target_pairs={{0,1},{1,0},{2,3},{3,2},{4,5},{5,4},{6,7},{7,6},{8,9},{9,8},{10,11... | collective-permute-start | bytes 1572872 | tf_op jit(solution)/shard_map/ppermute | solution.py:324
  118.1 12.2 %collective-permute-start.27 = (bf16[128,512]{1,0:T(8,128)(2,1)}, bf16[128,512]{1,0:T(8,128)(2,1)S(1)}, u32[]{:S(2)}, u32[]{:S(2)}) collective-permute-start(bf16[128,512]{1,0:T(8,128)(2,1)} %get-tuple-element.109), channel_id=1, source_target_pairs={{0,2},{1,3},{2,0},{3,1},{4,6},{5,7},{6,4},{7,5},{8,10},{9,11},{10,... | collective-permute-start | bytes 393224 | tf_op jit(solution)/shard_map/ppermute | solution.py:324
  119.4 10.9 %collective-permute-start.28 = (bf16[128,512]{1,0:T(8,128)(2,1)}, bf16[128,512]{1,0:T(8,128)(2,1)S(1)}, u32[]{:S(2)}, u32[]{:S(2)}) collective-permute-start(bf16[128,512]{1,0:T(8,128)(2,1)} %get-tuple-element.110), channel_id=1, source_target_pairs={{0,4},{1,5},{2,6},{3,7},{4,0},{5,1},{6,2},{7,3},{8,12},{9,13},{10,... | collective-permute-start | bytes 393224 | tf_op jit(solution)/shard_map/ppermute | solution.py:324
  120.4 9.8 %collective-permute-start.29 = (bf16[128,512]{1,0:T(8,128)(2,1)S(1)}, bf16[128,512]{1,0:T(8,128)(2,1)S(1)}, u32[]{:S(2)}, u32[]{:S(2)}) collective-permute-start(bf16[128,512]{1,0:T(8,128)(2,1)S(1)} %get-tuple-element.111), channel_id=1, source_target_pairs={{0,6},{1,7},{2,4},{3,5},{4,2},{5,3},{6,0},{7,1},{8,14},{9,15},{10,... | collective-permute-start | bytes 393224 | tf_op jit(solution)/shard_map/ppermute | solution.py:324
  127.1 60.7 %all-to-all-start.5 = ((bf16[32,16,512]{2,1,0:T(8,128)(2,1)}), bf16[32,16,512]{2,1,0:T(8,128)(2,1)S(1)}, u32[]{:S(2)}, u32[]{:S(2)}) async-start(bf16[32,16,512]{2,1,0:T(8,128)(2,1)} %bitcast.21), calls=%async_computation.5 | async-start | bytes 1048576 | tf_op jit(solution)/shard_map/all_to_all | solution.py:315
  130.4 12.7 %collective-permute-start.30 = (bf16[128,512]{1,0:T(8,128)(2,1)S(1)}, bf16[128,512]{1,0:T(8,128)(2,1)S(1)}, u32[]{:S(2)}, u32[]{:S(2)}) collective-permute-start(bf16[128,512]{1,0:T(8,128)(2,1)S(1)} %shard_map.124.refs_0_), channel_id=1, source_target_pairs={{0,8},{8,0},{16,24},{24,16},{1,9},{9,1},{17,25},{25,17},{2,10},{10... | collective-permute-start | bytes 393224 | tf_op jit(solution)/shard_map/ppermute | solution.py:347
  132.3 14.4 %collective-permute-start.14 = (bf16[128,512]{1,0:T(8,128)(2,1)S(1)}, bf16[128,512]{1,0:T(8,128)(2,1)S(1)}, u32[]{:S(2)}, u32[]{:S(2)}) collective-permute-start(bf16[128,512]{1,0:T(8,128)(2,1)S(1)} %get-tuple-element.100), channel_id=1, source_target_pairs={{0,2},{1,3},{2,0},{3,1},{4,6},{5,7},{6,4},{7,5},{8,10},{9,11},{10,... | collective-permute-start | bytes 393224 | tf_op jit(solution)/shard_map/ppermute | solution.py:324
  133.8 12.9 %collective-permute-start.15 = (bf16[128,512]{1,0:T(8,128)(2,1)S(1)}, bf16[128,512]{1,0:T(8,128)(2,1)S(1)}, u32[]{:S(2)}, u32[]{:S(2)}) collective-permute-start(bf16[128,512]{1,0:T(8,128)(2,1)S(1)} %get-tuple-element.101), channel_id=1, source_target_pairs={{0,4},{1,5},{2,6},{3,7},{4,0},{5,1},{6,2},{7,3},{8,12},{9,13},{10,... | collective-permute-start | bytes 393224 | tf_op jit(solution)/shard_map/ppermute | solution.py:324
  135.3 11.4 %collective-permute-start.16 = (bf16[128,512]{1,0:T(8,128)(2,1)S(1)}, bf16[128,512]{1,0:T(8,128)(2,1)S(1)}, u32[]{:S(2)}, u32[]{:S(2)}) collective-permute-start(bf16[128,512]{1,0:T(8,128)(2,1)S(1)} %get-tuple-element.102), channel_id=1, source_target_pairs={{0,6},{1,7},{2,4},{3,5},{4,2},{5,3},{6,0},{7,1},{8,14},{9,15},{10,... | collective-permute-start | bytes 393224 | tf_op jit(solution)/shard_map/ppermute | solution.py:324
  143.2 9.7 %collective-permute-start.31 = (bf16[128,512]{1,0:T(8,128)(2,1)S(1)}, bf16[128,512]{1,0:T(8,128)(2,1)S(1)}, u32[]{:S(2)}, u32[]{:S(2)}) collective-permute-start(bf16[128,512]{1,0:T(8,128)(2,1)S(1)} %shard_map.125.refs_0_), channel_id=1, source_target_pairs={{0,16},{8,24},{16,0},{24,8},{1,17},{9,25},{17,1},{25,9},{2,18},{10... | collective-permute-start | bytes 393224 | tf_op jit(solution)/shard_map/ppermute | solution.py:347
  146.8 8.5 %collective-permute-start.17 = (bf16[128,512]{1,0:T(8,128)(2,1)S(1)}, bf16[128,512]{1,0:T(8,128)(2,1)S(1)}, u32[]{:S(2)}, u32[]{:S(2)}) collective-permute-start(bf16[128,512]{1,0:T(8,128)(2,1)S(1)} %shard_map.119.refs_0_), channel_id=1, source_target_pairs={{0,8},{8,0},{16,24},{24,16},{1,9},{9,1},{17,25},{25,17},{2,10},{10... | collective-permute-start | bytes 393224 | tf_op jit(solution)/shard_map/ppermute | solution.py:347
  147.1 8.9 %collective-permute-start.1 = (bf16[128,512]{1,0:T(8,128)(2,1)S(1)}, bf16[128,512]{1,0:T(8,128)(2,1)S(1)}, u32[]{:S(2)}, u32[]{:S(2)}) collective-permute-start(bf16[128,512]{1,0:T(8,128)(2,1)S(1)} %get-tuple-element.91), channel_id=1, source_target_pairs={{0,2},{1,3},{2,0},{3,1},{4,6},{5,7},{6,4},{7,5},{8,10},{9,11},{10,... | collective-permute-start | bytes 393224 | tf_op jit(solution)/shard_map/ppermute | solution.py:324
  149.1 10.8 %collective-permute-start.2 = (bf16[128,512]{1,0:T(8,128)(2,1)S(1)}, bf16[128,512]{1,0:T(8,128)(2,1)S(1)}, u32[]{:S(2)}, u32[]{:S(2)}) collective-permute-start(bf16[128,512]{1,0:T(8,128)(2,1)S(1)} %get-tuple-element.92), channel_id=1, source_target_pairs={{0,4},{1,5},{2,6},{3,7},{4,0},{5,1},{6,2},{7,3},{8,12},{9,13},{10,... | collective-permute-start | bytes 393224 | tf_op jit(solution)/shard_map/ppermute | solution.py:324
  150.6 9.3 %collective-permute-start.3 = (bf16[128,512]{1,0:T(8,128)(2,1)S(1)}, bf16[128,512]{1,0:T(8,128)(2,1)S(1)}, u32[]{:S(2)}, u32[]{:S(2)}) collective-permute-start(bf16[128,512]{1,0:T(8,128)(2,1)S(1)} %get-tuple-element.93), channel_id=1, source_target_pairs={{0,6},{1,7},{2,4},{3,5},{4,2},{5,3},{6,0},{7,1},{8,14},{9,15},{10,... | collective-permute-start | bytes 393224 | tf_op jit(solution)/shard_map/ppermute | solution.py:324
  152.9 9.1 %collective-permute-start.34 = (bf16[128,512]{1,0:T(8,128)(2,1)S(1)}, bf16[128,512]{1,0:T(8,128)(2,1)S(1)}, u32[]{:S(2)}, u32[]{:S(2)}) collective-permute-start(bf16[128,512]{1,0:T(8,128)(2,1)S(1)} %shard_map.126.refs_0_), channel_id=1, source_target_pairs={{0,6},{1,7},{2,4},{3,5},{4,2},{5,3},{6,0},{7,1},{8,14},{9,15},{10,... | collective-permute-start | bytes 393224 | tf_op jit(solution)/shard_map/ppermute | solution.py:324
  165.8 8.3 %collective-permute-start.5 = (bf16[128,512]{1,0:T(8,128)(2,1)S(1)}, bf16[128,512]{1,0:T(8,128)(2,1)S(1)}, u32[]{:S(2)}, u32[]{:S(2)}) collective-permute-start(bf16[128,512]{1,0:T(8,128)(2,1)S(1)} %shard_map.115.refs_0_), channel_id=1, source_target_pairs={{0,16},{8,24},{16,0},{24,8},{1,17},{9,25},{17,1},{25,9},{2,18},{10... | collective-permute-start | bytes 393224 | tf_op jit(solution)/shard_map/ppermute | solution.py:347
  178.3 7.9 %collective-permute-start.23 = (bf16[128,512]{1,0:T(8,128)(2,1)S(1)}, bf16[128,512]{1,0:T(8,128)(2,1)S(1)}, u32[]{:S(2)}, u32[]{:S(2)}) collective-permute-start(bf16[128,512]{1,0:T(8,128)(2,1)S(1)} %collective-permute-done.19.refs_1_), channel_id=1, source_target_pairs={{0,1},{1,0},{2,3},{3,2},{4,5},{5,4},{6,7},{7,6},{8,9},{9,8},{10,11... | collective-permute-start | bytes 393224 | tf_op jit(solution)/shard_map/ppermute | solution.py:324
  178.3 11.4 %collective-permute-start.9 = (bf16[128,512]{1,0:T(8,128)(2,1)S(1)}, bf16[128,512]{1,0:T(8,128)(2,1)S(1)}, u32[]{:S(2)}, u32[]{:S(2)}) collective-permute-start(bf16[128,512]{1,0:T(8,128)(2,1)S(1)} %shard_map.116.refs_0_), channel_id=1, source_target_pairs={{0,1},{1,0},{2,3},{3,2},{4,5},{5,4},{6,7},{7,6},{8,9},{9,8},{10,11... | collective-permute-start | bytes 393224 | tf_op jit(solution)/shard_map/ppermute | solution.py:324
  (27 other events, 142.9 us)

commit v7 on v6

--- a/solution.py
+++ b/solution.py
@@ -91,8 +91,8 @@
 def load_kernel(layer, *refs):
     count = (len(refs) - 1) // 2
     go = Copies(refs[-1])
-    for n, (source, target) in enumerate(zip(refs[:count], refs[count:-1])):
-        go.store(source.at[layer] if n < 2 else source, target)
+    for source, target in zip(refs[:count], refs[count:-1]):
+        go.store(source if source.shape == target.shape else source.at[layer], target)
     go.finish()
 
 
@@ -164,39 +164,37 @@
     go.finish()
 
 
-def delta_of(loads, arr, row, before_v, slope_v):
-    back = return_rows(row[...], arr[...], before_v.shape[0])
-    for load in loads:
-        load.wait()
-    grad = (before_v[...] + back).astype(jnp.bfloat16)
-    return (grad.astype(jnp.float32) * slope_v[...]).astype(jnp.bfloat16)
+def delta_of(arr, before, slope, row):
+    back = return_rows(row[...], arr[...], before.shape[0])
+    grad = (before[...] + back).astype(jnp.bfloat16)
+    return (grad.astype(jnp.float32) * slope[...]).astype(jnp.bfloat16)
 
 
 def backward_kernel(
     cols, arr, before, slope, row, val, ws, wn, delta_out, halo_out, base_out,
-    before_v, slope_v, halo_v, base_v, acc_v, sems,
+    delta_v, halo_v, base_v, acc_v, sems,
 ):
     go = Copies(sems)
-    loads = [go.start(before, before_v), go.start(slope, slope_v)]
-    delta = delta_of(loads, arr, row, before_v, slope_v)
-    delta_out[...] = delta
+    delta = delta_of(arr, before, slope, row)
+    delta_v[...] = delta
+    go.store(delta_v, delta_out)
     spread_back(go, delta, cols, val, ws, wn, halo_out, base_out, halo_v, base_v, acc_v)
     go.finish()
 
 
-def top_kernel(
-    core, hid, agg, arr, before, slope, row, delta_out, keep, give, before_v, slope_v, sems
-):
-    go = Copies(sems)
-    loads = [go.start(before, before_v), go.start(slope, slope_v)]
-    delta = delta_of(loads, arr, row, before_v, slope_v)
+def top_kernel(core, hid, agg, arr, before, slope, row, delta_out, keep, give, sems):
+    delta = delta_of(arr, before, slope, row)
     delta_out[...] = delta
     products(core[0], hid, agg, delta, (give, keep))
 
 
-def spread_kernel(cols, delta, val, ws, wn, halo_out, base_out, halo_v, base_v, acc_v, sems):
-    go = Copies(sems)
-    spread_back(go, delta[...], cols, val, ws, wn, halo_out, base_out, halo_v, base_v, acc_v)
+def spread_kernel(
+    layer, cols, delta, val, ws, wn, halo_out, base_out, ws_v, wn_v, halo_v, base_v, acc_v, sems
+):
+    go = Copies(sems)
+    for load in (go.start(wn.at[layer], wn_v), go.start(ws.at[layer], ws_v)):
+        load.wait()
+    spread_back(go, delta[...], cols, val, ws_v, wn_v, halo_out, base_out, halo_v, base_v, acc_v)
     go.finish()
 
 
@@ -368,12 +366,16 @@
             alias={1 + 2 * chips: 0, 2 + 2 * chips: 1} if outs else None,
         )
 
-    def load(layer, *others):
-        arrays = (self_weight, neigh_weight, *others)
+    weights = (self_weight, neigh_weight)
+
+    def load(layer, *arrays):
         return call(
             functools.partial(load_kernel, layer),
             [(a, away) for a in arrays],
-            [(a.shape[1:] if n < 2 else a.shape, a.dtype, near) for n, a in enumerate(arrays)],
+            [
+                (a.shape[1:] if a is self_weight or a is neigh_weight else a.shape, a.dtype, near)
+                for a in arrays
+            ],
         )
 
     cols = (block_col, scalars)
@@ -386,7 +388,7 @@
         ),
     )
     arrived = exchange(send)
-    ws, wn, hidden, val = load(0, features, block_val)
+    ws, wn, hidden, val = load(0, *weights, features, block_val)
     hiddens, aggregates, slopes = [features], [], []
     for layer in range(layers - 1):
         aggregate, slope, kept, hidden, send = call(
@@ -404,7 +406,7 @@
         slopes.append(slope)
         arrived = exchange(send)
         last = layer + 2 == layers
-        ws, wn, *cot = load(layer + 1, *((cotangent,) if last else ()))
+        ws, wn, *cot = load(layer + 1, *weights, *((cotangent,) if last else ()))
     aggregate, delta, outgoing, base = call(
         last_kernel,
         (
@@ -416,7 +418,7 @@
         flops=2 * big,
     )
     aggregates.append(aggregate)
-    sums, delta_at = [], away
+    sums = []
     for layer in reversed(range(layers)):
         below = layer - 1
         if layer:
@@ -424,7 +426,7 @@
                 weight_kernel,
                 (
                     (core_arg, scalars), (hiddens[layer], away), (aggregates[layer], away),
-                    (delta, delta_at),
+                    (delta, away),
                 ),
                 ((*square, near), (*square, near)),
                 (rows, rows, rows),
@@ -434,17 +436,15 @@
         arrived = exchange(outgoing)
         if not layer:
             break
-        last = (hiddens[0], aggregates[0]) if below == 0 else ()
-        ws, wn, *more = load(below, *last)
-        back = ((arrived, near), (base, away), (slopes[below], away), (row, near))
-        graph = ((val, near), (ws, near), (wn, near))
-        delta_at = near
+        more = weights if below else (hiddens[0], aggregates[0])
+        base, slope, *more = load(below, base, slopes[below], *more)
+        back = ((arrived, near), (base, near), (slope, near), (row, near))
         if below:
             delta, outgoing, base = call(
                 backward_kernel,
-                (cols, *back, *graph),
-                ((*rows, near), (*halo_rows, away), (*rows32, away)),
-                (rows32, rows32, halo_rows, rows32, acc),
+                (cols, *back, (val, near), *((a, near) for a in more)),
+                ((*rows, away), (*halo_rows, away), (*rows32, away)),
+                (rows, halo_rows, rows32, acc),
                 flops=big,
             )
         else:
@@ -452,15 +452,14 @@
                 top_kernel,
                 ((core_arg, scalars), *((a, near) for a in more), *back),
                 ((*rows, near), (*square, near), (*square, near)),
-                (rows32, rows32),
                 flops=big,
             )
         if not below:
             outgoing, base = call(
-                spread_kernel,
-                (cols, (delta, near), *graph),
+                functools.partial(spread_kernel, 0),
+                (cols, (delta, near), (val, near), *((w, away) for w in weights)),
                 ((*halo_rows, away), (*rows32, away)),
-                (halo_rows, rows32, acc),
+                (square, square, halo_rows, rows32, acc),
                 flops=big,
             )
     (grad,) = call(

time: 192 us -> 192 us (level)
  blocking collectives: 18.6 us -> 0 us
  waiting for transfers between devices: 75.3 us -> 88.6 us
  starting transfers between devices: 50.8 us -> 53.8 us
    all_to_all x1 -> x0, blocking collectives: 18.6 us -> none  [exchange(): return lax.all_to_all(sent, AXES, 0, 0, tiled=True).reshape(halo, width)]
    all_to_all x5 -> x6, waiting for transfers between devices: 49.5 us -> 62.9 us  [exchange(): return lax.all_to_all(sent, AXES, 0, 0, tiled=True).reshape(halo, width)]
    all_to_all x5 -> x6, starting transfers between devices: 19.4 us -> 22.4 us  [exchange(): return lax.all_to_all(sent, AXES, 0, 0, tiled=True).reshape(halo, width)]
    unnamed x14 -> x18, local copies, waits for them, and re-layouts: 5.32 us -> 6.81 us
    pallas_call x29 -> x30, Pallas kernels: 40.1 us -> 40.8 us  [call(): pl.pallas_call(body, in_specs=[pl.BlockSpec(memory_space=space) for _, sp...]
  transfers between devices with their start and end apart: 44 -> 45, of which waited for: 15 -> 16; matrix products, arithmetic and copies ran while one was open for 0% -> 0% of each run, Pallas kernels for 12% -> 13%
where the time goes in v7:
time: 192 us; the launch traced here: 191 us
  waiting for transfers between devices  88.6 us (46%)
  starting transfers between devices  53.8 us (28%)
  Pallas kernels  40.8 us (21%)
  local copies, waits for them, and re-layouts  6.81 us (4%)
    all_to_all x6, waiting for transfers between devices, exchange(): return lax.all_to_all(sent, AXES, 0, 0, tiled=True).reshape(halo, width)  62.9 us
    pallas_call x30, Pallas kernels, call(): pl.pallas_call(body, in_specs=[pl.BlockSpec(memory_space=space) for _, sp...  40.8 us
    ppermute x33, starting transfers between devices, flip(): return lax.ppermute(array, 'gy', [(j, j ^ mask) for j in range(inner)])  22.4 us
    all_to_all x6, starting transfers between devices, exchange(): return lax.all_to_all(sent, AXES, 0, 0, tiled=True).reshape(halo, width)  22.4 us
    ppermute x6, waiting for transfers between devices, chip_sum(): got = lax.ppermute(total, 'gx', perm)  14.2 us
    ppermute x33, waiting for transfers between devices, flip(): return lax.ppermute(array, 'gy', [(j, j ^ mask) for j in range(inner)])  11.5 us
    ppermute x6, starting transfers between devices, chip_sum(): got = lax.ppermute(total, 'gx', perm)  9.01 us
    unnamed x18, local copies, waits for them, and re-layouts  6.81 us
  transfers between devices with their start and end apart: 45, of which 16 were waited for; matrix products, arithmetic and copies ran while one was open for 0% of the time, Pallas kernels for 13%

profile of v7, /device:TPU:0, one launch (start us, length us, event | category | flops | bytes accessed | tf_op | source)
XLA Modules:
  0.0 191.3 jit_solution(5996323753721860062)
XLA Ops:
  2.8 7.3 %all-to-all-start = ((bf16[32,16,512]{2,1,0:T(8,128)(2,1)}), bf16[32,16,512]{2,1,0:T(8,128)(2,1)S(1)}, u32[]{:S(2)}, u32[]{:S(2)}) async-start(bf16[32,16,512]{2,1,0:T(8,128)(2,1)} %bitcast.26), calls=%async_computation | async-start | bytes 1048576 | tf_op jit(solution)/shard_map/all_to_all | solution.py:313
  11.5 14.2 %all-to-all-done = bf16[32,16,512]{2,1,0:T(8,128)(2,1)S(1)} async-done(((bf16[32,16,512]{2,1,0:T(8,128)(2,1)}), bf16[32,16,512]{2,1,0:T(8,128)(2,1)S(1)}, u32[]{:S(2)}, u32[]{:S(2)}) %all-to-all-start) | async-done | bytes 524320 | tf_op jit(solution)/shard_map/all_to_all | solution.py:313
  25.7 2.6 %shard_map.105 = (bf16[256,512]{1,0:T(8,128)(2,1)}, f32[256,512]{1,0:T(8,128)}, bf16[256,512]{1,0:T(8,128)(2,1)}, bf16[256,512]{1,0:T(8,128)(2,1)S(1)}, bf16[512,512]{1,0:T(8,128)(2,1)}) custom-call(s32[2,4]{1,0:T(2,128)S(1)} %copy-done.8, bf16[256,512]{1,0:T(8,128)(2,1)S(1)} %get-tuple-element.67.hid, bf16[512,512]{1,0:T(8,128)(2,1)S(1)} %bitcast.18, ...), custom_call_target="tpu_custom_call" | custom-call | flops 536870912 | bytes 3670016 | tf_op jit(solution)/shard_map/pallas_call | solution.py:293
  28.4 3.0 %all-to-all-start.1 = ((bf16[32,16,512]{2,1,0:T(8,128)(2,1)}), bf16[32,16,512]{2,1,0:T(8,128)(2,1)S(1)}, u32[]{:S(2)}, u32[]{:S(2)}) async-start(bf16[32,16,512]{2,1,0:T(8,128)(2,1)} %bitcast.25), calls=%async_computation.1 | async-start | bytes 1048576 | tf_op jit(solution)/shard_map/all_to_all | solution.py:313
  32.6 14.4 %all-to-all-done.1 = bf16[32,16,512]{2,1,0:T(8,128)(2,1)S(1)} async-done(((bf16[32,16,512]{2,1,0:T(8,128)(2,1)}), bf16[32,16,512]{2,1,0:T(8,128)(2,1)S(1)}, u32[]{:S(2)}, u32[]{:S(2)}) %all-to-all-start.1) | async-done | bytes 524320 | tf_op jit(solution)/shard_map/all_to_all | solution.py:313
  47.0 2.6 %shard_map.107 = (bf16[256,512]{1,0:T(8,128)(2,1)}, f32[256,512]{1,0:T(8,128)}, bf16[256,512]{1,0:T(8,128)(2,1)}, bf16[256,512]{1,0:T(8,128)(2,1)S(1)}, bf16[512,512]{1,0:T(8,128)(2,1)}) custom-call(s32[2,4]{1,0:T(2,128)S(1)} %copy-done.8, bf16[256,512]{1,0:T(8,128)(2,1)S(1)} %get-tuple-element.73.hid, bf16[512,512]{1,0:T(8,128)(2,1)S(1)} %bitcast.19, ...), custom_call_target="tpu_custom_call" | custom-call | flops 536870912 | bytes 3670016 | tf_op jit(solution)/shard_map/pallas_call | solution.py:293
  49.6 3.0 %all-to-all-start.2 = ((bf16[32,16,512]{2,1,0:T(8,128)(2,1)}), bf16[32,16,512]{2,1,0:T(8,128)(2,1)S(1)}, u32[]{:S(2)}, u32[]{:S(2)}) async-start(bf16[32,16,512]{2,1,0:T(8,128)(2,1)} %bitcast.24), calls=%async_computation.2 | async-start | bytes 1048576 | tf_op jit(solution)/shard_map/all_to_all | solution.py:313
  53.9 14.3 %all-to-all-done.2 = bf16[32,16,512]{2,1,0:T(8,128)(2,1)S(1)} async-done(((bf16[32,16,512]{2,1,0:T(8,128)(2,1)}), bf16[32,16,512]{2,1,0:T(8,128)(2,1)S(1)}, u32[]{:S(2)}, u32[]{:S(2)}) %all-to-all-start.2) | async-done | bytes 524320 | tf_op jit(solution)/shard_map/all_to_all | solution.py:313
  68.2 3.4 %shard_map.109 = (bf16[256,512]{1,0:T(8,128)(2,1)}, bf16[256,512]{1,0:T(8,128)(2,1)}, bf16[512,512]{1,0:T(8,128)(2,1)}, f32[256,512]{1,0:T(8,128)}) custom-call(s32[2,4]{1,0:T(2,128)S(1)} %copy-done.8, bf16[256,512]{1,0:T(8,128)(2,1)S(1)} %get-tuple-element.77.hid, bf16[512,512]{1,0:T(8,128)(2,1)S(1)} %bitcast.20, ...), custom_call_target="tpu_custom_call" | custom-call | flops 1073741824 | bytes 3145728 | tf_op jit(solution)/shard_map/pallas_call | solution.py:293
  71.6 3.0 %all-to-all-start.3 = ((bf16[32,16,512]{2,1,0:T(8,128)(2,1)}), bf16[32,16,512]{2,1,0:T(8,128)(2,1)S(1)}, u32[]{:S(2)}, u32[]{:S(2)}) async-start(bf16[32,16,512]{2,1,0:T(8,128)(2,1)} %bitcast.23), calls=%async_computation.3 | async-start | bytes 1048576 | tf_op jit(solution)/shard_map/all_to_all | solution.py:313
  76.1 14.0 %all-to-all-done.3 = bf16[32,16,512]{2,1,0:T(8,128)(2,1)S(1)} async-done(((bf16[32,16,512]{2,1,0:T(8,128)(2,1)}), bf16[32,16,512]{2,1,0:T(8,128)(2,1)S(1)}, u32[]{:S(2)}, u32[]{:S(2)}) %all-to-all-start.3) | async-done | bytes 524320 | tf_op jit(solution)/shard_map/all_to_all | solution.py:313
  90.2 2.7 %shard_map.111 = (bf16[256,512]{1,0:T(8,128)(2,1)}, bf16[512,512]{1,0:T(8,128)(2,1)}, f32[256,512]{1,0:T(8,128)}) custom-call(s32[2,4]{1,0:T(2,128)S(1)} %copy-done.8, bf16[512,512]{1,0:T(8,128)(2,1)S(1)} %bitcast.17, f32[256,512]{1,0:T(8,128)S(1)} %get-tuple-element.85.before, f32[256,512]{1,0:T(8,128)S(1)} %get-tuple-element.86.slope, ...), custom_call_target="tpu_custom_call" | custom-call | flops 536870912 | bytes 2621440 | tf_op jit(solution)/shard_map/pallas_call | solution.py:293
  92.9 3.0 %all-to-all-start.4 = ((bf16[32,16,512]{2,1,0:T(8,128)(2,1)}), bf16[32,16,512]{2,1,0:T(8,128)(2,1)S(1)}, u32[]{:S(2)}, u32[]{:S(2)}) async-start(bf16[32,16,512]{2,1,0:T(8,128)(2,1)} %bitcast.22), calls=%async_computation.4 | async-start | bytes 1048576 | tf_op jit(solution)/shard_map/all_to_all | solution.py:313
  95.9 2.6 %shard_map.123 = (bf16[512,512]{1,0:T(8,128)(2,1)S(1)}, bf16[512,512]{1,0:T(8,128)(2,1)}) custom-call(s32[1]{0:T(128)} %bitcast.core, bf16[256,512]{1,0:T(8,128)(2,1)} %get-tuple-element.113.hid, bf16[256,512]{1,0:T(8,128)(2,1)} %get-tuple-element.114.agg, bf16[256,512]{1,0:T(8,128)(2,1)} %get-tuple-element.115.delta), custom_call_target="tpu_custom_call" | custom-call | flops 268435456 | bytes 2097152 | tf_op jit(solution)/shard_map/pallas_call | solution.py:293
  98.8 2.6 %shard_map.118 = (bf16[512,512]{1,0:T(8,128)(2,1)S(1)}, bf16[512,512]{1,0:T(8,128)(2,1)}) custom-call(s32[1]{0:T(128)} %bitcast.core, bf16[256,512]{1,0:T(8,128)(2,1)} %get-tuple-element.104.hid, bf16[256,512]{1,0:T(8,128)(2,1)} %get-tuple-element.105.agg, bf16[256,512]{1,0:T(8,128)(2,1)} %get-tuple-element.106.delta), custom_call_target="tpu_custom_call" | custom-call | flops 268435456 | bytes 2097152 | tf_op jit(solution)/shard_map/pallas_call | solution.py:293
  105.5 6.0 %all-to-all-done.4 = bf16[32,16,512]{2,1,0:T(8,128)(2,1)S(1)} async-done(((bf16[32,16,512]{2,1,0:T(8,128)(2,1)}), bf16[32,16,512]{2,1,0:T(8,128)(2,1)S(1)}, u32[]{:S(2)}, u32[]{:S(2)}) %all-to-all-start.4) | async-done | bytes 524320 | tf_op jit(solution)/shard_map/all_to_all | solution.py:313
  123.3 3.6 %shard_map.131 = (bf16[512,512]{1,0:T(8,128)(2,1)}, f32[256,512]{1,0:T(8,128)}) custom-call(s32[2,4]{1,0:T(2,128)S(1)} %copy-done.8, bf16[256,512]{1,0:T(8,128)(2,1)S(1)} %copy-done.3, bf16[2,4,128,128]{3,2,1,0:T(8,128)(2,1)S(1)} %get-tuple-element.69.val, bf16[3,512,512]{2,1,0:T(8,128)(2,1)} %ws.1, bf16[3,512,512]{2,1,0:T(8,128)(2,1)} %wn.1), custom_call_target="tpu_custom_call" | custom-call | flops 536870912 | bytes 2097152 | tf_op jit(solution)/shard_map/pallas_call | solution.py:293
  127.0 3.2 %all-to-all-start.5 = ((bf16[32,16,512]{2,1,0:T(8,128)(2,1)}), bf16[32,16,512]{2,1,0:T(8,128)(2,1)S(1)}, u32[]{:S(2)}, u32[]{:S(2)}) async-start(bf16[32,16,512]{2,1,0:T(8,128)(2,1)} %bitcast.21), calls=%async_computation.5 | async-start | bytes 1048576 | tf_op jit(solution)/shard_map/all_to_all | solution.py:313
  135.7 7.3 %collective-permute-done.30.refs_1_ = bf16[128,512]{1,0:T(8,128)(2,1)S(1)} collective-permute-done((bf16[128,512]{1,0:T(8,128)(2,1)S(1)}, bf16[128,512]{1,0:T(8,128)(2,1)S(1)}, u32[]{:S(2)}, u32[]{:S(2)}) %collective-permute-start.30) | collective-permute-done | bytes 131104 | tf_op jit(solution)/shard_map/ppermute | solution.py:345
  143.0 3.5 %collective-permute-start.31 = (bf16[128,512]{1,0:T(8,128)(2,1)S(1)}, bf16[128,512]{1,0:T(8,128)(2,1)S(1)}, u32[]{:S(2)}, u32[]{:S(2)}) collective-permute-start(bf16[128,512]{1,0:T(8,128)(2,1)S(1)} %shard_map.126.refs_0_), channel_id=1, source_target_pairs={{0,16},{8,24},{16,0},{24,8},{1,17},{9,25},{17,1},{25,9},{2,18},{10... | collective-permute-start | bytes 393224 | tf_op jit(solution)/shard_map/ppermute | solution.py:345
  152.8 2.5 %collective-permute-start.34 = (bf16[128,512]{1,0:T(8,128)(2,1)S(1)}, bf16[128,512]{1,0:T(8,128)(2,1)S(1)}, u32[]{:S(2)}, u32[]{:S(2)}) collective-permute-start(bf16[128,512]{1,0:T(8,128)(2,1)S(1)} %shard_map.127.refs_0_), channel_id=1, source_target_pairs={{0,6},{1,7},{2,4},{3,5},{4,2},{5,3},{6,0},{7,1},{8,14},{9,15},{10,... | collective-permute-start | bytes 393224 | tf_op jit(solution)/shard_map/ppermute | solution.py:322
  157.1 2.8 %collective-permute-done.2.refs_2_ = bf16[128,512]{1,0:T(8,128)(2,1)S(1)} collective-permute-done((bf16[128,512]{1,0:T(8,128)(2,1)S(1)}, bf16[128,512]{1,0:T(8,128)(2,1)S(1)}, u32[]{:S(2)}, u32[]{:S(2)}) %collective-permute-start.2) | collective-permute-done | bytes 131104 | tf_op jit(solution)/shard_map/ppermute | solution.py:322
  171.7 2.3 %collective-permute-done.5.refs_1_ = bf16[128,512]{1,0:T(8,128)(2,1)S(1)} collective-permute-done((bf16[128,512]{1,0:T(8,128)(2,1)S(1)}, bf16[128,512]{1,0:T(8,128)(2,1)S(1)}, u32[]{:S(2)}, u32[]{:S(2)}) %collective-permute-start.5) | collective-permute-done | bytes 131104 | tf_op jit(solution)/shard_map/ppermute | solution.py:345
  178.7 3.3 %collective-permute-done.8.refs_3_ = bf16[128,512]{1,0:T(8,128)(2,1)S(1)} collective-permute-done((bf16[128,512]{1,0:T(8,128)(2,1)S(1)}, bf16[128,512]{1,0:T(8,128)(2,1)S(1)}, u32[]{:S(2)}, u32[]{:S(2)}) %collective-permute-start.8) | collective-permute-done | bytes 131104 | tf_op jit(solution)/shard_map/ppermute | solution.py:322
  (115 shorter events, 62.9 us)
Async XLA Ops:
  2.8 22.9 %all-to-all-start = ((bf16[32,16,512]{2,1,0:T(8,128)(2,1)}), bf16[32,16,512]{2,1,0:T(8,128)(2,1)S(1)}, u32[]{:S(2)}, u32[]{:S(2)}) async-start(bf16[32,16,512]{2,1,0:T(8,128)(2,1)} %bitcast.26), calls=%async_computation | async-start | bytes 1048576 | tf_op jit(solution)/shard_map/all_to_all | solution.py:313
  28.4 18.6 %all-to-all-start.1 = ((bf16[32,16,512]{2,1,0:T(8,128)(2,1)}), bf16[32,16,512]{2,1,0:T(8,128)(2,1)S(1)}, u32[]{:S(2)}, u32[]{:S(2)}) async-start(bf16[32,16,512]{2,1,0:T(8,128)(2,1)} %bitcast.25), calls=%async_computation.1 | async-start | bytes 1048576 | tf_op jit(solution)/shard_map/all_to_all | solution.py:313
  49.6 18.6 %all-to-all-start.2 = ((bf16[32,16,512]{2,1,0:T(8,128)(2,1)}), bf16[32,16,512]{2,1,0:T(8,128)(2,1)S(1)}, u32[]{:S(2)}, u32[]{:S(2)}) async-start(bf16[32,16,512]{2,1,0:T(8,128)(2,1)} %bitcast.24), calls=%async_computation.2 | async-start | bytes 1048576 | tf_op jit(solution)/shard_map/all_to_all | solution.py:313
  71.6 18.6 %all-to-all-start.3 = ((bf16[32,16,512]{2,1,0:T(8,128)(2,1)}), bf16[32,16,512]{2,1,0:T(8,128)(2,1)S(1)}, u32[]{:S(2)}, u32[]{:S(2)}) async-start(bf16[32,16,512]{2,1,0:T(8,128)(2,1)} %bitcast.23), calls=%async_computation.3 | async-start | bytes 1048576 | tf_op jit(solution)/shard_map/all_to_all | solution.py:313
  92.9 18.6 %all-to-all-start.4 = ((bf16[32,16,512]{2,1,0:T(8,128)(2,1)}), bf16[32,16,512]{2,1,0:T(8,128)(2,1)S(1)}, u32[]{:S(2)}, u32[]{:S(2)}) async-start(bf16[32,16,512]{2,1,0:T(8,128)(2,1)} %bitcast.22), calls=%async_computation.4 | async-start | bytes 1048576 | tf_op jit(solution)/shard_map/all_to_all | solution.py:313
  98.5 18.5 %collective-permute-start.26 = (bf16[512,512]{1,0:T(8,128)(2,1)}, bf16[512,512]{1,0:T(8,128)(2,1)}, u32[]{:S(2)}, u32[]{:S(2)}) collective-permute-start(bf16[512,512]{1,0:T(8,128)(2,1)} %get-tuple-element.117), channel_id=1, source_target_pairs={{0,1},{1,0},{2,3},{3,2},{4,5},{5,4},{6,7},{7,6},{8,9},{9,8},{10,11... | collective-permute-start | bytes 1572872 | tf_op jit(solution)/shard_map/ppermute | solution.py:322
  101.5 30.5 %collective-permute-start.13 = (bf16[512,512]{1,0:T(8,128)(2,1)}, bf16[512,512]{1,0:T(8,128)(2,1)S(1)}, u32[]{:S(2)}, u32[]{:S(2)}) collective-permute-start(bf16[512,512]{1,0:T(8,128)(2,1)} %get-tuple-element.108), channel_id=1, source_target_pairs={{0,1},{1,0},{2,3},{3,2},{4,5},{5,4},{6,7},{7,6},{8,9},{9,8},{10,11... | collective-permute-start | bytes 1572872 | tf_op jit(solution)/shard_map/ppermute | solution.py:322
  117.0 29.8 %collective-permute-start = (bf16[512,512]{1,0:T(8,128)(2,1)}, bf16[512,512]{1,0:T(8,128)(2,1)S(1)}, u32[]{:S(2)}, u32[]{:S(2)}) collective-permute-start(bf16[512,512]{1,0:T(8,128)(2,1)} %get-tuple-element.99), channel_id=1, source_target_pairs={{0,1},{1,0},{2,3},{3,2},{4,5},{5,4},{6,7},{7,6},{8,9},{9,8},{10,11... | collective-permute-start | bytes 1572872 | tf_op jit(solution)/shard_map/ppermute | solution.py:322
  118.8 11.3 %collective-permute-start.27 = (bf16[128,512]{1,0:T(8,128)(2,1)}, bf16[128,512]{1,0:T(8,128)(2,1)S(1)}, u32[]{:S(2)}, u32[]{:S(2)}) collective-permute-start(bf16[128,512]{1,0:T(8,128)(2,1)} %get-tuple-element.119), channel_id=1, source_target_pairs={{0,2},{1,3},{2,0},{3,1},{4,6},{5,7},{6,4},{7,5},{8,10},{9,11},{10,... | collective-permute-start | bytes 393224 | tf_op jit(solution)/shard_map/ppermute | solution.py:322
  120.1 10.0 %collective-permute-start.28 = (bf16[128,512]{1,0:T(8,128)(2,1)}, bf16[128,512]{1,0:T(8,128)(2,1)S(1)}, u32[]{:S(2)}, u32[]{:S(2)}) collective-permute-start(bf16[128,512]{1,0:T(8,128)(2,1)} %get-tuple-element.120), channel_id=1, source_target_pairs={{0,4},{1,5},{2,6},{3,7},{4,0},{5,1},{6,2},{7,3},{8,12},{9,13},{10,... | collective-permute-start | bytes 393224 | tf_op jit(solution)/shard_map/ppermute | solution.py:322
  121.2 8.9 %collective-permute-start.29 = (bf16[128,512]{1,0:T(8,128)(2,1)S(1)}, bf16[128,512]{1,0:T(8,128)(2,1)S(1)}, u32[]{:S(2)}, u32[]{:S(2)}) collective-permute-start(bf16[128,512]{1,0:T(8,128)(2,1)S(1)} %get-tuple-element.121), channel_id=1, source_target_pairs={{0,6},{1,7},{2,4},{3,5},{4,2},{5,3},{6,0},{7,1},{8,14},{9,15},{10,... | collective-permute-start | bytes 393224 | tf_op jit(solution)/shard_map/ppermute | solution.py:322
  127.0 60.7 %all-to-all-start.5 = ((bf16[32,16,512]{2,1,0:T(8,128)(2,1)}), bf16[32,16,512]{2,1,0:T(8,128)(2,1)S(1)}, u32[]{:S(2)}, u32[]{:S(2)}) async-start(bf16[32,16,512]{2,1,0:T(8,128)(2,1)} %bitcast.21), calls=%async_computation.5 | async-start | bytes 1048576 | tf_op jit(solution)/shard_map/all_to_all | solution.py:313
  130.3 12.7 %collective-permute-start.30 = (bf16[128,512]{1,0:T(8,128)(2,1)S(1)}, bf16[128,512]{1,0:T(8,128)(2,1)S(1)}, u32[]{:S(2)}, u32[]{:S(2)}) collective-permute-start(bf16[128,512]{1,0:T(8,128)(2,1)S(1)} %shard_map.125.refs_0_), channel_id=1, source_target_pairs={{0,8},{8,0},{16,24},{24,16},{1,9},{9,1},{17,25},{25,17},{2,10},{10... | collective-permute-start | bytes 393224 | tf_op jit(solution)/shard_map/ppermute | solution.py:345
  132.2 14.4 %collective-permute-start.14 = (bf16[128,512]{1,0:T(8,128)(2,1)S(1)}, bf16[128,512]{1,0:T(8,128)(2,1)S(1)}, u32[]{:S(2)}, u32[]{:S(2)}) collective-permute-start(bf16[128,512]{1,0:T(8,128)(2,1)S(1)} %get-tuple-element.110), channel_id=1, source_target_pairs={{0,2},{1,3},{2,0},{3,1},{4,6},{5,7},{6,4},{7,5},{8,10},{9,11},{10,... | collective-permute-start | bytes 393224 | tf_op jit(solution)/shard_map/ppermute | solution.py:322
  133.7 12.9 %collective-permute-start.15 = (bf16[128,512]{1,0:T(8,128)(2,1)S(1)}, bf16[128,512]{1,0:T(8,128)(2,1)S(1)}, u32[]{:S(2)}, u32[]{:S(2)}) collective-permute-start(bf16[128,512]{1,0:T(8,128)(2,1)S(1)} %get-tuple-element.111), channel_id=1, source_target_pairs={{0,4},{1,5},{2,6},{3,7},{4,0},{5,1},{6,2},{7,3},{8,12},{9,13},{10,... | collective-permute-start | bytes 393224 | tf_op jit(solution)/shard_map/ppermute | solution.py:322
  135.2 11.4 %collective-permute-start.16 = (bf16[128,512]{1,0:T(8,128)(2,1)S(1)}, bf16[128,512]{1,0:T(8,128)(2,1)S(1)}, u32[]{:S(2)}, u32[]{:S(2)}) collective-permute-start(bf16[128,512]{1,0:T(8,128)(2,1)S(1)} %get-tuple-element.112), channel_id=1, source_target_pairs={{0,6},{1,7},{2,4},{3,5},{4,2},{5,3},{6,0},{7,1},{8,14},{9,15},{10,... | collective-permute-start | bytes 393224 | tf_op jit(solution)/shard_map/ppermute | solution.py:322
  143.0 9.7 %collective-permute-start.31 = (bf16[128,512]{1,0:T(8,128)(2,1)S(1)}, bf16[128,512]{1,0:T(8,128)(2,1)S(1)}, u32[]{:S(2)}, u32[]{:S(2)}) collective-permute-start(bf16[128,512]{1,0:T(8,128)(2,1)S(1)} %shard_map.126.refs_0_), channel_id=1, source_target_pairs={{0,16},{8,24},{16,0},{24,8},{1,17},{9,25},{17,1},{25,9},{2,18},{10... | collective-permute-start | bytes 393224 | tf_op jit(solution)/shard_map/ppermute | solution.py:345
  146.7 8.5 %collective-permute-start.17 = (bf16[128,512]{1,0:T(8,128)(2,1)S(1)}, bf16[128,512]{1,0:T(8,128)(2,1)S(1)}, u32[]{:S(2)}, u32[]{:S(2)}) collective-permute-start(bf16[128,512]{1,0:T(8,128)(2,1)S(1)} %shard_map.120.refs_0_), channel_id=1, source_target_pairs={{0,8},{8,0},{16,24},{24,16},{1,9},{9,1},{17,25},{25,17},{2,10},{10... | collective-permute-start | bytes 393224 | tf_op jit(solution)/shard_map/ppermute | solution.py:345
  147.0 8.9 %collective-permute-start.1 = (bf16[128,512]{1,0:T(8,128)(2,1)S(1)}, bf16[128,512]{1,0:T(8,128)(2,1)S(1)}, u32[]{:S(2)}, u32[]{:S(2)}) collective-permute-start(bf16[128,512]{1,0:T(8,128)(2,1)S(1)} %get-tuple-element.101), channel_id=1, source_target_pairs={{0,2},{1,3},{2,0},{3,1},{4,6},{5,7},{6,4},{7,5},{8,10},{9,11},{10,... | collective-permute-start | bytes 393224 | tf_op jit(solution)/shard_map/ppermute | solution.py:322
  149.0 10.8 %collective-permute-start.2 = (bf16[128,512]{1,0:T(8,128)(2,1)S(1)}, bf16[128,512]{1,0:T(8,128)(2,1)S(1)}, u32[]{:S(2)}, u32[]{:S(2)}) collective-permute-start(bf16[128,512]{1,0:T(8,128)(2,1)S(1)} %get-tuple-element.102), channel_id=1, source_target_pairs={{0,4},{1,5},{2,6},{3,7},{4,0},{5,1},{6,2},{7,3},{8,12},{9,13},{10,... | collective-permute-start | bytes 393224 | tf_op jit(solution)/shard_map/ppermute | solution.py:322
  150.5 9.3 %collective-permute-start.3 = (bf16[128,512]{1,0:T(8,128)(2,1)S(1)}, bf16[128,512]{1,0:T(8,128)(2,1)S(1)}, u32[]{:S(2)}, u32[]{:S(2)}) collective-permute-start(bf16[128,512]{1,0:T(8,128)(2,1)S(1)} %get-tuple-element.103), channel_id=1, source_target_pairs={{0,6},{1,7},{2,4},{3,5},{4,2},{5,3},{6,0},{7,1},{8,14},{9,15},{10,... | collective-permute-start | bytes 393224 | tf_op jit(solution)/shard_map/ppermute | solution.py:322
  152.8 9.1 %collective-permute-start.34 = (bf16[128,512]{1,0:T(8,128)(2,1)S(1)}, bf16[128,512]{1,0:T(8,128)(2,1)S(1)}, u32[]{:S(2)}, u32[]{:S(2)}) collective-permute-start(bf16[128,512]{1,0:T(8,128)(2,1)S(1)} %shard_map.127.refs_0_), channel_id=1, source_target_pairs={{0,6},{1,7},{2,4},{3,5},{4,2},{5,3},{6,0},{7,1},{8,14},{9,15},{10,... | collective-permute-start | bytes 393224 | tf_op jit(solution)/shard_map/ppermute | solution.py:322
  165.7 8.3 %collective-permute-start.5 = (bf16[128,512]{1,0:T(8,128)(2,1)S(1)}, bf16[128,512]{1,0:T(8,128)(2,1)S(1)}, u32[]{:S(2)}, u32[]{:S(2)}) collective-permute-start(bf16[128,512]{1,0:T(8,128)(2,1)S(1)} %shard_map.116.refs_0_), channel_id=1, source_target_pairs={{0,16},{8,24},{16,0},{24,8},{1,17},{9,25},{17,1},{25,9},{2,18},{10... | collective-permute-start | bytes 393224 | tf_op jit(solution)/shard_map/ppermute | solution.py:345
  178.2 11.4 %collective-permute-start.9 = (bf16[128,512]{1,0:T(8,128)(2,1)S(1)}, bf16[128,512]{1,0:T(8,128)(2,1)S(1)}, u32[]{:S(2)}, u32[]{:S(2)}) collective-permute-start(bf16[128,512]{1,0:T(8,128)(2,1)S(1)} %shard_map.117.refs_0_), channel_id=1, source_target_pairs={{0,1},{1,0},{2,3},{3,2},{4,5},{5,4},{6,7},{7,6},{8,9},{9,8},{10,11... | collective-permute-start | bytes 393224 | tf_op jit(solution)/shard_map/ppermute | solution.py:322
  (30 other events, 152.2 us)

commit v8 on v7

--- a/solution.py
+++ b/solution.py
@@ -129,9 +129,9 @@
     go.finish()
 
 
-def spread_back(go, delta, cols, val, ws, wn, halo_out, base_out, halo_v, base_v, acc_v):
+def spread_back(go, delta, cols, val, ws, wn, halo_out, base, halo_v, acc_v, ready=None):
     tiles, blocks, tile, _ = val.shape
-    own = base_out.shape[0] // tile
+    own = base.shape[0] // tile
     acc_v[...] = jnp.zeros_like(acc_v)
     upstream = mm_nt(delta, wn[...]).astype(jnp.bfloat16)
     for r in range(tiles):
@@ -141,11 +141,12 @@
     for t in range(halo_out.shape[0] // tile):
         halo_v[t * tile : (t + 1) * tile, :] = acc_v[own + t].astype(jnp.bfloat16)
     go.store(halo_v, halo_out)
+    if ready is not None:
+        ready.wait()
     own_part = mm_nt(delta, ws[...])
     for t in range(own):
         at = slice(t * tile, (t + 1) * tile)
-        base_v[at, :] = own_part[at, :] + acc_v[t]
-    go.store(base_v, base_out)
+        base[at, :] = own_part[at, :] + acc_v[t]
 
 
 def last_kernel(
@@ -160,7 +161,8 @@
     delta = (cot[...].astype(jnp.float32) * slope).astype(jnp.bfloat16)
     delta_v[...] = delta
     go.store(delta_v, delta_out)
-    spread_back(go, delta, cols, val, ws, wn, halo_out, base_out, halo_v, base_v, acc_v)
+    spread_back(go, delta, cols, val, ws, wn, halo_out, base_v, halo_v, acc_v)
+    go.store(base_v, base_out)
     go.finish()
 
 
@@ -178,7 +180,8 @@
     delta = delta_of(arr, before, slope, row)
     delta_v[...] = delta
     go.store(delta_v, delta_out)
-    spread_back(go, delta, cols, val, ws, wn, halo_out, base_out, halo_v, base_v, acc_v)
+    spread_back(go, delta, cols, val, ws, wn, halo_out, base_v, halo_v, acc_v)
+    go.store(base_v, base_out)
     go.finish()
 
 
@@ -192,18 +195,17 @@
     layer, cols, delta, val, ws, wn, halo_out, base_out, ws_v, wn_v, halo_v, base_v, acc_v, sems
 ):
     go = Copies(sems)
-    for load in (go.start(wn.at[layer], wn_v), go.start(ws.at[layer], ws_v)):
-        load.wait()
-    spread_back(go, delta[...], cols, val, ws_v, wn_v, halo_out, base_out, halo_v, base_v, acc_v)
-    go.finish()
-
-
-def final_kernel(arr, before, row, grad_out, before_v, grad_v, sems):
-    go = Copies(sems)
-    load = go.start(before, before_v)
+    first, second = go.start(wn.at[layer], wn_v), go.start(ws.at[layer], ws_v)
+    first.wait()
+    spread_back(go, delta[...], cols, val, ws_v, wn_v, halo_out, base_v, halo_v, acc_v, second)
+    go.store(base_v, base_out)
+    go.finish()
+
+
+def final_kernel(arr, before, row, grad_out, grad_v, sems):
+    go = Copies(sems)
     back = return_rows(row[...], arr[...], before.shape[0])
-    load.wait()
-    grad_v[...] = (before_v[...] + back).astype(jnp.bfloat16)
+    grad_v[...] = (before[...] + back).astype(jnp.bfloat16)
     go.store(grad_v, grad_out)
     go.finish()
 
@@ -462,8 +464,9 @@
                 (square, square, halo_rows, rows32, acc),
                 flops=big,
             )
+    (base,) = load(0, base)
     (grad,) = call(
-        final_kernel, ((arrived, near), (base, away), (row, near)), ((*rows, away),), (rows32, rows)
+        final_kernel, ((arrived, near), (base, near), (row, near)), ((*rows, away),), (rows,)
     )
     outs = ()
     for layer, piece in zip(reversed(range(layers)), sums):

time: 192 us -> 193 us (level)
    pallas_call x30 -> x31, Pallas kernels: 40.8 us -> 41 us  [call(): pl.pallas_call(body, in_specs=[pl.BlockSpec(memory_space=space) for _, sp...]
  transfers between devices with their start and end apart: 45 -> 45, of which waited for: 16 -> 16; matrix products, arithmetic and copies ran while one was open for 0% -> 0% of each run, Pallas kernels for 13% -> 14%
where the time goes in v8:
time: 193 us; the launch traced here: 192 us
  waiting for transfers between devices  88.6 us (46%)
  starting transfers between devices  53.8 us (28%)
  Pallas kernels  41 us (21%)
  local copies, waits for them, and re-layouts  6.81 us (4%)
    all_to_all x6, waiting for transfers between devices, exchange(): return lax.all_to_all(sent, AXES, 0, 0, tiled=True).reshape(halo, width)  62.9 us
    pallas_call x31, Pallas kernels, call(): pl.pallas_call(body, in_specs=[pl.BlockSpec(memory_space=space) for _, sp...  41 us
    ppermute x33, starting transfers between devices, flip(): return lax.ppermute(array, 'gy', [(j, j ^ mask) for j in range(inner)])  22.4 us
    all_to_all x6, starting transfers between devices, exchange(): return lax.all_to_all(sent, AXES, 0, 0, tiled=True).reshape(halo, width)  22.4 us
    ppermute x6, waiting for transfers between devices, chip_sum(): got = lax.ppermute(total, 'gx', perm)  14.2 us
    ppermute x33, waiting for transfers between devices, flip(): return lax.ppermute(array, 'gy', [(j, j ^ mask) for j in range(inner)])  11.5 us
    ppermute x6, starting transfers between devices, chip_sum(): got = lax.ppermute(total, 'gx', perm)  9.01 us
    unnamed x18, local copies, waits for them, and re-layouts  6.81 us
  transfers between devices with their start and end apart: 45, of which 16 were waited for; matrix products, arithmetic and copies ran while one was open for 0% of the time, Pallas kernels for 14%

profile of v8, /device:TPU:0, one launch (start us, length us, event | category | flops | bytes accessed | tf_op | source)
XLA Modules:
  0.0 191.5 jit_solution(13219123591732882401)
XLA Ops:
  2.8 7.3 %all-to-all-start = ((bf16[32,16,512]{2,1,0:T(8,128)(2,1)}), bf16[32,16,512]{2,1,0:T(8,128)(2,1)S(1)}, u32[]{:S(2)}, u32[]{:S(2)}) async-start(bf16[32,16,512]{2,1,0:T(8,128)(2,1)} %bitcast.26), calls=%async_computation | async-start | bytes 1048576 | tf_op jit(solution)/shard_map/all_to_all | solution.py:315
  11.5 14.2 %all-to-all-done = bf16[32,16,512]{2,1,0:T(8,128)(2,1)S(1)} async-done(((bf16[32,16,512]{2,1,0:T(8,128)(2,1)}), bf16[32,16,512]{2,1,0:T(8,128)(2,1)S(1)}, u32[]{:S(2)}, u32[]{:S(2)}) %all-to-all-start) | async-done | bytes 524320 | tf_op jit(solution)/shard_map/all_to_all | solution.py:315
  25.7 2.6 %shard_map.105 = (bf16[256,512]{1,0:T(8,128)(2,1)}, f32[256,512]{1,0:T(8,128)}, bf16[256,512]{1,0:T(8,128)(2,1)}, bf16[256,512]{1,0:T(8,128)(2,1)S(1)}, bf16[512,512]{1,0:T(8,128)(2,1)}) custom-call(s32[2,4]{1,0:T(2,128)S(1)} %copy-done.8, bf16[256,512]{1,0:T(8,128)(2,1)S(1)} %get-tuple-element.67.hid, bf16[512,512]{1,0:T(8,128)(2,1)S(1)} %bitcast.18, ...), custom_call_target="tpu_custom_call" | custom-call | flops 536870912 | bytes 3670016 | tf_op jit(solution)/shard_map/pallas_call | solution.py:295
  28.4 3.0 %all-to-all-start.1 = ((bf16[32,16,512]{2,1,0:T(8,128)(2,1)}), bf16[32,16,512]{2,1,0:T(8,128)(2,1)S(1)}, u32[]{:S(2)}, u32[]{:S(2)}) async-start(bf16[32,16,512]{2,1,0:T(8,128)(2,1)} %bitcast.25), calls=%async_computation.1 | async-start | bytes 1048576 | tf_op jit(solution)/shard_map/all_to_all | solution.py:315
  32.6 14.4 %all-to-all-done.1 = bf16[32,16,512]{2,1,0:T(8,128)(2,1)S(1)} async-done(((bf16[32,16,512]{2,1,0:T(8,128)(2,1)}), bf16[32,16,512]{2,1,0:T(8,128)(2,1)S(1)}, u32[]{:S(2)}, u32[]{:S(2)}) %all-to-all-start.1) | async-done | bytes 524320 | tf_op jit(solution)/shard_map/all_to_all | solution.py:315
  47.0 2.6 %shard_map.107 = (bf16[256,512]{1,0:T(8,128)(2,1)}, f32[256,512]{1,0:T(8,128)}, bf16[256,512]{1,0:T(8,128)(2,1)}, bf16[256,512]{1,0:T(8,128)(2,1)S(1)}, bf16[512,512]{1,0:T(8,128)(2,1)}) custom-call(s32[2,4]{1,0:T(2,128)S(1)} %copy-done.8, bf16[256,512]{1,0:T(8,128)(2,1)S(1)} %get-tuple-element.73.hid, bf16[512,512]{1,0:T(8,128)(2,1)S(1)} %bitcast.19, ...), custom_call_target="tpu_custom_call" | custom-call | flops 536870912 | bytes 3670016 | tf_op jit(solution)/shard_map/pallas_call | solution.py:295
  49.6 3.0 %all-to-all-start.2 = ((bf16[32,16,512]{2,1,0:T(8,128)(2,1)}), bf16[32,16,512]{2,1,0:T(8,128)(2,1)S(1)}, u32[]{:S(2)}, u32[]{:S(2)}) async-start(bf16[32,16,512]{2,1,0:T(8,128)(2,1)} %bitcast.24), calls=%async_computation.2 | async-start | bytes 1048576 | tf_op jit(solution)/shard_map/all_to_all | solution.py:315
  53.9 14.3 %all-to-all-done.2 = bf16[32,16,512]{2,1,0:T(8,128)(2,1)S(1)} async-done(((bf16[32,16,512]{2,1,0:T(8,128)(2,1)}), bf16[32,16,512]{2,1,0:T(8,128)(2,1)S(1)}, u32[]{:S(2)}, u32[]{:S(2)}) %all-to-all-start.2) | async-done | bytes 524320 | tf_op jit(solution)/shard_map/all_to_all | solution.py:315
  68.2 3.4 %shard_map.109 = (bf16[256,512]{1,0:T(8,128)(2,1)}, bf16[256,512]{1,0:T(8,128)(2,1)}, bf16[512,512]{1,0:T(8,128)(2,1)}, f32[256,512]{1,0:T(8,128)}) custom-call(s32[2,4]{1,0:T(2,128)S(1)} %copy-done.8, bf16[256,512]{1,0:T(8,128)(2,1)S(1)} %get-tuple-element.77.hid, bf16[512,512]{1,0:T(8,128)(2,1)S(1)} %bitcast.20, ...), custom_call_target="tpu_custom_call" | custom-call | flops 1073741824 | bytes 3145728 | tf_op jit(solution)/shard_map/pallas_call | solution.py:295
  71.6 3.0 %all-to-all-start.3 = ((bf16[32,16,512]{2,1,0:T(8,128)(2,1)}), bf16[32,16,512]{2,1,0:T(8,128)(2,1)S(1)}, u32[]{:S(2)}, u32[]{:S(2)}) async-start(bf16[32,16,512]{2,1,0:T(8,128)(2,1)} %bitcast.23), calls=%async_computation.3 | async-start | bytes 1048576 | tf_op jit(solution)/shard_map/all_to_all | solution.py:315
  76.1 14.0 %all-to-all-done.3 = bf16[32,16,512]{2,1,0:T(8,128)(2,1)S(1)} async-done(((bf16[32,16,512]{2,1,0:T(8,128)(2,1)}), bf16[32,16,512]{2,1,0:T(8,128)(2,1)S(1)}, u32[]{:S(2)}, u32[]{:S(2)}) %all-to-all-start.3) | async-done | bytes 524320 | tf_op jit(solution)/shard_map/all_to_all | solution.py:315
  90.2 2.7 %shard_map.111 = (bf16[256,512]{1,0:T(8,128)(2,1)}, bf16[512,512]{1,0:T(8,128)(2,1)}, f32[256,512]{1,0:T(8,128)}) custom-call(s32[2,4]{1,0:T(2,128)S(1)} %copy-done.8, bf16[512,512]{1,0:T(8,128)(2,1)S(1)} %bitcast.17, f32[256,512]{1,0:T(8,128)S(1)} %get-tuple-element.85.before, f32[256,512]{1,0:T(8,128)S(1)} %get-tuple-element.86.slope, ...), custom_call_target="tpu_custom_call" | custom-call | flops 536870912 | bytes 2621440 | tf_op jit(solution)/shard_map/pallas_call | solution.py:295
  92.9 3.0 %all-to-all-start.4 = ((bf16[32,16,512]{2,1,0:T(8,128)(2,1)}), bf16[32,16,512]{2,1,0:T(8,128)(2,1)S(1)}, u32[]{:S(2)}, u32[]{:S(2)}) async-start(bf16[32,16,512]{2,1,0:T(8,128)(2,1)} %bitcast.22), calls=%async_computation.4 | async-start | bytes 1048576 | tf_op jit(solution)/shard_map/all_to_all | solution.py:315
  95.9 2.6 %shard_map.123 = (bf16[512,512]{1,0:T(8,128)(2,1)S(1)}, bf16[512,512]{1,0:T(8,128)(2,1)}) custom-call(s32[1]{0:T(128)} %bitcast.core, bf16[256,512]{1,0:T(8,128)(2,1)} %get-tuple-element.113.hid, bf16[256,512]{1,0:T(8,128)(2,1)} %get-tuple-element.114.agg, bf16[256,512]{1,0:T(8,128)(2,1)} %get-tuple-element.115.delta), custom_call_target="tpu_custom_call" | custom-call | flops 268435456 | bytes 2097152 | tf_op jit(solution)/shard_map/pallas_call | solution.py:295
  98.8 2.6 %shard_map.118 = (bf16[512,512]{1,0:T(8,128)(2,1)S(1)}, bf16[512,512]{1,0:T(8,128)(2,1)}) custom-call(s32[1]{0:T(128)} %bitcast.core, bf16[256,512]{1,0:T(8,128)(2,1)} %get-tuple-element.104.hid, bf16[256,512]{1,0:T(8,128)(2,1)} %get-tuple-element.105.agg, bf16[256,512]{1,0:T(8,128)(2,1)} %get-tuple-element.106.delta), custom_call_target="tpu_custom_call" | custom-call | flops 268435456 | bytes 2097152 | tf_op jit(solution)/shard_map/pallas_call | solution.py:295
  105.5 6.0 %all-to-all-done.4 = bf16[32,16,512]{2,1,0:T(8,128)(2,1)S(1)} async-done(((bf16[32,16,512]{2,1,0:T(8,128)(2,1)}), bf16[32,16,512]{2,1,0:T(8,128)(2,1)S(1)}, u32[]{:S(2)}, u32[]{:S(2)}) %all-to-all-start.4) | async-done | bytes 524320 | tf_op jit(solution)/shard_map/all_to_all | solution.py:315
  123.3 3.6 %shard_map.131 = (bf16[512,512]{1,0:T(8,128)(2,1)}, f32[256,512]{1,0:T(8,128)}) custom-call(s32[2,4]{1,0:T(2,128)S(1)} %copy-done.8, bf16[256,512]{1,0:T(8,128)(2,1)S(1)} %copy-done.3, bf16[2,4,128,128]{3,2,1,0:T(8,128)(2,1)S(1)} %get-tuple-element.69.val, bf16[3,512,512]{2,1,0:T(8,128)(2,1)} %ws.1, bf16[3,512,512]{2,1,0:T(8,128)(2,1)} %wn.1), custom_call_target="tpu_custom_call" | custom-call | flops 536870912 | bytes 2097152 | tf_op jit(solution)/shard_map/pallas_call | solution.py:295
  127.0 3.2 %all-to-all-start.5 = ((bf16[32,16,512]{2,1,0:T(8,128)(2,1)}), bf16[32,16,512]{2,1,0:T(8,128)(2,1)S(1)}, u32[]{:S(2)}, u32[]{:S(2)}) async-start(bf16[32,16,512]{2,1,0:T(8,128)(2,1)} %bitcast.21), calls=%async_computation.5 | async-start | bytes 1048576 | tf_op jit(solution)/shard_map/all_to_all | solution.py:315
  135.7 7.3 %collective-permute-done.30.refs_1_ = bf16[128,512]{1,0:T(8,128)(2,1)S(1)} collective-permute-done((bf16[128,512]{1,0:T(8,128)(2,1)S(1)}, bf16[128,512]{1,0:T(8,128)(2,1)S(1)}, u32[]{:S(2)}, u32[]{:S(2)}) %collective-permute-start.30) | collective-permute-done | bytes 131104 | tf_op jit(solution)/shard_map/ppermute | solution.py:347
  143.0 3.5 %collective-permute-start.31 = (bf16[128,512]{1,0:T(8,128)(2,1)S(1)}, bf16[128,512]{1,0:T(8,128)(2,1)S(1)}, u32[]{:S(2)}, u32[]{:S(2)}) collective-permute-start(bf16[128,512]{1,0:T(8,128)(2,1)S(1)} %shard_map.126.refs_0_), channel_id=1, source_target_pairs={{0,16},{8,24},{16,0},{24,8},{1,17},{9,25},{17,1},{25,9},{2,18},{10... | collective-permute-start | bytes 393224 | tf_op jit(solution)/shard_map/ppermute | solution.py:347
  152.8 2.5 %collective-permute-start.34 = (bf16[128,512]{1,0:T(8,128)(2,1)S(1)}, bf16[128,512]{1,0:T(8,128)(2,1)S(1)}, u32[]{:S(2)}, u32[]{:S(2)}) collective-permute-start(bf16[128,512]{1,0:T(8,128)(2,1)S(1)} %shard_map.127.refs_0_), channel_id=1, source_target_pairs={{0,6},{1,7},{2,4},{3,5},{4,2},{5,3},{6,0},{7,1},{8,14},{9,15},{10,... | collective-permute-start | bytes 393224 | tf_op jit(solution)/shard_map/ppermute | solution.py:324
  157.1 2.8 %collective-permute-done.2.refs_2_ = bf16[128,512]{1,0:T(8,128)(2,1)S(1)} collective-permute-done((bf16[128,512]{1,0:T(8,128)(2,1)S(1)}, bf16[128,512]{1,0:T(8,128)(2,1)S(1)}, u32[]{:S(2)}, u32[]{:S(2)}) %collective-permute-start.2) | collective-permute-done | bytes 131104 | tf_op jit(solution)/shard_map/ppermute | solution.py:324
  171.7 2.3 %collective-permute-done.5.refs_1_ = bf16[128,512]{1,0:T(8,128)(2,1)S(1)} collective-permute-done((bf16[128,512]{1,0:T(8,128)(2,1)S(1)}, bf16[128,512]{1,0:T(8,128)(2,1)S(1)}, u32[]{:S(2)}, u32[]{:S(2)}) %collective-permute-start.5) | collective-permute-done | bytes 131104 | tf_op jit(solution)/shard_map/ppermute | solution.py:347
  178.7 3.3 %collective-permute-done.8.refs_3_ = bf16[128,512]{1,0:T(8,128)(2,1)S(1)} collective-permute-done((bf16[128,512]{1,0:T(8,128)(2,1)S(1)}, bf16[128,512]{1,0:T(8,128)(2,1)S(1)}, u32[]{:S(2)}, u32[]{:S(2)}) %collective-permute-start.8) | collective-permute-done | bytes 131104 | tf_op jit(solution)/shard_map/ppermute | solution.py:324
  (116 shorter events, 63.2 us)
Async XLA Ops:
  2.8 22.9 %all-to-all-start = ((bf16[32,16,512]{2,1,0:T(8,128)(2,1)}), bf16[32,16,512]{2,1,0:T(8,128)(2,1)S(1)}, u32[]{:S(2)}, u32[]{:S(2)}) async-start(bf16[32,16,512]{2,1,0:T(8,128)(2,1)} %bitcast.26), calls=%async_computation | async-start | bytes 1048576 | tf_op jit(solution)/shard_map/all_to_all | solution.py:315
  28.4 18.6 %all-to-all-start.1 = ((bf16[32,16,512]{2,1,0:T(8,128)(2,1)}), bf16[32,16,512]{2,1,0:T(8,128)(2,1)S(1)}, u32[]{:S(2)}, u32[]{:S(2)}) async-start(bf16[32,16,512]{2,1,0:T(8,128)(2,1)} %bitcast.25), calls=%async_computation.1 | async-start | bytes 1048576 | tf_op jit(solution)/shard_map/all_to_all | solution.py:315
  49.6 18.6 %all-to-all-start.2 = ((bf16[32,16,512]{2,1,0:T(8,128)(2,1)}), bf16[32,16,512]{2,1,0:T(8,128)(2,1)S(1)}, u32[]{:S(2)}, u32[]{:S(2)}) async-start(bf16[32,16,512]{2,1,0:T(8,128)(2,1)} %bitcast.24), calls=%async_computation.2 | async-start | bytes 1048576 | tf_op jit(solution)/shard_map/all_to_all | solution.py:315
  71.6 18.6 %all-to-all-start.3 = ((bf16[32,16,512]{2,1,0:T(8,128)(2,1)}), bf16[32,16,512]{2,1,0:T(8,128)(2,1)S(1)}, u32[]{:S(2)}, u32[]{:S(2)}) async-start(bf16[32,16,512]{2,1,0:T(8,128)(2,1)} %bitcast.23), calls=%async_computation.3 | async-start | bytes 1048576 | tf_op jit(solution)/shard_map/all_to_all | solution.py:315
  92.9 18.6 %all-to-all-start.4 = ((bf16[32,16,512]{2,1,0:T(8,128)(2,1)}), bf16[32,16,512]{2,1,0:T(8,128)(2,1)S(1)}, u32[]{:S(2)}, u32[]{:S(2)}) async-start(bf16[32,16,512]{2,1,0:T(8,128)(2,1)} %bitcast.22), calls=%async_computation.4 | async-start | bytes 1048576 | tf_op jit(solution)/shard_map/all_to_all | solution.py:315
  98.5 18.5 %collective-permute-start.26 = (bf16[512,512]{1,0:T(8,128)(2,1)}, bf16[512,512]{1,0:T(8,128)(2,1)}, u32[]{:S(2)}, u32[]{:S(2)}) collective-permute-start(bf16[512,512]{1,0:T(8,128)(2,1)} %get-tuple-element.117), channel_id=1, source_target_pairs={{0,1},{1,0},{2,3},{3,2},{4,5},{5,4},{6,7},{7,6},{8,9},{9,8},{10,11... | collective-permute-start | bytes 1572872 | tf_op jit(solution)/shard_map/ppermute | solution.py:324
  101.5 30.5 %collective-permute-start.13 = (bf16[512,512]{1,0:T(8,128)(2,1)}, bf16[512,512]{1,0:T(8,128)(2,1)S(1)}, u32[]{:S(2)}, u32[]{:S(2)}) collective-permute-start(bf16[512,512]{1,0:T(8,128)(2,1)} %get-tuple-element.108), channel_id=1, source_target_pairs={{0,1},{1,0},{2,3},{3,2},{4,5},{5,4},{6,7},{7,6},{8,9},{9,8},{10,11... | collective-permute-start | bytes 1572872 | tf_op jit(solution)/shard_map/ppermute | solution.py:324
  117.0 29.8 %collective-permute-start = (bf16[512,512]{1,0:T(8,128)(2,1)}, bf16[512,512]{1,0:T(8,128)(2,1)S(1)}, u32[]{:S(2)}, u32[]{:S(2)}) collective-permute-start(bf16[512,512]{1,0:T(8,128)(2,1)} %get-tuple-element.99), channel_id=1, source_target_pairs={{0,1},{1,0},{2,3},{3,2},{4,5},{5,4},{6,7},{7,6},{8,9},{9,8},{10,11... | collective-permute-start | bytes 1572872 | tf_op jit(solution)/shard_map/ppermute | solution.py:324
  118.8 11.3 %collective-permute-start.27 = (bf16[128,512]{1,0:T(8,128)(2,1)}, bf16[128,512]{1,0:T(8,128)(2,1)S(1)}, u32[]{:S(2)}, u32[]{:S(2)}) collective-permute-start(bf16[128,512]{1,0:T(8,128)(2,1)} %get-tuple-element.119), channel_id=1, source_target_pairs={{0,2},{1,3},{2,0},{3,1},{4,6},{5,7},{6,4},{7,5},{8,10},{9,11},{10,... | collective-permute-start | bytes 393224 | tf_op jit(solution)/shard_map/ppermute | solution.py:324
  120.1 10.0 %collective-permute-start.28 = (bf16[128,512]{1,0:T(8,128)(2,1)}, bf16[128,512]{1,0:T(8,128)(2,1)S(1)}, u32[]{:S(2)}, u32[]{:S(2)}) collective-permute-start(bf16[128,512]{1,0:T(8,128)(2,1)} %get-tuple-element.120), channel_id=1, source_target_pairs={{0,4},{1,5},{2,6},{3,7},{4,0},{5,1},{6,2},{7,3},{8,12},{9,13},{10,... | collective-permute-start | bytes 393224 | tf_op jit(solution)/shard_map/ppermute | solution.py:324
  121.2 8.9 %collective-permute-start.29 = (bf16[128,512]{1,0:T(8,128)(2,1)S(1)}, bf16[128,512]{1,0:T(8,128)(2,1)S(1)}, u32[]{:S(2)}, u32[]{:S(2)}) collective-permute-start(bf16[128,512]{1,0:T(8,128)(2,1)S(1)} %get-tuple-element.121), channel_id=1, source_target_pairs={{0,6},{1,7},{2,4},{3,5},{4,2},{5,3},{6,0},{7,1},{8,14},{9,15},{10,... | collective-permute-start | bytes 393224 | tf_op jit(solution)/shard_map/ppermute | solution.py:324
  127.0 61.7 %all-to-all-start.5 = ((bf16[32,16,512]{2,1,0:T(8,128)(2,1)}), bf16[32,16,512]{2,1,0:T(8,128)(2,1)S(1)}, u32[]{:S(2)}, u32[]{:S(2)}) async-start(bf16[32,16,512]{2,1,0:T(8,128)(2,1)} %bitcast.21), calls=%async_computation.5 | async-start | bytes 1048576 | tf_op jit(solution)/shard_map/all_to_all | solution.py:315
  130.3 12.7 %collective-permute-start.30 = (bf16[128,512]{1,0:T(8,128)(2,1)S(1)}, bf16[128,512]{1,0:T(8,128)(2,1)S(1)}, u32[]{:S(2)}, u32[]{:S(2)}) collective-permute-start(bf16[128,512]{1,0:T(8,128)(2,1)S(1)} %shard_map.125.refs_0_), channel_id=1, source_target_pairs={{0,8},{8,0},{16,24},{24,16},{1,9},{9,1},{17,25},{25,17},{2,10},{10... | collective-permute-start | bytes 393224 | tf_op jit(solution)/shard_map/ppermute | solution.py:347
  132.2 14.4 %collective-permute-start.14 = (bf16[128,512]{1,0:T(8,128)(2,1)S(1)}, bf16[128,512]{1,0:T(8,128)(2,1)S(1)}, u32[]{:S(2)}, u32[]{:S(2)}) collective-permute-start(bf16[128,512]{1,0:T(8,128)(2,1)S(1)} %get-tuple-element.110), channel_id=1, source_target_pairs={{0,2},{1,3},{2,0},{3,1},{4,6},{5,7},{6,4},{7,5},{8,10},{9,11},{10,... | collective-permute-start | bytes 393224 | tf_op jit(solution)/shard_map/ppermute | solution.py:324
  133.7 12.9 %collective-permute-start.15 = (bf16[128,512]{1,0:T(8,128)(2,1)S(1)}, bf16[128,512]{1,0:T(8,128)(2,1)S(1)}, u32[]{:S(2)}, u32[]{:S(2)}) collective-permute-start(bf16[128,512]{1,0:T(8,128)(2,1)S(1)} %get-tuple-element.111), channel_id=1, source_target_pairs={{0,4},{1,5},{2,6},{3,7},{4,0},{5,1},{6,2},{7,3},{8,12},{9,13},{10,... | collective-permute-start | bytes 393224 | tf_op jit(solution)/shard_map/ppermute | solution.py:324
  135.1 11.4 %collective-permute-start.16 = (bf16[128,512]{1,0:T(8,128)(2,1)S(1)}, bf16[128,512]{1,0:T(8,128)(2,1)S(1)}, u32[]{:S(2)}, u32[]{:S(2)}) collective-permute-start(bf16[128,512]{1,0:T(8,128)(2,1)S(1)} %get-tuple-element.112), channel_id=1, source_target_pairs={{0,6},{1,7},{2,4},{3,5},{4,2},{5,3},{6,0},{7,1},{8,14},{9,15},{10,... | collective-permute-start | bytes 393224 | tf_op jit(solution)/shard_map/ppermute | solution.py:324
  143.0 9.7 %collective-permute-start.31 = (bf16[128,512]{1,0:T(8,128)(2,1)S(1)}, bf16[128,512]{1,0:T(8,128)(2,1)S(1)}, u32[]{:S(2)}, u32[]{:S(2)}) collective-permute-start(bf16[128,512]{1,0:T(8,128)(2,1)S(1)} %shard_map.126.refs_0_), channel_id=1, source_target_pairs={{0,16},{8,24},{16,0},{24,8},{1,17},{9,25},{17,1},{25,9},{2,18},{10... | collective-permute-start | bytes 393224 | tf_op jit(solution)/shard_map/ppermute | solution.py:347
  146.7 8.5 %collective-permute-start.17 = (bf16[128,512]{1,0:T(8,128)(2,1)S(1)}, bf16[128,512]{1,0:T(8,128)(2,1)S(1)}, u32[]{:S(2)}, u32[]{:S(2)}) collective-permute-start(bf16[128,512]{1,0:T(8,128)(2,1)S(1)} %shard_map.120.refs_0_), channel_id=1, source_target_pairs={{0,8},{8,0},{16,24},{24,16},{1,9},{9,1},{17,25},{25,17},{2,10},{10... | collective-permute-start | bytes 393224 | tf_op jit(solution)/shard_map/ppermute | solution.py:347
  147.0 8.9 %collective-permute-start.1 = (bf16[128,512]{1,0:T(8,128)(2,1)S(1)}, bf16[128,512]{1,0:T(8,128)(2,1)S(1)}, u32[]{:S(2)}, u32[]{:S(2)}) collective-permute-start(bf16[128,512]{1,0:T(8,128)(2,1)S(1)} %get-tuple-element.101), channel_id=1, source_target_pairs={{0,2},{1,3},{2,0},{3,1},{4,6},{5,7},{6,4},{7,5},{8,10},{9,11},{10,... | collective-permute-start | bytes 393224 | tf_op jit(solution)/shard_map/ppermute | solution.py:324
  149.0 10.8 %collective-permute-start.2 = (bf16[128,512]{1,0:T(8,128)(2,1)S(1)}, bf16[128,512]{1,0:T(8,128)(2,1)S(1)}, u32[]{:S(2)}, u32[]{:S(2)}) collective-permute-start(bf16[128,512]{1,0:T(8,128)(2,1)S(1)} %get-tuple-element.102), channel_id=1, source_target_pairs={{0,4},{1,5},{2,6},{3,7},{4,0},{5,1},{6,2},{7,3},{8,12},{9,13},{10,... | collective-permute-start | bytes 393224 | tf_op jit(solution)/shard_map/ppermute | solution.py:324
  150.5 9.3 %collective-permute-start.3 = (bf16[128,512]{1,0:T(8,128)(2,1)S(1)}, bf16[128,512]{1,0:T(8,128)(2,1)S(1)}, u32[]{:S(2)}, u32[]{:S(2)}) collective-permute-start(bf16[128,512]{1,0:T(8,128)(2,1)S(1)} %get-tuple-element.103), channel_id=1, source_target_pairs={{0,6},{1,7},{2,4},{3,5},{4,2},{5,3},{6,0},{7,1},{8,14},{9,15},{10,... | collective-permute-start | bytes 393224 | tf_op jit(solution)/shard_map/ppermute | solution.py:324
  152.8 9.1 %collective-permute-start.34 = (bf16[128,512]{1,0:T(8,128)(2,1)S(1)}, bf16[128,512]{1,0:T(8,128)(2,1)S(1)}, u32[]{:S(2)}, u32[]{:S(2)}) collective-permute-start(bf16[128,512]{1,0:T(8,128)(2,1)S(1)} %shard_map.127.refs_0_), channel_id=1, source_target_pairs={{0,6},{1,7},{2,4},{3,5},{4,2},{5,3},{6,0},{7,1},{8,14},{9,15},{10,... | collective-permute-start | bytes 393224 | tf_op jit(solution)/shard_map/ppermute | solution.py:324
  178.2 8.9 %collective-permute-start.23 = (bf16[128,512]{1,0:T(8,128)(2,1)S(1)}, bf16[128,512]{1,0:T(8,128)(2,1)S(1)}, u32[]{:S(2)}, u32[]{:S(2)}) collective-permute-start(bf16[128,512]{1,0:T(8,128)(2,1)S(1)} %collective-permute-done.19.refs_1_), channel_id=1, source_target_pairs={{0,1},{1,0},{2,3},{3,2},{4,5},{5,4},{6,7},{7,6},{8,9},{9,8},{10,11... | collective-permute-start | bytes 393224 | tf_op jit(solution)/shard_map/ppermute | solution.py:324
  178.2 11.6 %collective-permute-start.9 = (bf16[128,512]{1,0:T(8,128)(2,1)S(1)}, bf16[128,512]{1,0:T(8,128)(2,1)S(1)}, u32[]{:S(2)}, u32[]{:S(2)}) collective-permute-start(bf16[128,512]{1,0:T(8,128)(2,1)S(1)} %shard_map.117.refs_0_), channel_id=1, source_target_pairs={{0,1},{1,0},{2,3},{3,2},{4,5},{5,4},{6,7},{7,6},{8,9},{9,8},{10,11... | collective-permute-start | bytes 393224 | tf_op jit(solution)/shard_map/ppermute | solution.py:324
  (30 other events, 153.3 us)

commit v9 on v8

--- a/solution.py
+++ b/solution.py
@@ -96,6 +96,14 @@
     go.finish()
 
 
+def store_kernel(*refs):
+    count = (len(refs) - 1) // 2
+    go = Copies(refs[-1])
+    for source, target in zip(refs[:count], refs[count:-1]):
+        go.store(source, target)
+    go.finish()
+
+
 def pre_activation(cols, hid, arr, val, ws, wn, agg_v, ext_v):
     tiles, blocks, tile, _ = val.shape
     own = hid.shape[0] // tile
@@ -112,20 +120,16 @@
 
 
 def middle_kernel(
-    cols, hid, arr, val, ws, wn, col, agg_out, slope_out, next_out, next_near, send_out,
-    ext_v, agg_v, slope_v, send_v, sems,
+    cols, hid, arr, val, ws, wn, col, agg, slope, after, send_out, ext_v, send_v, sems
 ):
     go = Copies(sems)
-    pre = pre_activation(cols, hid, arr, val, ws, wn, agg_v, ext_v)
-    go.store(agg_v, agg_out)
+    pre = pre_activation(cols, hid, arr, val, ws, wn, agg, ext_v)
     sigma = jax.nn.sigmoid(pre)
     hidden = (pre * sigma).astype(jnp.bfloat16)
-    next_near[...] = hidden
-    go.store(next_near, next_out)
-    slope_v[...] = sigma * (1.0 + pre * (1.0 - sigma))
-    go.store(slope_v, slope_out)
+    after[...] = hidden
     send_v[...] = pick_rows(col[...], hidden)
     go.store(send_v, send_out)
+    slope[...] = sigma * (1.0 + pre * (1.0 - sigma))
     go.finish()
 
 
@@ -150,8 +154,8 @@
 
 
 def last_kernel(
-    cols, hid, arr, val, ws, wn, cot, agg_out, delta_out, halo_out, base_out,
-    ext_v, agg_v, delta_v, halo_v, base_v, acc_v, sems,
+    cols, hid, arr, val, ws, wn, cot, agg_out, delta_out, halo_out, base,
+    ext_v, agg_v, delta_v, halo_v, acc_v, sems,
 ):
     go = Copies(sems)
     pre = pre_activation(cols, hid, arr, val, ws, wn, agg_v, ext_v)
@@ -161,8 +165,7 @@
     delta = (cot[...].astype(jnp.float32) * slope).astype(jnp.bfloat16)
     delta_v[...] = delta
     go.store(delta_v, delta_out)
-    spread_back(go, delta, cols, val, ws, wn, halo_out, base_v, halo_v, acc_v)
-    go.store(base_v, base_out)
+    spread_back(go, delta, cols, val, ws, wn, halo_out, base, halo_v, acc_v)
     go.finish()
 
 
@@ -173,15 +176,14 @@
 
 
 def backward_kernel(
-    cols, arr, before, slope, row, val, ws, wn, delta_out, halo_out, base_out,
-    delta_v, halo_v, base_v, acc_v, sems,
+    cols, arr, before, slope, row, val, ws, wn, delta_out, halo_out, base,
+    delta_v, halo_v, acc_v, sems,
 ):
     go = Copies(sems)
     delta = delta_of(arr, before, slope, row)
     delta_v[...] = delta
     go.store(delta_v, delta_out)
-    spread_back(go, delta, cols, val, ws, wn, halo_out, base_v, halo_v, acc_v)
-    go.store(base_v, base_out)
+    spread_back(go, delta, cols, val, ws, wn, halo_out, base, halo_v, acc_v)
     go.finish()
 
 
@@ -202,14 +204,6 @@
     go.finish()
 
 
-def final_kernel(arr, before, row, grad_out, grad_v, sems):
-    go = Copies(sems)
-    back = return_rows(row[...], arr[...], before.shape[0])
-    grad_v[...] = (before[...] + back).astype(jnp.bfloat16)
-    go.store(grad_v, grad_out)
-    go.finish()
-
-
 def products(core, hid_v, agg_v, delta, pairs):
     for side, target in ((1 - core, pairs[0]), (core, pairs[1])):
         for n, source in enumerate((hid_v, agg_v)):
@@ -244,29 +238,42 @@
     refs[-2][...] = total.astype(jnp.bfloat16)
 
 
-def place_kernel(layers, count, where, *refs):
-    mine, other = refs[:count], refs[count : 2 * count]
-    self_out, neigh_out, sems = refs[-3:]
-    size = mine[0].shape[0] // len(layers)
-    for core, outs in enumerate(((self_out, neigh_out), (neigh_out, self_out))):
+def place_copies(layers, count, where, sources, targets, sems, step):
+    size = sources[0].shape[0] // len(layers)
+    for core in range(2):
 
         @pl.when(where[0] == core)
-        def _(outs=outs):
-            copies = []
-            for m, source in enumerate((*mine, *other)):
+        def _(outs=targets if core == 0 else targets[::-1]):
+            used = 0
+            for m, source in enumerate(sources):
                 to = pl.multiple_of((where[1] ^ (m % count)) * size, size)
                 for n, layer in enumerate(layers):
-                    copies.append(
-                        pltpu.make_async_copy(
-                            source.at[pl.ds(n * size, size)],
-                            outs[m // count].at[layer, pl.ds(to, size)],
-                            sems.at[len(copies)],
-                        )
+                    copy = pltpu.make_async_copy(
+                        source.at[pl.ds(n * size, size)],
+                        outs[m // count].at[layer, pl.ds(to, size)],
+                        sems.at[used],
                     )
-            for copy in copies:
-                copy.start()
-            for copy in copies:
-                copy.wait()
+                    used += 1
+                    getattr(copy, step)()
+
+
+def place_kernel(layers, count, where, *refs):
+    for step in ("start", "wait"):
+        place_copies(layers, count, where, refs[: 2 * count], refs[-3:-1], refs[-1], step)
+
+
+def end_kernel(layers, count, where, *refs):
+    ops = 1 + 2 * count
+    arr, before, row = refs[ops - 1 : ops + 2]
+    self_out, neigh_out, grad, grad_v, sems = refs[-5:]
+    source = refs[: 2 * count]
+    place_copies(layers, count, where, source, (self_out, neigh_out), sems, "start")
+    back = return_rows(row[...], arr[...], before.shape[0])
+    grad_v[...] = (before[...] + back).astype(jnp.bfloat16)
+    last = pltpu.make_async_copy(grad_v, grad, sems.at[2 * count * len(layers)])
+    last.start()
+    place_copies(layers, count, where, source, (self_out, neigh_out), sems, "wait")
+    last.wait()
 
 
 def per_device(
@@ -380,6 +387,11 @@
             ],
         )
 
+    def store(*arrays):
+        return call(
+            store_kernel, [(a, near) for a in arrays], [(a.shape, a.dtype, away) for a in arrays]
+        )
+
     cols = (block_col, scalars)
     row, col, send = call(
         first_kernel,
@@ -393,20 +405,21 @@
     ws, wn, hidden, val = load(0, *weights, features, block_val)
     hiddens, aggregates, slopes = [features], [], []
     for layer in range(layers - 1):
-        aggregate, slope, kept, hidden, send = call(
+        aggregate, slope, hidden, send = call(
             middle_kernel,
             (
                 cols, (hidden, near), (arrived, near), (val, near), (ws, near), (wn, near),
                 (col, near),
             ),
-            ((*rows, away), (*rows32, away), (*rows, away), (*rows, near), (*halo_rows, away)),
-            (ext, rows, rows32, halo_rows),
+            ((*rows, near), (*rows32, near), (*rows, near), (*halo_rows, away)),
+            (ext, halo_rows),
             flops=big,
         )
+        arrived = exchange(send)
+        aggregate, slope, kept = store(aggregate, slope, hidden)
         hiddens.append(kept)
         aggregates.append(aggregate)
         slopes.append(slope)
-        arrived = exchange(send)
         last = layer + 2 == layers
         ws, wn, *cot = load(layer + 1, *weights, *((cotangent,) if last else ()))
     aggregate, delta, outgoing, base = call(
@@ -415,8 +428,8 @@
             cols, (hidden, near), (arrived, near), (val, near), (ws, near), (wn, near),
             (cot[0], near),
         ),
-        ((*rows, away), (*rows, away), (*halo_rows, away), (*rows32, away)),
-        (ext, rows, rows, halo_rows, rows32, acc),
+        ((*rows, away), (*rows, away), (*halo_rows, away), (*rows32, near)),
+        (ext, rows, rows, halo_rows, acc),
         flops=2 * big,
     )
     aggregates.append(aggregate)
@@ -439,14 +452,15 @@
         if not layer:
             break
         more = weights if below else (hiddens[0], aggregates[0])
+        (base,) = store(base)
         base, slope, *more = load(below, base, slopes[below], *more)
         back = ((arrived, near), (base, near), (slope, near), (row, near))
         if below:
             delta, outgoing, base = call(
                 backward_kernel,
                 (cols, *back, (val, near), *((a, near) for a in more)),
-                ((*rows, away), (*halo_rows, away), (*rows32, away)),
-                (rows, halo_rows, rows32, acc),
+                ((*rows, away), (*halo_rows, away), (*rows32, near)),
+                (rows, halo_rows, acc),
                 flops=big,
             )
         else:
@@ -465,14 +479,26 @@
                 flops=big,
             )
     (base,) = load(0, base)
-    (grad,) = call(
-        final_kernel, ((arrived, near), (base, near), (row, near)), ((*rows, away),), (rows,)
-    )
     outs = ()
     for layer, piece in zip(reversed(range(layers)), sums):
         mine, other = gather(piece)
-        outs = place((layer,), mine, other, outs)
-    return (*outs, grad)
+        if layer:
+            outs = place((layer,), mine, other, outs)
+        else:
+            args = (
+                (where, scalars), *((a, near) for a in (*mine, *other)),
+                (arrived, near), (base, near), (row, near), *((o, away) for o in outs),
+            )
+            first = len(args) - len(outs)
+            outs = call(
+                functools.partial(end_kernel, (0,), chips),
+                args,
+                (*((self_weight.shape, bf16, away),) * 2, (*rows, away)),
+                (rows,),
+                2 * chips + 1,
+                alias={first: 0, first + 1: 1} if len(outs) else None,
+            )
+    return tuple(outs)
 
 
 def solution(mesh):

time: 193 us -> 198 us (1.026)
  local copies, waits for them, and re-layouts: 6.81 us -> 16.3 us
  waiting for transfers between devices: 88.6 us -> 83 us
  Pallas kernels: 41 us -> 43.5 us
    unnamed x18 -> x46, local copies, waits for them, and re-layouts: 6.81 us -> 16.3 us
    all_to_all x6, waiting for transfers between devices: 62.9 us -> 55.8 us  [exchange(): return lax.all_to_all(sent, AXES, 0, 0, tiled=True).reshape(halo, width)]
    ppermute x6, waiting for transfers between devices: 14.2 us -> 18 us  [chip_sum(): got = lax.ppermute(total, 'gx', perm)]
    pallas_call x31 -> x34, Pallas kernels: 41 us -> 43.5 us  [call(): pl.pallas_call(body, in_specs=[pl.BlockSpec(memory_space=space) for _, sp...]
    ppermute x33, waiting for transfers between devices: 11.5 us -> 9.18 us  [flip(): return lax.ppermute(array, 'gy', [(j, j ^ mask) for j in range(inner)])]
    ppermute x33, starting transfers between devices: 22.4 us -> 20.4 us  [flip(): return lax.ppermute(array, 'gy', [(j, j ^ mask) for j in range(inner)])]
  transfers between devices with their start and end apart: 45 -> 45, of which waited for: 16 -> 17; matrix products, arithmetic and copies ran while one was open for 0% -> 0% of each run, Pallas kernels for 14% -> 15%
where the time goes in v9:
time: 198 us; the launch traced here: 197 us
  waiting for transfers between devices  83 us (42%)
  starting transfers between devices  52.5 us (27%)
  Pallas kernels  43.5 us (22%)
  local copies, waits for them, and re-layouts  16.3 us (8%)
    all_to_all x6, waiting for transfers between devices, exchange(): return lax.all_to_all(sent, AXES, 0, 0, tiled=True).reshape(halo, width)  55.8 us
    pallas_call x34, Pallas kernels, call(): pl.pallas_call(body, in_specs=[pl.BlockSpec(memory_space=space) for _, sp...  43.5 us
    all_to_all x6, starting transfers between devices, exchange(): return lax.all_to_all(sent, AXES, 0, 0, tiled=True).reshape(halo, width)  22.4 us
    ppermute x33, starting transfers between devices, flip(): return lax.ppermute(array, 'gy', [(j, j ^ mask) for j in range(inner)])  20.4 us
    ppermute x6, waiting for transfers between devices, chip_sum(): got = lax.ppermute(total, 'gx', perm)  18 us
    unnamed x46, local copies, waits for them, and re-layouts  16.3 us
    ppermute x6, starting transfers between devices, chip_sum(): got = lax.ppermute(total, 'gx', perm)  9.7 us
    ppermute x33, waiting for transfers between devices, flip(): return lax.ppermute(array, 'gy', [(j, j ^ mask) for j in range(inner)])  9.18 us
  transfers between devices with their start and end apart: 45, of which 17 were waited for; matrix products, arithmetic and copies ran while one was open for 0% of the time, Pallas kernels for 15%

profile of v9, /device:TPU:0, one launch (start us, length us, event | category | flops | bytes accessed | tf_op | source)
XLA Modules:
  0.0 196.7 jit_solution(16921199380542614904)
XLA Ops:
  2.8 7.3 %all-to-all-start = ((bf16[32,16,512]{2,1,0:T(8,128)(2,1)}), bf16[32,16,512]{2,1,0:T(8,128)(2,1)S(1)}, u32[]{:S(2)}, u32[]{:S(2)}) async-start(bf16[32,16,512]{2,1,0:T(8,128)(2,1)} %bitcast.26), calls=%async_computation | async-start | bytes 1048576 | tf_op jit(solution)/shard_map/all_to_all | solution.py:322
  11.5 14.2 %all-to-all-done = bf16[32,16,512]{2,1,0:T(8,128)(2,1)S(1)} async-done(((bf16[32,16,512]{2,1,0:T(8,128)(2,1)}), bf16[32,16,512]{2,1,0:T(8,128)(2,1)S(1)}, u32[]{:S(2)}, u32[]{:S(2)}) %all-to-all-start) | async-done | bytes 524320 | tf_op jit(solution)/shard_map/all_to_all | solution.py:322
  25.7 2.6 %shard_map.105 = (bf16[256,512]{1,0:T(8,128)(2,1)S(1)}, f32[256,512]{1,0:T(8,128)S(1)}, bf16[256,512]{1,0:T(8,128)(2,1)S(1)}, bf16[512,512]{1,0:T(8,128)(2,1)}) custom-call(s32[2,4]{1,0:T(2,128)S(1)} %copy-done.18, bf16[256,512]{1,0:T(8,128)(2,1)S(1)} %get-tuple-element.69.hid, bf16[512,512]{1,0:T(8,128)(2,1)S(1)} %bitcast.18, ...), custom_call_target="tpu_custom_call" | custom-call | flops 536870912 | bytes 3145728 | tf_op jit(solution)/shard_map/pallas_call | solution.py:302
  29.1 3.0 %all-to-all-start.1 = ((bf16[32,16,512]{2,1,0:T(8,128)(2,1)}), bf16[32,16,512]{2,1,0:T(8,128)(2,1)S(1)}, u32[]{:S(2)}, u32[]{:S(2)}) async-start(bf16[32,16,512]{2,1,0:T(8,128)(2,1)} %bitcast.25), calls=%async_computation.1 | async-start | bytes 1048576 | tf_op jit(solution)/shard_map/all_to_all | solution.py:322
  33.3 14.4 %all-to-all-done.1 = bf16[32,16,512]{2,1,0:T(8,128)(2,1)S(1)} async-done(((bf16[32,16,512]{2,1,0:T(8,128)(2,1)}), bf16[32,16,512]{2,1,0:T(8,128)(2,1)S(1)}, u32[]{:S(2)}, u32[]{:S(2)}) %all-to-all-start.1) | async-done | bytes 524320 | tf_op jit(solution)/shard_map/all_to_all | solution.py:322
  47.7 2.6 %shard_map.107 = (bf16[256,512]{1,0:T(8,128)(2,1)S(1)}, f32[256,512]{1,0:T(8,128)S(1)}, bf16[256,512]{1,0:T(8,128)(2,1)S(1)}, bf16[512,512]{1,0:T(8,128)(2,1)}) custom-call(s32[2,4]{1,0:T(2,128)S(1)} %copy-done.18, bf16[256,512]{1,0:T(8,128)(2,1)S(1)} %get-tuple-element.75.hid.refs_2_, bf16[512,512]{1,0:T(8,128)(2,1)S(1)} %bitcast.19, ...), custom_call_target="tpu_custom_call" | custom-call | flops 536870912 | bytes 3145728 | tf_op jit(solution)/shard_map/pallas_call | solution.py:302
  51.7 3.0 %all-to-all-start.2 = ((bf16[32,16,512]{2,1,0:T(8,128)(2,1)}), bf16[32,16,512]{2,1,0:T(8,128)(2,1)S(1)}, u32[]{:S(2)}, u32[]{:S(2)}) async-start(bf16[32,16,512]{2,1,0:T(8,128)(2,1)} %bitcast.24), calls=%async_computation.2 | async-start | bytes 1048576 | tf_op jit(solution)/shard_map/all_to_all | solution.py:322
  57.7 12.6 %all-to-all-done.2 = bf16[32,16,512]{2,1,0:T(8,128)(2,1)S(1)} async-done(((bf16[32,16,512]{2,1,0:T(8,128)(2,1)}), bf16[32,16,512]{2,1,0:T(8,128)(2,1)S(1)}, u32[]{:S(2)}, u32[]{:S(2)}) %all-to-all-start.2) | async-done | bytes 524320 | tf_op jit(solution)/shard_map/all_to_all | solution.py:322
  72.4 3.2 %shard_map.109 = (bf16[256,512]{1,0:T(8,128)(2,1)}, bf16[256,512]{1,0:T(8,128)(2,1)}, bf16[512,512]{1,0:T(8,128)(2,1)}, f32[256,512]{1,0:T(8,128)S(1)}) custom-call(s32[2,4]{1,0:T(2,128)S(1)} %copy-done.18, bf16[256,512]{1,0:T(8,128)(2,1)S(1)} %copy-done.11, bf16[512,512]{1,0:T(8,128)(2,1)S(1)} %bitcast.20, ...), custom_call_target="tpu_custom_call" | custom-call | flops 1073741824 | bytes 3145728 | tf_op jit(solution)/shard_map/pallas_call | solution.py:302
  75.6 3.0 %all-to-all-start.3 = ((bf16[32,16,512]{2,1,0:T(8,128)(2,1)}), bf16[32,16,512]{2,1,0:T(8,128)(2,1)S(1)}, u32[]{:S(2)}, u32[]{:S(2)}) async-start(bf16[32,16,512]{2,1,0:T(8,128)(2,1)} %bitcast.23), calls=%async_computation.3 | async-start | bytes 1048576 | tf_op jit(solution)/shard_map/all_to_all | solution.py:322
  83.7 10.5 %all-to-all-done.3 = bf16[32,16,512]{2,1,0:T(8,128)(2,1)S(1)} async-done(((bf16[32,16,512]{2,1,0:T(8,128)(2,1)}), bf16[32,16,512]{2,1,0:T(8,128)(2,1)S(1)}, u32[]{:S(2)}, u32[]{:S(2)}) %all-to-all-start.3) | async-done | bytes 524320 | tf_op jit(solution)/shard_map/all_to_all | solution.py:322
  96.3 2.5 %shard_map.113 = (bf16[256,512]{1,0:T(8,128)(2,1)}, bf16[512,512]{1,0:T(8,128)(2,1)}, f32[256,512]{1,0:T(8,128)S(1)}) custom-call(s32[2,4]{1,0:T(2,128)S(1)} %copy-done.18, bf16[512,512]{1,0:T(8,128)(2,1)S(1)} %bitcast.17, f32[256,512]{1,0:T(8,128)S(1)} %get-tuple-element.89.before, f32[256,512]{1,0:T(8,128)S(1)} %get-tuple-element.90.slope, ...), custom_call_target="tpu_custom_call" | custom-call | flops 536870912 | bytes 2621440 | tf_op jit(solution)/shard_map/pallas_call | solution.py:302
  98.8 3.0 %all-to-all-start.4 = ((bf16[32,16,512]{2,1,0:T(8,128)(2,1)}), bf16[32,16,512]{2,1,0:T(8,128)(2,1)S(1)}, u32[]{:S(2)}, u32[]{:S(2)}) async-start(bf16[32,16,512]{2,1,0:T(8,128)(2,1)} %bitcast.22), calls=%async_computation.4 | async-start | bytes 1048576 | tf_op jit(solution)/shard_map/all_to_all | solution.py:322
  101.8 2.6 %shard_map.129 = (bf16[512,512]{1,0:T(8,128)(2,1)S(1)}, bf16[512,512]{1,0:T(8,128)(2,1)}) custom-call(s32[1]{0:T(128)} %bitcast.core, bf16[256,512]{1,0:T(8,128)(2,1)} %get-tuple-element.122.hid, bf16[256,512]{1,0:T(8,128)(2,1)} %get-tuple-element.123.agg, bf16[256,512]{1,0:T(8,128)(2,1)} %get-tuple-element.124.delta), custom_call_target="tpu_custom_call" | custom-call | flops 268435456 | bytes 2097152 | tf_op jit(solution)/shard_map/pallas_call | solution.py:302
  105.8 2.6 %shard_map.124 = (bf16[512,512]{1,0:T(8,128)(2,1)S(1)}, bf16[512,512]{1,0:T(8,128)(2,1)}) custom-call(s32[1]{0:T(128)} %bitcast.core, bf16[256,512]{1,0:T(8,128)(2,1)} %get-tuple-element.113.hid, bf16[256,512]{1,0:T(8,128)(2,1)} %get-tuple-element.114.agg, bf16[256,512]{1,0:T(8,128)(2,1)} %get-tuple-element.115.delta), custom_call_target="tpu_custom_call" | custom-call | flops 268435456 | bytes 2097152 | tf_op jit(solution)/shard_map/pallas_call | solution.py:302
  113.2 4.2 %all-to-all-done.4 = bf16[32,16,512]{2,1,0:T(8,128)(2,1)S(1)} async-done(((bf16[32,16,512]{2,1,0:T(8,128)(2,1)}), bf16[32,16,512]{2,1,0:T(8,128)(2,1)S(1)}, u32[]{:S(2)}, u32[]{:S(2)}) %all-to-all-start.4) | async-done | bytes 524320 | tf_op jit(solution)/shard_map/all_to_all | solution.py:322
  129.3 3.6 %shard_map.122 = (bf16[512,512]{1,0:T(8,128)(2,1)}, f32[256,512]{1,0:T(8,128)}) custom-call(s32[2,4]{1,0:T(2,128)S(1)} %copy-done.18, bf16[256,512]{1,0:T(8,128)(2,1)S(1)} %copy-done.13, bf16[2,4,128,128]{3,2,1,0:T(8,128)(2,1)S(1)} %get-tuple-element.71.val, bf16[3,512,512]{2,1,0:T(8,128)(2,1)} %ws.1, bf16[3,512,512]{2,1,0:T(8,128)(2,1)} %wn.1), custom_call_target="tpu_custom_call" | custom-call | flops 536870912 | bytes 2097152 | tf_op jit(solution)/shard_map/pallas_call | solution.py:302
  132.9 3.2 %all-to-all-start.5 = ((bf16[32,16,512]{2,1,0:T(8,128)(2,1)}), bf16[32,16,512]{2,1,0:T(8,128)(2,1)S(1)}, u32[]{:S(2)}, u32[]{:S(2)}) async-start(bf16[32,16,512]{2,1,0:T(8,128)(2,1)} %bitcast.21), calls=%async_computation.5 | async-start | bytes 1048576 | tf_op jit(solution)/shard_map/all_to_all | solution.py:322
  141.6 7.3 %collective-permute-done.30.refs_1_ = bf16[128,512]{1,0:T(8,128)(2,1)S(1)} collective-permute-done((bf16[128,512]{1,0:T(8,128)(2,1)S(1)}, bf16[128,512]{1,0:T(8,128)(2,1)S(1)}, u32[]{:S(2)}, u32[]{:S(2)}) %collective-permute-start.30) | collective-permute-done | bytes 131104 | tf_op jit(solution)/shard_map/ppermute | solution.py:354
  149.0 3.5 %collective-permute-start.31 = (bf16[128,512]{1,0:T(8,128)(2,1)S(1)}, bf16[128,512]{1,0:T(8,128)(2,1)S(1)}, u32[]{:S(2)}, u32[]{:S(2)}) collective-permute-start(bf16[128,512]{1,0:T(8,128)(2,1)S(1)} %shard_map.132.refs_0_), channel_id=1, source_target_pairs={{0,16},{8,24},{16,0},{24,8},{1,17},{9,25},{17,1},{25,9},{2,18},{10... | collective-permute-start | bytes 393224 | tf_op jit(solution)/shard_map/ppermute | solution.py:354
  162.2 3.8 %collective-permute-start.4 = (bf16[128,512]{1,0:T(8,128)(2,1)S(1)}, bf16[128,512]{1,0:T(8,128)(2,1)S(1)}, u32[]{:S(2)}, u32[]{:S(2)}) collective-permute-start(bf16[128,512]{1,0:T(8,128)(2,1)S(1)} %shard_map.119.refs_0_), channel_id=1, source_target_pairs={{0,8},{8,0},{16,24},{24,16},{1,9},{9,1},{17,25},{25,17},{2,10},{10... | collective-permute-start | bytes 393224 | tf_op jit(solution)/shard_map/ppermute | solution.py:354
  169.0 3.8 %collective-permute-done.18.refs_1_ = bf16[128,512]{1,0:T(8,128)(2,1)S(1)} collective-permute-done((bf16[128,512]{1,0:T(8,128)(2,1)S(1)}, bf16[128,512]{1,0:T(8,128)(2,1)S(1)}, u32[]{:S(2)}, u32[]{:S(2)}) %collective-permute-start.18) | collective-permute-done | bytes 131104 | tf_op jit(solution)/shard_map/ppermute | solution.py:354
  175.2 3.6 %collective-permute-done.5.refs_1_ = bf16[128,512]{1,0:T(8,128)(2,1)S(1)} collective-permute-done((bf16[128,512]{1,0:T(8,128)(2,1)S(1)}, bf16[128,512]{1,0:T(8,128)(2,1)S(1)}, u32[]{:S(2)}, u32[]{:S(2)}) %collective-permute-start.5) | collective-permute-done | bytes 131104 | tf_op jit(solution)/shard_map/ppermute | solution.py:354
  184.6 3.0 %collective-permute-done.8.refs_3_ = bf16[128,512]{1,0:T(8,128)(2,1)S(1)} collective-permute-done((bf16[128,512]{1,0:T(8,128)(2,1)S(1)}, bf16[128,512]{1,0:T(8,128)(2,1)S(1)}, u32[]{:S(2)}, u32[]{:S(2)}) %collective-permute-start.8) | collective-permute-done | bytes 131104 | tf_op jit(solution)/shard_map/ppermute | solution.py:331
  (147 shorter events, 72.2 us)
Async XLA Ops:
  2.8 22.9 %all-to-all-start = ((bf16[32,16,512]{2,1,0:T(8,128)(2,1)}), bf16[32,16,512]{2,1,0:T(8,128)(2,1)S(1)}, u32[]{:S(2)}, u32[]{:S(2)}) async-start(bf16[32,16,512]{2,1,0:T(8,128)(2,1)} %bitcast.26), calls=%async_computation | async-start | bytes 1048576 | tf_op jit(solution)/shard_map/all_to_all | solution.py:322
  29.1 18.6 %all-to-all-start.1 = ((bf16[32,16,512]{2,1,0:T(8,128)(2,1)}), bf16[32,16,512]{2,1,0:T(8,128)(2,1)S(1)}, u32[]{:S(2)}, u32[]{:S(2)}) async-start(bf16[32,16,512]{2,1,0:T(8,128)(2,1)} %bitcast.25), calls=%async_computation.1 | async-start | bytes 1048576 | tf_op jit(solution)/shard_map/all_to_all | solution.py:322
  51.7 18.6 %all-to-all-start.2 = ((bf16[32,16,512]{2,1,0:T(8,128)(2,1)}), bf16[32,16,512]{2,1,0:T(8,128)(2,1)S(1)}, u32[]{:S(2)}, u32[]{:S(2)}) async-start(bf16[32,16,512]{2,1,0:T(8,128)(2,1)} %bitcast.24), calls=%async_computation.2 | async-start | bytes 1048576 | tf_op jit(solution)/shard_map/all_to_all | solution.py:322
  75.6 18.6 %all-to-all-start.3 = ((bf16[32,16,512]{2,1,0:T(8,128)(2,1)}), bf16[32,16,512]{2,1,0:T(8,128)(2,1)S(1)}, u32[]{:S(2)}, u32[]{:S(2)}) async-start(bf16[32,16,512]{2,1,0:T(8,128)(2,1)} %bitcast.23), calls=%async_computation.3 | async-start | bytes 1048576 | tf_op jit(solution)/shard_map/all_to_all | solution.py:322
  98.8 18.6 %all-to-all-start.4 = ((bf16[32,16,512]{2,1,0:T(8,128)(2,1)}), bf16[32,16,512]{2,1,0:T(8,128)(2,1)S(1)}, u32[]{:S(2)}, u32[]{:S(2)}) async-start(bf16[32,16,512]{2,1,0:T(8,128)(2,1)} %bitcast.22), calls=%async_computation.4 | async-start | bytes 1048576 | tf_op jit(solution)/shard_map/all_to_all | solution.py:322
  104.4 18.5 %collective-permute-start.26 = (bf16[512,512]{1,0:T(8,128)(2,1)}, bf16[512,512]{1,0:T(8,128)(2,1)}, u32[]{:S(2)}, u32[]{:S(2)}) collective-permute-start(bf16[512,512]{1,0:T(8,128)(2,1)} %get-tuple-element.126), channel_id=1, source_target_pairs={{0,1},{1,0},{2,3},{3,2},{4,5},{5,4},{6,7},{7,6},{8,9},{9,8},{10,11... | collective-permute-start | bytes 1572872 | tf_op jit(solution)/shard_map/ppermute | solution.py:331
  108.4 29.5 %collective-permute-start.13 = (bf16[512,512]{1,0:T(8,128)(2,1)}, bf16[512,512]{1,0:T(8,128)(2,1)S(1)}, u32[]{:S(2)}, u32[]{:S(2)}) collective-permute-start(bf16[512,512]{1,0:T(8,128)(2,1)} %get-tuple-element.117), channel_id=1, source_target_pairs={{0,1},{1,0},{2,3},{3,2},{4,5},{5,4},{6,7},{7,6},{8,9},{9,8},{10,11... | collective-permute-start | bytes 1572872 | tf_op jit(solution)/shard_map/ppermute | solution.py:331
  122.9 29.6 %collective-permute-start = (bf16[512,512]{1,0:T(8,128)(2,1)}, bf16[512,512]{1,0:T(8,128)(2,1)S(1)}, u32[]{:S(2)}, u32[]{:S(2)}) collective-permute-start(bf16[512,512]{1,0:T(8,128)(2,1)} %get-tuple-element.105), channel_id=1, source_target_pairs={{0,1},{1,0},{2,3},{3,2},{4,5},{5,4},{6,7},{7,6},{8,9},{9,8},{10,11... | collective-permute-start | bytes 1572872 | tf_op jit(solution)/shard_map/ppermute | solution.py:331
  124.8 11.3 %collective-permute-start.27 = (bf16[128,512]{1,0:T(8,128)(2,1)}, bf16[128,512]{1,0:T(8,128)(2,1)S(1)}, u32[]{:S(2)}, u32[]{:S(2)}) collective-permute-start(bf16[128,512]{1,0:T(8,128)(2,1)} %get-tuple-element.128), channel_id=1, source_target_pairs={{0,2},{1,3},{2,0},{3,1},{4,6},{5,7},{6,4},{7,5},{8,10},{9,11},{10,... | collective-permute-start | bytes 393224 | tf_op jit(solution)/shard_map/ppermute | solution.py:331
  126.1 10.0 %collective-permute-start.28 = (bf16[128,512]{1,0:T(8,128)(2,1)}, bf16[128,512]{1,0:T(8,128)(2,1)S(1)}, u32[]{:S(2)}, u32[]{:S(2)}) collective-permute-start(bf16[128,512]{1,0:T(8,128)(2,1)} %get-tuple-element.129), channel_id=1, source_target_pairs={{0,4},{1,5},{2,6},{3,7},{4,0},{5,1},{6,2},{7,3},{8,12},{9,13},{10,... | collective-permute-start | bytes 393224 | tf_op jit(solution)/shard_map/ppermute | solution.py:331
  127.2 8.9 %collective-permute-start.29 = (bf16[128,512]{1,0:T(8,128)(2,1)S(1)}, bf16[128,512]{1,0:T(8,128)(2,1)S(1)}, u32[]{:S(2)}, u32[]{:S(2)}) collective-permute-start(bf16[128,512]{1,0:T(8,128)(2,1)S(1)} %get-tuple-element.130), channel_id=1, source_target_pairs={{0,6},{1,7},{2,4},{3,5},{4,2},{5,3},{6,0},{7,1},{8,14},{9,15},{10,... | collective-permute-start | bytes 393224 | tf_op jit(solution)/shard_map/ppermute | solution.py:331
  132.9 61.9 %all-to-all-start.5 = ((bf16[32,16,512]{2,1,0:T(8,128)(2,1)}), bf16[32,16,512]{2,1,0:T(8,128)(2,1)S(1)}, u32[]{:S(2)}, u32[]{:S(2)}) async-start(bf16[32,16,512]{2,1,0:T(8,128)(2,1)} %bitcast.21), calls=%async_computation.5 | async-start | bytes 1048576 | tf_op jit(solution)/shard_map/all_to_all | solution.py:322
  136.2 12.7 %collective-permute-start.30 = (bf16[128,512]{1,0:T(8,128)(2,1)S(1)}, bf16[128,512]{1,0:T(8,128)(2,1)S(1)}, u32[]{:S(2)}, u32[]{:S(2)}) collective-permute-start(bf16[128,512]{1,0:T(8,128)(2,1)S(1)} %shard_map.131.refs_0_), channel_id=1, source_target_pairs={{0,8},{8,0},{16,24},{24,16},{1,9},{9,1},{17,25},{25,17},{2,10},{10... | collective-permute-start | bytes 393224 | tf_op jit(solution)/shard_map/ppermute | solution.py:354
  138.1 16.2 %collective-permute-start.14 = (bf16[128,512]{1,0:T(8,128)(2,1)S(1)}, bf16[128,512]{1,0:T(8,128)(2,1)S(1)}, u32[]{:S(2)}, u32[]{:S(2)}) collective-permute-start(bf16[128,512]{1,0:T(8,128)(2,1)S(1)} %get-tuple-element.119), channel_id=1, source_target_pairs={{0,2},{1,3},{2,0},{3,1},{4,6},{5,7},{6,4},{7,5},{8,10},{9,11},{10,... | collective-permute-start | bytes 393224 | tf_op jit(solution)/shard_map/ppermute | solution.py:331
  139.6 16.1 %collective-permute-start.15 = (bf16[128,512]{1,0:T(8,128)(2,1)S(1)}, bf16[128,512]{1,0:T(8,128)(2,1)S(1)}, u32[]{:S(2)}, u32[]{:S(2)}) collective-permute-start(bf16[128,512]{1,0:T(8,128)(2,1)S(1)} %get-tuple-element.120), channel_id=1, source_target_pairs={{0,4},{1,5},{2,6},{3,7},{4,0},{5,1},{6,2},{7,3},{8,12},{9,13},{10,... | collective-permute-start | bytes 393224 | tf_op jit(solution)/shard_map/ppermute | solution.py:331
  141.1 15.2 %collective-permute-start.16 = (bf16[128,512]{1,0:T(8,128)(2,1)S(1)}, bf16[128,512]{1,0:T(8,128)(2,1)S(1)}, u32[]{:S(2)}, u32[]{:S(2)}) collective-permute-start(bf16[128,512]{1,0:T(8,128)(2,1)S(1)} %get-tuple-element.121), channel_id=1, source_target_pairs={{0,6},{1,7},{2,4},{3,5},{4,2},{5,3},{6,0},{7,1},{8,14},{9,15},{10,... | collective-permute-start | bytes 393224 | tf_op jit(solution)/shard_map/ppermute | solution.py:331
  149.0 9.7 %collective-permute-start.31 = (bf16[128,512]{1,0:T(8,128)(2,1)S(1)}, bf16[128,512]{1,0:T(8,128)(2,1)S(1)}, u32[]{:S(2)}, u32[]{:S(2)}) collective-permute-start(bf16[128,512]{1,0:T(8,128)(2,1)S(1)} %shard_map.132.refs_0_), channel_id=1, source_target_pairs={{0,16},{8,24},{16,0},{24,8},{1,17},{9,25},{17,1},{25,9},{2,18},{10... | collective-permute-start | bytes 393224 | tf_op jit(solution)/shard_map/ppermute | solution.py:354
  152.7 8.5 %collective-permute-start.1 = (bf16[128,512]{1,0:T(8,128)(2,1)S(1)}, bf16[128,512]{1,0:T(8,128)(2,1)S(1)}, u32[]{:S(2)}, u32[]{:S(2)}) collective-permute-start(bf16[128,512]{1,0:T(8,128)(2,1)S(1)} %get-tuple-element.107), channel_id=1, source_target_pairs={{0,2},{1,3},{2,0},{3,1},{4,6},{5,7},{6,4},{7,5},{8,10},{9,11},{10,... | collective-permute-start | bytes 393224 | tf_op jit(solution)/shard_map/ppermute | solution.py:331
  154.3 7.8 %collective-permute-start.2 = (bf16[128,512]{1,0:T(8,128)(2,1)S(1)}, bf16[128,512]{1,0:T(8,128)(2,1)S(1)}, u32[]{:S(2)}, u32[]{:S(2)}) collective-permute-start(bf16[128,512]{1,0:T(8,128)(2,1)S(1)} %get-tuple-element.108), channel_id=1, source_target_pairs={{0,4},{1,5},{2,6},{3,7},{4,0},{5,1},{6,2},{7,3},{8,12},{9,13},{10,... | collective-permute-start | bytes 393224 | tf_op jit(solution)/shard_map/ppermute | solution.py:331
  156.4 9.6 %collective-permute-start.17 = (bf16[128,512]{1,0:T(8,128)(2,1)S(1)}, bf16[128,512]{1,0:T(8,128)(2,1)S(1)}, u32[]{:S(2)}, u32[]{:S(2)}) collective-permute-start(bf16[128,512]{1,0:T(8,128)(2,1)S(1)} %shard_map.126.refs_0_), channel_id=1, source_target_pairs={{0,8},{8,0},{16,24},{24,16},{1,9},{9,1},{17,25},{25,17},{2,10},{10... | collective-permute-start | bytes 393224 | tf_op jit(solution)/shard_map/ppermute | solution.py:354
  180.1 7.5 %collective-permute-start.8 = (bf16[128,512]{1,0:T(8,128)(2,1)S(1)}, bf16[128,512]{1,0:T(8,128)(2,1)S(1)}, u32[]{:S(2)}, u32[]{:S(2)}) collective-permute-start(bf16[128,512]{1,0:T(8,128)(2,1)S(1)} %shard_map.121.refs_0_), channel_id=1, source_target_pairs={{0,6},{1,7},{2,4},{3,5},{4,2},{5,3},{6,0},{7,1},{8,14},{9,15},{10,... | collective-permute-start | bytes 393224 | tf_op jit(solution)/shard_map/ppermute | solution.py:331
  182.2 7.8 %collective-permute-start.7 = (bf16[128,512]{1,0:T(8,128)(2,1)S(1)}, bf16[128,512]{1,0:T(8,128)(2,1)S(1)}, u32[]{:S(2)}, u32[]{:S(2)}) collective-permute-start(bf16[128,512]{1,0:T(8,128)(2,1)S(1)} %shard_map.121.refs_0_), channel_id=1, source_target_pairs={{0,4},{1,5},{2,6},{3,7},{4,0},{5,1},{6,2},{7,3},{8,12},{9,13},{10,... | collective-permute-start | bytes 393224 | tf_op jit(solution)/shard_map/ppermute | solution.py:331
  184.0 9.1 %collective-permute-start.23 = (bf16[128,512]{1,0:T(8,128)(2,1)S(1)}, bf16[128,512]{1,0:T(8,128)(2,1)S(1)}, u32[]{:S(2)}, u32[]{:S(2)}) collective-permute-start(bf16[128,512]{1,0:T(8,128)(2,1)S(1)} %collective-permute-done.19.refs_1_), channel_id=1, source_target_pairs={{0,1},{1,0},{2,3},{3,2},{4,5},{5,4},{6,7},{7,6},{8,9},{9,8},{10,11... | collective-permute-start | bytes 393224 | tf_op jit(solution)/shard_map/ppermute | solution.py:331
  184.1 10.7 %collective-permute-start.9 = (bf16[128,512]{1,0:T(8,128)(2,1)S(1)}, bf16[128,512]{1,0:T(8,128)(2,1)S(1)}, u32[]{:S(2)}, u32[]{:S(2)}) collective-permute-start(bf16[128,512]{1,0:T(8,128)(2,1)S(1)} %shard_map.121.refs_0_), channel_id=1, source_target_pairs={{0,1},{1,0},{2,3},{3,2},{4,5},{5,4},{6,7},{7,6},{8,9},{9,8},{10,11... | collective-permute-start | bytes 393224 | tf_op jit(solution)/shard_map/ppermute | solution.py:331
  (44 other events, 188.9 us)
